TPU v7x, 256 devices: a whole 4x4x8 slice. The times are simulated.
256 devices in a mesh: pipe: 8 (over y, core), space: 32 (over x, z).
Axes of the slice: x: 4, y: 4, z: 8, core: 2. Of those that a mesh axis runs over, the one named last changes fastest.
Arguments:
- activations: bfloat16 [8, 64, 128, 2048], P('pipe', 'space'), may hold values from -6 to 6
- cotangent: bfloat16 [64, 128, 2048], P('space'), may hold values from -6 to 6
- w_first: bfloat16 [8, 2, 8, 256, 256], P('pipe'), may hold values from -0.25 to 0.25
- w_second: bfloat16 [8, 2, 8, 256, 256], P('pipe'), may hold values from -0.25 to 0.25
- b_first: float32 [8, 2, 2048], P('pipe'), may hold values from -1 to 1
Outputs:
- grads: bfloat16 [8, 64, 128, 2048], P('pipe', 'space')
All inputs are finite; a program needn't handle non-finite values.
Results may differ from a plain program's by a relative error of at most 0.028.
Values may be sent and summed in bfloat16 or wider, within the bound.
No kernel may reach another device: no remote copies, remote signals or barrier semaphores. Data moves between devices by JAX's collectives and lax.ppermute only.
A program may use at most 64 MiB of HBM per device.

v0:
```python
import math

import jax
import jax.numpy as jnp
import numpy as np
from jax import lax
from jax.experimental import pallas as pl
from jax.experimental.pallas import tpu as pltpu
from jax.sharding import PartitionSpec as P


BF16 = jnp.bfloat16
F32 = jnp.float32
X, Y, Z = 4, 4, 8


def two_parts(table):
    high = table.astype(np.float32).astype(BF16)
    low = (table - high.astype(np.float64)).astype(np.float32).astype(BF16)
    return np.concatenate([high, low], axis=1)


def row_matrix(rows, width, columns):
    modes = width // 2
    pair = modes // columns
    angles = 2.0 * math.pi * (np.outer(np.arange(modes), np.arange(width)) % width) / width
    scale = 1.0 / math.sqrt(width)
    parts = np.stack([np.cos(angles), -np.sin(angles)]) * scale
    table = np.zeros((columns, rows, 2, pair, rows, width))
    by_column = parts.reshape(2, columns, pair, width).transpose(1, 0, 2, 3)
    for h in range(rows):
        table[:, h, :, :, h, :] = by_column
    return table.reshape(columns * rows * 2 * pair, rows * width)


def column_matrix(height, pair):
    angles = 2.0 * math.pi * (np.outer(np.arange(height), np.arange(height)) % height) / height
    scale = 1.0 / math.sqrt(height)
    cosines, sines = np.cos(angles) * scale, np.sin(angles) * scale
    table = np.zeros((2, pair, height, height, 2, pair))
    for k in range(pair):
        table[0, k, :, :, 0, k] = cosines
        table[0, k, :, :, 1, k] = sines
        table[1, k, :, :, 1, k] = cosines
        table[1, k, :, :, 0, k] = -sines
    return table.reshape(2 * pair * height, 2 * pair * height)


def fold_matrices(height, pair):
    size = 2 * pair * height
    plain = np.eye(size)
    folded = np.eye(size).reshape(2, pair, height, 2, pair, height)
    eye = np.eye(height)
    flip = eye[(-np.arange(height)) % height]
    folded[0, 0, :, 0, 0, :] = 0.5 * (eye + flip)
    folded[1, 0, :, 1, 0, :] = 0.5 * (eye - flip)
    return np.stack([plain, folded.reshape(size, size)]).astype(np.float32).astype(BF16)


def dot(left, right):
    return jnp.dot(left, right, preferred_element_type=F32)


def dot_t(left, right):
    return lax.dot_general(left, right, (((1,), (1,)), ((), ())), preferred_element_type=F32)


def gelu_slope(values):
    return (
        0.5 * (1.0 + lax.erf(values * 0.7071067811865476))
        + values * jnp.exp(-0.5 * values * values) * 0.3989422804014327
    )


def twice(table_ref, operand):
    depth = operand.shape[0]
    return dot(table_ref[:, :depth], operand) + dot(table_ref[:, depth:], operand)


def place(where_ref):
    me, here = where_ref[0], where_ref[1]
    return lax.shift_right_logical(me, 1), me & 1, lax.shift_right_logical(here, 3), here & (Z - 1)


def prologue_kernel(where_ref, table_ref, act_ref, cot_ref, first_ref, second_ref, bias_ref, *rest):
    pieces, rows_ref, cots = rest[:Y], rest[Y], rest[Y + 1 : Y + 1 + Z]
    cot_buf, bias_buf, found, sems, cot_sem = rest[Y + 1 + Z :]
    size = cot_buf.shape[1] // 2
    y, c, x, z = place(where_ref)
    odd = x & 1
    cot_copy = pltpu.make_async_copy(cot_ref.at[:, pl.ds(y * 2 * size, 2 * size)], cot_buf, cot_sem)
    cot_copy.start()
    copies = []
    for d in range(Y):
        block = ((y + d) & (Y - 1)) * 2 + odd
        for i in range(2):
            for j, ref in enumerate((first_ref, second_ref)):
                copy = pltpu.make_async_copy(
                    ref.at[0, i, block],
                    pieces[d].at[pl.ds((2 * j + i) * size, size)],
                    sems.at[d, 2 * j + i],
                )
                copy.start()
                copies.append(copy)
        bias = bias_ref[0, :, pl.ds(block * size, size)]
        high = bias.astype(BF16).astype(F32)
        middle = (bias - high).astype(BF16).astype(F32)
        low = bias - high - middle
        packed = jnp.concatenate([high, middle, low, jnp.zeros((10, size), F32)], axis=0)
        bias_buf[d] = packed.astype(BF16)
        copy = pltpu.make_async_copy(bias_buf.at[d], pieces[d].at[pl.ds(4 * size, 16)], sems.at[d, 4])
        copy.start()
        copies.append(copy)

    depth = table_ref.shape[1] // 2
    half = table_ref.shape[0] // 2
    cot_copy.wait()
    own = pl.ds(pl.multiple_of(c * half, half), half)
    line = lax.broadcasted_iota(jnp.int32, (half, size), 0)
    zero_mode = jnp.logical_and(jnp.logical_and(line < 8, (line & 1) == 0), c == 0)
    factor = jnp.where(zero_mode, 1.0, 2.0).astype(F32)
    for k in range(2):
        field = cot_buf[:, k * size : (k + 1) * size]
        spectrum = dot(table_ref[own, :depth], field) + dot(table_ref[own, depth:], field)
        found[k] = (spectrum * factor).astype(BF16).reshape(half // 8, 8, size)
    for d in range(Z):
        to = (z + d) & (Z - 1)
        for k in range(X):
            cots[d][k] = found[k & 1, (k >> 1) * Z + to]

    for n in range(2 * Y):
        spectrum = twice(table_ref, act_ref[:, n * size : (n + 1) * size]).astype(BF16)
        rows_ref[n // 2, :, n % 2] = spectrum.reshape(4, half // 2, size)
    for copy in copies:
        copy.wait()


def turn_kernel(where_ref, *rest):
    arrived, outs = rest[:Z], rest[Z:]
    _, _, x, _ = place(where_ref)
    for e in range(X):
        to = (x + e) & (X - 1)
        for d in range(Z):
            outs[e][d] = arrived[d][to]


def inverse_kernel(table_ref, spec_ref, cot_ref, out_ref):
    rows = table_ref.shape[1] // 2
    size = spec_ref.shape[4]
    for k in range(2):
        block = slice(k * size, (k + 1) * size)
        field = twice(table_ref, spec_ref[0, :, k].reshape(rows, size))
        out_ref[:, block] = (field + cot_ref[:, block].astype(F32)).astype(BF16)


def chain_kernel(where_ref, act_ref, col_ref, inv_ref, fold_ref, *rest):
    sections = act_ref.shape[0]
    cots, weights = rest[:X], rest[X : X + sections]
    out_ref, held, found, sems = rest[X + sections :]
    size = act_ref.shape[2]
    half = act_ref.shape[1] // 2
    y, c, x, z = place(where_ref)
    copies = []
    for d in range(Y):
        for i in range(2):
            slot = ((y - d) & (Y - 1)) * 2 + (c if i == 0 else 1 - c)
            copy = pltpu.make_async_copy(weights[2 * d + i], held.at[slot], sems.at[2 * d + i])
            copy.start()
            copies.append(copy)
    for e in range(X):
        for d in range(Z):
            found[((x - e) & (X - 1)) * Z + ((z - d) & (Z - 1))] = cots[e][d]

    base = twice(col_ref, found[...].reshape(2 * half, size))
    total = jnp.zeros_like(base)
    height_total = jnp.zeros_like(base)
    grad = base.astype(BF16)
    spectra = [twice(col_ref, act_ref[p]).astype(BF16) for p in range(sections)]
    for copy in copies:
        copy.wait()

    for p in range(sections - 1, -1, -1):
        a_re, a_im = held[p, 0:size], held[p, size : 2 * size]
        b_re, b_im = held[p, 2 * size : 3 * size], held[p, 3 * size : 4 * size]
        bias = held[p, 4 * size : 4 * size + 16].astype(F32)
        bias_re = bias[0:1] + bias[2:3] + bias[4:5]
        bias_im = bias[1:2] + bias[3:4] + bias[5:6]
        s = spectra[p]
        s_turned = jnp.concatenate([-s[half:], s[:half]], axis=0)
        z_both = dot(s, a_re) + dot(s_turned, a_im)
        slope = gelu_slope(jnp.concatenate([z_both[:half] + bias_re, z_both[half:] + bias_im], axis=0))
        g_turned = jnp.concatenate([grad[half:], -grad[:half]], axis=0)
        u = dot_t(grad, b_re) + dot_t(g_turned, b_im)
        q = (u * slope).astype(BF16)
        q_turned = jnp.concatenate([q[half:], -q[:half]], axis=0)
        e = (dot_t(q, a_re) + dot_t(q_turned, a_im)).astype(BF16)
        height_total = height_total + twice(inv_ref, e)
        out_ref[p] = height_total.astype(BF16)
        if p > 0:
            total = total + dot(fold_ref[0], e)
            grad = (base + total).astype(BF16)


def body(activations, cotangent, w_first, w_second, b_first):
    sections = lax.axis_size("pipe")
    columns = lax.axis_size("space")
    me = lax.axis_index("pipe")
    here = lax.axis_index("space")
    _, rows, width, channels = activations.shape
    size = w_first.shape[3]
    height = rows * columns
    pair = width // 2 // columns
    count = rows * width
    tile = 2 * rows * pair
    forward_rows = two_parts(row_matrix(rows, width, columns))
    inverse_rows = two_parts(row_matrix(rows, width, columns).T)
    forward_columns = two_parts(column_matrix(height, pair))
    inverse_columns = two_parts(column_matrix(height, pair).T)
    folds = fold_matrices(height, pair)
    where = jnp.stack([me, here]).astype(jnp.int32)

    smem = pl.BlockSpec(memory_space=pltpu.SMEM)
    vmem = pl.BlockSpec(memory_space=pltpu.VMEM)
    hbm = pl.BlockSpec(memory_space=pl.ANY)

    def shaped(*dims):
        return jax.ShapeDtypeStruct(dims, BF16)

    def exchange(value):
        return lax.all_to_all(
            value.reshape(sections * columns, tile, size),
            ("pipe", "space"),
            split_axis=0,
            concat_axis=0,
            tiled=True,
        )

    flat_cot = cotangent.reshape(count, channels)
    made = pl.pallas_call(
        prologue_kernel,
        in_specs=[smem, vmem, vmem, hbm, hbm, hbm, vmem],
        out_specs=[hbm] * Y + [vmem] * (1 + Z),
        out_shape=[shaped(4 * size + 16, size)] * Y
        + [shaped(Y, 4, 2, count // 4, size)]
        + [shaped(X, tile, size)] * Z,
        scratch_shapes=[
            pltpu.VMEM((count, 2 * size), BF16),
            pltpu.VMEM((Y, 16, size), BF16),
            pltpu.VMEM((2, columns // 2, tile, size), BF16),
            pltpu.SemaphoreType.DMA((Y, 5)),
            pltpu.SemaphoreType.DMA(()),
        ],
        name="prologue",
    )(where, forward_rows, activations.reshape(count, channels), flat_cot, w_first, w_second, b_first)
    pieces, act_rows, cot_rows = made[:Y], made[Y], made[Y + 1 :]

    weights = []
    for d in range(Y):
        route = [(i, (i + 2 * d) % sections) for i in range(sections)]
        piece = lax.ppermute(pieces[d], "pipe", route) if d else pieces[0]
        weights += [piece, lax.ppermute(piece, "pipe", [(i, i ^ 1) for i in range(sections)])]

    arrived = [cot_rows[0]]
    for d in range(1, Z):
        route = [(x * Z + z, x * Z + (z + d) % Z) for x in range(X) for z in range(Z)]
        arrived.append(lax.ppermute(cot_rows[d], "space", route))
    turned = pl.pallas_call(
        turn_kernel,
        in_specs=[smem] + [vmem] * Z,
        out_specs=[vmem] * X,
        out_shape=[shaped(Z, tile, size)] * X,
        name="turn",
    )(where, *arrived)
    cots = [turned[0]]
    for e in range(1, X):
        route = [(x * Z + z, (x + e) % X * Z + z) for x in range(X) for z in range(Z)]
        cots.append(lax.ppermute(turned[e], "space", route))

    act_columns = exchange(act_rows).reshape(sections, count, size)

    y, core, x, z = lax.div(me, 2), lax.rem(me, 2), lax.div(here, Z), lax.rem(here, Z)
    has_zero = jnp.logical_and(jnp.logical_and(core == 0, x < 2), z == 0)
    fold = lax.dynamic_slice_in_dim(jnp.asarray(folds), jnp.where(has_zero, 1, 0), 1, 0)
    back = pl.pallas_call(
        chain_kernel,
        in_specs=[smem] + [vmem] * (4 + X) + [hbm] * sections,
        out_specs=vmem,
        out_shape=shaped(sections, count, size),
        scratch_shapes=[
            pltpu.VMEM((sections, 4 * size + 16, size), BF16),
            pltpu.VMEM((columns, tile, size), BF16),
            pltpu.SemaphoreType.DMA((sections,)),
        ],
        name="chain",
    )(where, act_columns, forward_columns, inverse_columns, fold, *cots, *weights)
    spec_rows = exchange(back).reshape(Y, 4, 2, count // 4, size)
    grads = pl.pallas_call(
        inverse_kernel,
        grid=(Y,),
        in_specs=[
            pl.BlockSpec((count, 2 * count), lambda i: (0, 0)),
            pl.BlockSpec((1, 4, 2, count // 4, size), lambda i: (i, 0, 0, 0, 0)),
            pl.BlockSpec((count, 2 * size), lambda i: (0, i)),
        ],
        out_specs=pl.BlockSpec((count, 2 * size), lambda i: (0, i)),
        out_shape=shaped(count, channels),
        name="inverse_rows",
    )(inverse_rows, spec_rows, flat_cot)
    return grads.reshape(1, rows, width, channels)


def solution(mesh):
    in_specs = (
        P("pipe", "space", None, None),
        P("space", None, None),
        P("pipe", None, None, None, None),
        P("pipe", None, None, None, None),
        P("pipe", None, None),
    )
    out_specs = P("pipe", "space", None, None)
    return jax.shard_map(body, mesh=mesh, in_specs=in_specs, out_specs=out_specs, check_vma=False)
```

profile of v0, /device:TPU:1, one launch (start us, length us, event | category | flops | bytes accessed | tf_op | source)
XLA Modules:
  0.0 237.1 jit_solution(8329248627431067750)
XLA Ops:
  0.6 67.1 %prologue.1 = (bf16[1040,256]{1,0:T(8,128)(2,1)}, bf16[1040,256]{1,0:T(8,128)(2,1)}, bf16[1040,256]{1,0:T(8,128)(2,1)}, bf16[1040,256]{1,0:T(8,128)(2,1)}, bf16[...) custom-call(s32[2]{0:T(128)} %pad_add_fusion.where_ref, ...), custom_call_target="tpu_custom_call" | custom-call | tf_op jit(solution)/shard_map/prologue/pallas_call | solution.py:239
  67.8 15.7 %all-to-all-start = ((bf16[256,8,256]{2,1,0:T(8,128)(2,1)}), bf16[256,8,256]{2,1,0:T(8,128)(2,1)S(1)}, u32[]{:S(2)}, u32[]{:S(2)}) async-start(bf16[256,8,256]{2,1,0:T(8,128)(2,1)} %bitcast.14), calls=%async_computation | async-start | bytes 2097152 | tf_op jit(solution)/shard_map/all_to_all | solution.py:230
  83.5 1.4 collective-permute-start.11
  84.9 2.5 %collective-permute-start.13 = (bf16[1040,256]{1,0:T(8,128)(2,1)}, bf16[1040,256]{1,0:T(8,128)(2,1)S(1)}, u32[]{:S(2)}, u32[]{:S(2)}) collective-permute-start(bf16[1040,256]{1,0:T(8,128)(2,1)} %get-tuple-element.37), channel_id=1, source_target_pairs={{0,128},{32,160},{64,192},{96,224},{128,0},{160,32},{192,64},{224,... | collective-permute-start | bytes 1597448 | tf_op jit(solution)/shard_map/ppermute | solution.py:260
  88.5 1.2 collective-permute-start.10
  89.7 15.3 %collective-permute-done.11.rest_6_ = bf16[1040,256]{1,0:T(8,128)(2,1)S(1)} collective-permute-done((bf16[1040,256]{1,0:T(8,128)(2,1)}, bf16[1040,256]{1,0:T(8,128)(2,1)S(1)}, u32[]{:S(2)}, u32[]{:S(2)}) %collective-permute-start.11) | collective-permute-done | bytes 532512 | tf_op jit(solution)/shard_map/ppermute | solution.py:260
  105.1 2.9 %collective-permute-start.12 = (bf16[1040,256]{1,0:T(8,128)(2,1)S(1)}, bf16[1040,256]{1,0:T(8,128)(2,1)}, u32[]{:S(2)}, u32[]{:S(2)}) collective-permute-start(bf16[1040,256]{1,0:T(8,128)(2,1)S(1)} %collective-permute-done.11.rest_6_), channel_id=1, source_target_pairs={{0,32},{32,0},{64,96},{96,64},{128,160},{160,128},{192,224},{224,1... | collective-permute-start | bytes 1597448 | tf_op jit(solution)/shard_map/ppermute | solution.py:261
  108.0 13.6 %collective-permute-done.13.rest_8_ = bf16[1040,256]{1,0:T(8,128)(2,1)S(1)} collective-permute-done((bf16[1040,256]{1,0:T(8,128)(2,1)}, bf16[1040,256]{1,0:T(8,128)(2,1)S(1)}, u32[]{:S(2)}, u32[]{:S(2)}) %collective-permute-start.13) | collective-permute-done | bytes 532512 | tf_op jit(solution)/shard_map/ppermute | solution.py:260
  123.7 3.5 %collective-permute-done.rest_1_ = bf16[4,8,256]{2,1,0:T(8,128)(2,1)S(1)} collective-permute-done((bf16[4,8,256]{2,1,0:T(8,128)(2,1)S(1)}, bf16[4,8,256]{2,1,0:T(8,128)(2,1)S(1)}, u32[]{:S(2)}, u32[]{:S(2)}) %collective-permute-start) | collective-permute-done | bytes 16416 | tf_op jit(solution)/shard_map/ppermute | solution.py:266
  127.4 4.7 %collective-permute-done.1.rest_2_ = bf16[4,8,256]{2,1,0:T(8,128)(2,1)S(1)} collective-permute-done((bf16[4,8,256]{2,1,0:T(8,128)(2,1)S(1)}, bf16[4,8,256]{2,1,0:T(8,128)(2,1)S(1)}, u32[]{:S(2)}, u32[]{:S(2)}) %collective-permute-start.1) | collective-permute-done | bytes 16416 | tf_op jit(solution)/shard_map/ppermute | solution.py:266
  132.6 5.0 %collective-permute-done.2.rest_3_ = bf16[4,8,256]{2,1,0:T(8,128)(2,1)S(1)} collective-permute-done((bf16[4,8,256]{2,1,0:T(8,128)(2,1)S(1)}, bf16[4,8,256]{2,1,0:T(8,128)(2,1)S(1)}, u32[]{:S(2)}, u32[]{:S(2)}) %collective-permute-start.2) | collective-permute-done | bytes 16416 | tf_op jit(solution)/shard_map/ppermute | solution.py:266
  137.7 4.6 %collective-permute-start.3 = (bf16[4,8,256]{2,1,0:T(8,128)(2,1)S(1)}, bf16[4,8,256]{2,1,0:T(8,128)(2,1)S(1)}, u32[]{:S(2)}, u32[]{:S(2)}) collective-permute-start(bf16[4,8,256]{2,1,0:T(8,128)(2,1)S(1)} %copy-done.18), channel_id=1, source_target_pairs={{0,4},{1,5},{2,6},{3,7},{4,0},{5,1},{6,2},{7,3},{8,12},{9,13},{10,... | collective-permute-start | bytes 49160 | tf_op jit(solution)/shard_map/ppermute | solution.py:266
  142.2 1.9 collective-permute-done.3.rest_4_
  144.2 2.7 %collective-permute-start.4 = (bf16[4,8,256]{2,1,0:T(8,128)(2,1)S(1)}, bf16[4,8,256]{2,1,0:T(8,128)(2,1)S(1)}, u32[]{:S(2)}, u32[]{:S(2)}) collective-permute-start(bf16[4,8,256]{2,1,0:T(8,128)(2,1)S(1)} %copy-done.17), channel_id=1, source_target_pairs={{0,5},{1,6},{2,7},{3,0},{4,1},{5,2},{6,3},{7,4},{8,13},{9,14},{10,... | collective-permute-start | bytes 49160 | tf_op jit(solution)/shard_map/ppermute | solution.py:266
  146.9 1.7 collective-permute-done.4.rest_5_
  148.6 2.5 %collective-permute-start.5 = (bf16[4,8,256]{2,1,0:T(8,128)(2,1)S(1)}, bf16[4,8,256]{2,1,0:T(8,128)(2,1)S(1)}, u32[]{:S(2)}, u32[]{:S(2)}) collective-permute-start(bf16[4,8,256]{2,1,0:T(8,128)(2,1)S(1)} %copy-done.16), channel_id=1, source_target_pairs={{0,6},{1,7},{2,0},{3,1},{4,2},{5,3},{6,4},{7,5},{8,14},{9,15},{10,... | collective-permute-start | bytes 49160 | tf_op jit(solution)/shard_map/ppermute | solution.py:266
  152.1 3.4 %collective-permute-start.6 = (bf16[4,8,256]{2,1,0:T(8,128)(2,1)}, bf16[4,8,256]{2,1,0:T(8,128)(2,1)S(1)}, u32[]{:S(2)}, u32[]{:S(2)}) collective-permute-start(bf16[4,8,256]{2,1,0:T(8,128)(2,1)} %get-tuple-element.30), channel_id=1, source_target_pairs={{0,7},{1,0},{2,1},{3,2},{4,3},{5,4},{6,5},{7,6},{8,15},{9,8},{10,9... | collective-permute-start | bytes 49160 | tf_op jit(solution)/shard_map/ppermute | solution.py:266
  157.2 1.5 turn.1
  159.4 3.5 %collective-permute-done.7.rest_1_ = bf16[8,8,256]{2,1,0:T(8,128)(2,1)S(1)} collective-permute-done((bf16[8,8,256]{2,1,0:T(8,128)(2,1)}, bf16[8,8,256]{2,1,0:T(8,128)(2,1)S(1)}, u32[]{:S(2)}, u32[]{:S(2)}) %collective-permute-start.7) | collective-permute-done | bytes 32800 | tf_op jit(solution)/shard_map/ppermute | solution.py:277
  163.3 4.1 %collective-permute-done.8.rest_2_ = bf16[8,8,256]{2,1,0:T(8,128)(2,1)S(1)} collective-permute-done((bf16[8,8,256]{2,1,0:T(8,128)(2,1)}, bf16[8,8,256]{2,1,0:T(8,128)(2,1)S(1)}, u32[]{:S(2)}, u32[]{:S(2)}) %collective-permute-start.8) | collective-permute-done | bytes 32800 | tf_op jit(solution)/shard_map/ppermute | solution.py:277
  168.3 2.3 collective-permute-done.9.rest_3_
  171.7 10.4 %chain.1 = bf16[8,256,256]{2,1,0:T(8,128)(2,1)} custom-call(s32[2]{0:T(128)} %pad_add_fusion.where_ref, bf16[8,256,256]{2,1,0:T(8,128)(2,1)} %bitcast.9, bf16[256,512]{1,0:T(8,128)(2,1)} %constant.37.clone.col_ref, bf16[256,512]{1,0:T(8,128)(2,1)} %constant.38.clone.inv_ref, bf16[1,256,256]{2,1,0:T(8,128)(2,1)} %constant_dynamic-slice_fusion.fold_ref, ...), custom_call_target="tpu_custom_call" | custom-call | tf_op jit(solution)/shard_map/chain/pallas_call | solution.py:284
  182.0 50.7 %all_to_all.10 = bf16[256,8,256]{2,1,0:T(8,128)(2,1)} all-to-all(bf16[256,8,256]{2,1,0:T(8,128)(2,1)} %bitcast.10), channel_id=1, replica_groups=mesh['pipe'=8,'space'=32] {'pipe','space'}, dimensions={0} | all-to-all | bytes 2097152 | tf_op jit(solution)/shard_map/all_to_all | solution.py:230
  232.8 4.3 %inverse_rows.1 = bf16[256,2048]{1,0:T(8,128)(2,1)} custom-call(bf16[256,512]{1,0:T(8,128)(2,1)} %constant.39.clone.table_ref, bf16[4,4,2,64,256]{4,3,2,1,0:T(8,128)(2,1)} %bitcast.11, bf16[256,2048]{1,0:T(8,128)(2,1)} %bitcast.13), custom_call_target="tpu_custom_call" | custom-call | tf_op jit(solution)/shard_map/inverse_rows/pallas_call | solution.py:297
  (63 shorter events, 10.3 us)
Async XLA Ops:
  67.8 64.3 %copy-start.19 = (bf16[4,8,256]{2,1,0:T(8,128)(2,1)S(1)}, bf16[4,8,256]{2,1,0:T(8,128)(2,1)}, u32[]{:S(2)}) copy-start(bf16[4,8,256]{2,1,0:T(8,128)(2,1)} %get-tuple-element.26) | copy-start | bytes 49156
  67.8 69.9 %copy-start.18 = (bf16[4,8,256]{2,1,0:T(8,128)(2,1)S(1)}, bf16[4,8,256]{2,1,0:T(8,128)(2,1)}, u32[]{:S(2)}) copy-start(bf16[4,8,256]{2,1,0:T(8,128)(2,1)} %get-tuple-element.27) | copy-start | bytes 49156
  67.8 76.4 %copy-start.17 = (bf16[4,8,256]{2,1,0:T(8,128)(2,1)S(1)}, bf16[4,8,256]{2,1,0:T(8,128)(2,1)}, u32[]{:S(2)}) copy-start(bf16[4,8,256]{2,1,0:T(8,128)(2,1)} %get-tuple-element.28) | copy-start | bytes 49156
  67.8 80.8 %copy-start.16 = (bf16[4,8,256]{2,1,0:T(8,128)(2,1)S(1)}, bf16[4,8,256]{2,1,0:T(8,128)(2,1)}, u32[]{:S(2)}) copy-start(bf16[4,8,256]{2,1,0:T(8,128)(2,1)} %get-tuple-element.29) | copy-start | bytes 49156
  67.8 99.8 %copy-start.5 = (bf16[2,256,256]{2,1,0:T(8,128)(2,1)S(1)}, bf16[2,256,256]{2,1,0:T(8,128)(2,1)}, u32[]{:S(2)}) copy-start(bf16[2,256,256]{2,1,0:T(8,128)(2,1)} %constant.36.clone) | copy-start | bytes 786436
  67.8 102.9 %all-to-all-start = ((bf16[256,8,256]{2,1,0:T(8,128)(2,1)}), bf16[256,8,256]{2,1,0:T(8,128)(2,1)S(1)}, u32[]{:S(2)}, u32[]{:S(2)}) async-start(bf16[256,8,256]{2,1,0:T(8,128)(2,1)} %bitcast.14), calls=%async_computation | async-start | bytes 2097152 | tf_op jit(solution)/shard_map/all_to_all | solution.py:230
  83.5 21.6 %collective-permute-start.11 = (bf16[1040,256]{1,0:T(8,128)(2,1)}, bf16[1040,256]{1,0:T(8,128)(2,1)S(1)}, u32[]{:S(2)}, u32[]{:S(2)}) collective-permute-start(bf16[1040,256]{1,0:T(8,128)(2,1)} %get-tuple-element.36), channel_id=1, source_target_pairs={{0,64},{32,96},{64,128},{96,160},{128,192},{160,224},{192,0},{224,... | collective-permute-start | bytes 1597448 | tf_op jit(solution)/shard_map/ppermute | solution.py:260
  84.9 36.6 %collective-permute-start.13 = (bf16[1040,256]{1,0:T(8,128)(2,1)}, bf16[1040,256]{1,0:T(8,128)(2,1)S(1)}, u32[]{:S(2)}, u32[]{:S(2)}) collective-permute-start(bf16[1040,256]{1,0:T(8,128)(2,1)} %get-tuple-element.37), channel_id=1, source_target_pairs={{0,128},{32,160},{64,192},{96,224},{128,0},{160,32},{192,64},{224,... | collective-permute-start | bytes 1597448 | tf_op jit(solution)/shard_map/ppermute | solution.py:260
  87.4 35.0 %collective-permute-start.15 = (bf16[1040,256]{1,0:T(8,128)(2,1)}, bf16[1040,256]{1,0:T(8,128)(2,1)S(1)}, u32[]{:S(2)}, u32[]{:S(2)}) collective-permute-start(bf16[1040,256]{1,0:T(8,128)(2,1)} %get-tuple-element.38), channel_id=1, source_target_pairs={{0,192},{32,224},{64,0},{96,32},{128,64},{160,96},{192,128},{224,1... | collective-permute-start | bytes 1597448 | tf_op jit(solution)/shard_map/ppermute | solution.py:260
  88.5 82.2 %collective-permute-start.10 = (bf16[1040,256]{1,0:T(8,128)(2,1)S(1)}, bf16[1040,256]{1,0:T(8,128)(2,1)}, u32[]{:S(2)}, u32[]{:S(2)}) collective-permute-start(bf16[1040,256]{1,0:T(8,128)(2,1)S(1)} %copy-done.1), channel_id=1, source_target_pairs={{0,32},{32,0},{64,96},{96,64},{128,160},{160,128},{192,224},{224,1... | collective-permute-start | bytes 1597448 | tf_op jit(solution)/shard_map/ppermute | solution.py:261
  105.1 65.6 %copy-start.2 = (bf16[1040,256]{1,0:T(8,128)(2,1)}, bf16[1040,256]{1,0:T(8,128)(2,1)S(1)}, u32[]{:S(2)}) copy-start(bf16[1040,256]{1,0:T(8,128)(2,1)S(1)} %collective-permute-done.11.rest_6_) | copy-start | bytes 1597444
  105.1 65.6 %collective-permute-start.12 = (bf16[1040,256]{1,0:T(8,128)(2,1)S(1)}, bf16[1040,256]{1,0:T(8,128)(2,1)}, u32[]{:S(2)}, u32[]{:S(2)}) collective-permute-start(bf16[1040,256]{1,0:T(8,128)(2,1)S(1)} %collective-permute-done.11.rest_6_), channel_id=1, source_target_pairs={{0,32},{32,0},{64,96},{96,64},{128,160},{160,128},{192,224},{224,1... | collective-permute-start | bytes 1597448 | tf_op jit(solution)/shard_map/ppermute | solution.py:261
  121.6 49.1 %collective-permute-start.14 = (bf16[1040,256]{1,0:T(8,128)(2,1)S(1)}, bf16[1040,256]{1,0:T(8,128)(2,1)}, u32[]{:S(2)}, u32[]{:S(2)}) collective-permute-start(bf16[1040,256]{1,0:T(8,128)(2,1)S(1)} %collective-permute-done.13.rest_8_), channel_id=1, source_target_pairs={{0,32},{32,0},{64,96},{96,64},{128,160},{160,128},{192,224},{224,1... | collective-permute-start | bytes 1597448 | tf_op jit(solution)/shard_map/ppermute | solution.py:261
  122.4 48.3 %collective-permute-start.16 = (bf16[1040,256]{1,0:T(8,128)(2,1)S(1)}, bf16[1040,256]{1,0:T(8,128)(2,1)}, u32[]{:S(2)}, u32[]{:S(2)}) collective-permute-start(bf16[1040,256]{1,0:T(8,128)(2,1)S(1)} %collective-permute-done.15.rest_10_), channel_id=1, source_target_pairs={{0,32},{32,0},{64,96},{96,64},{128,160},{160,128},{192,224},{224,1... | collective-permute-start | bytes 1597448 | tf_op jit(solution)/shard_map/ppermute | solution.py:261
  122.5 4.7 %collective-permute-start = (bf16[4,8,256]{2,1,0:T(8,128)(2,1)S(1)}, bf16[4,8,256]{2,1,0:T(8,128)(2,1)S(1)}, u32[]{:S(2)}, u32[]{:S(2)}) collective-permute-start(bf16[4,8,256]{2,1,0:T(8,128)(2,1)S(1)} %copy-done.21), channel_id=1, source_target_pairs={{0,1},{1,2},{2,3},{3,4},{4,5},{5,6},{6,7},{7,0},{8,9},{9,10},{10,1... | collective-permute-start | bytes 49160 | tf_op jit(solution)/shard_map/ppermute | solution.py:266
  127.2 4.8 %collective-permute-start.1 = (bf16[4,8,256]{2,1,0:T(8,128)(2,1)S(1)}, bf16[4,8,256]{2,1,0:T(8,128)(2,1)S(1)}, u32[]{:S(2)}, u32[]{:S(2)}) collective-permute-start(bf16[4,8,256]{2,1,0:T(8,128)(2,1)S(1)} %copy-done.20), channel_id=1, source_target_pairs={{0,2},{1,3},{2,4},{3,5},{4,6},{5,7},{6,0},{7,1},{8,10},{9,11},{10,... | collective-permute-start | bytes 49160 | tf_op jit(solution)/shard_map/ppermute | solution.py:266
  132.1 5.6 %collective-permute-start.2 = (bf16[4,8,256]{2,1,0:T(8,128)(2,1)S(1)}, bf16[4,8,256]{2,1,0:T(8,128)(2,1)S(1)}, u32[]{:S(2)}, u32[]{:S(2)}) collective-permute-start(bf16[4,8,256]{2,1,0:T(8,128)(2,1)S(1)} %copy-done.19), channel_id=1, source_target_pairs={{0,3},{1,4},{2,5},{3,6},{4,7},{5,0},{6,1},{7,2},{8,11},{9,12},{10,... | collective-permute-start | bytes 49160 | tf_op jit(solution)/shard_map/ppermute | solution.py:266
  137.7 6.5 %collective-permute-start.3 = (bf16[4,8,256]{2,1,0:T(8,128)(2,1)S(1)}, bf16[4,8,256]{2,1,0:T(8,128)(2,1)S(1)}, u32[]{:S(2)}, u32[]{:S(2)}) collective-permute-start(bf16[4,8,256]{2,1,0:T(8,128)(2,1)S(1)} %copy-done.18), channel_id=1, source_target_pairs={{0,4},{1,5},{2,6},{3,7},{4,0},{5,1},{6,2},{7,3},{8,12},{9,13},{10,... | collective-permute-start | bytes 49160 | tf_op jit(solution)/shard_map/ppermute | solution.py:266
  144.2 4.4 %collective-permute-start.4 = (bf16[4,8,256]{2,1,0:T(8,128)(2,1)S(1)}, bf16[4,8,256]{2,1,0:T(8,128)(2,1)S(1)}, u32[]{:S(2)}, u32[]{:S(2)}) collective-permute-start(bf16[4,8,256]{2,1,0:T(8,128)(2,1)S(1)} %copy-done.17), channel_id=1, source_target_pairs={{0,5},{1,6},{2,7},{3,0},{4,1},{5,2},{6,3},{7,4},{8,13},{9,14},{10,... | collective-permute-start | bytes 49160 | tf_op jit(solution)/shard_map/ppermute | solution.py:266
  148.6 3.5 %collective-permute-start.5 = (bf16[4,8,256]{2,1,0:T(8,128)(2,1)S(1)}, bf16[4,8,256]{2,1,0:T(8,128)(2,1)S(1)}, u32[]{:S(2)}, u32[]{:S(2)}) collective-permute-start(bf16[4,8,256]{2,1,0:T(8,128)(2,1)S(1)} %copy-done.16), channel_id=1, source_target_pairs={{0,6},{1,7},{2,0},{3,1},{4,2},{5,3},{6,4},{7,5},{8,14},{9,15},{10,... | collective-permute-start | bytes 49160 | tf_op jit(solution)/shard_map/ppermute | solution.py:266
  152.1 4.5 %collective-permute-start.6 = (bf16[4,8,256]{2,1,0:T(8,128)(2,1)}, bf16[4,8,256]{2,1,0:T(8,128)(2,1)S(1)}, u32[]{:S(2)}, u32[]{:S(2)}) collective-permute-start(bf16[4,8,256]{2,1,0:T(8,128)(2,1)} %get-tuple-element.30), channel_id=1, source_target_pairs={{0,7},{1,0},{2,1},{3,2},{4,3},{5,4},{6,5},{7,6},{8,15},{9,8},{10,9... | collective-permute-start | bytes 49160 | tf_op jit(solution)/shard_map/ppermute | solution.py:266
  158.7 4.2 %collective-permute-start.7 = (bf16[8,8,256]{2,1,0:T(8,128)(2,1)}, bf16[8,8,256]{2,1,0:T(8,128)(2,1)S(1)}, u32[]{:S(2)}, u32[]{:S(2)}) collective-permute-start(bf16[8,8,256]{2,1,0:T(8,128)(2,1)} %get-tuple-element.32), channel_id=1, source_target_pairs={{0,8},{1,9},{2,10},{3,11},{4,12},{5,13},{6,14},{7,15},{8,16},{9,17... | collective-permute-start | bytes 98312 | tf_op jit(solution)/shard_map/ppermute | solution.py:277
  162.9 4.5 %collective-permute-start.8 = (bf16[8,8,256]{2,1,0:T(8,128)(2,1)}, bf16[8,8,256]{2,1,0:T(8,128)(2,1)S(1)}, u32[]{:S(2)}, u32[]{:S(2)}) collective-permute-start(bf16[8,8,256]{2,1,0:T(8,128)(2,1)} %get-tuple-element.33), channel_id=1, source_target_pairs={{0,16},{1,17},{2,18},{3,19},{4,20},{5,21},{6,22},{7,23},{8,24},{9,... | collective-permute-start | bytes 98312 | tf_op jit(solution)/shard_map/ppermute | solution.py:277
  167.4 3.3 %collective-permute-start.9 = (bf16[8,8,256]{2,1,0:T(8,128)(2,1)}, bf16[8,8,256]{2,1,0:T(8,128)(2,1)S(1)}, u32[]{:S(2)}, u32[]{:S(2)}) collective-permute-start(bf16[8,8,256]{2,1,0:T(8,128)(2,1)} %get-tuple-element.34), channel_id=1, source_target_pairs={{0,24},{1,25},{2,26},{3,27},{4,28},{5,29},{6,30},{7,31},{8,0},{9,1... | collective-permute-start | bytes 98312 | tf_op jit(solution)/shard_map/ppermute | solution.py:277
  (16 other events, 343.7 us)
where the time goes:
time: 237 us
  Pallas kernels  83.3 us (35%)
  waiting for transfers between devices  57.8 us (24%)
  blocking collectives  50.7 us (21%)
  starting transfers between devices  42.2 us (18%)
    pallas_call x1, Pallas kernels, body(): pl.pallas_call(prologue_kernel, in_specs=[smem, vmem, vmem, hbm, hbm, hbm...  67.1 us
    all_to_all x1, blocking collectives, exchange(): lax.all_to_all(value.reshape(sections * columns, tile, size), ('pipe', 's...  50.7 us
    ppermute x3, waiting for transfers between devices, body(): piece = lax.ppermute(pieces[d], 'pipe', route) if d else pieces[0]  28.9 us
    ppermute x7, waiting for transfers between devices, body(): arrived.append(lax.ppermute(cot_rows[d], 'space', route))  18.9 us
    all_to_all x1, starting transfers between devices, exchange(): lax.all_to_all(value.reshape(sections * columns, tile, size), ('pipe', 's...  15.7 us
    ppermute x7, starting transfers between devices, body(): arrived.append(lax.ppermute(cot_rows[d], 'space', route))  15.1 us
    pallas_call x1, Pallas kernels, body(): pl.pallas_call(chain_kernel, in_specs=[smem] + [vmem] * (4 + X) + [hbm] *...  10.4 us
    ppermute x3, waiting for transfers between devices, body(): cots.append(lax.ppermute(turned[e], 'space', route))  9.92 us
  transfers between devices with their start and end apart: 18, of which 12 were waited for; matrix products, arithmetic and copies ran while one was open for 0% of the time, Pallas kernels for 1%

commit v1 on v0

v1 whole, which is shorter than its diff:
```python
import math

import jax
import jax.numpy as jnp
import numpy as np
from jax import lax
from jax.experimental import pallas as pl
from jax.experimental.pallas import tpu as pltpu
from jax.sharding import Mesh
from jax.sharding import PartitionSpec as P


BF16 = jnp.bfloat16
F32 = jnp.float32
X, Y, Z = 4, 4, 8
EVERYONE = ("z", "core", "x", "y")


def two_parts(table):
    high = table.astype(np.float32).astype(BF16)
    low = (table - high.astype(np.float64)).astype(np.float32).astype(BF16)
    return np.concatenate([high, low], axis=1)


def row_matrix(rows, width, columns):
    modes = width // 2
    pair = modes // columns
    angles = 2.0 * math.pi * (np.outer(np.arange(modes), np.arange(width)) % width) / width
    scale = 1.0 / math.sqrt(width)
    parts = np.stack([np.cos(angles), -np.sin(angles)]) * scale
    table = np.zeros((columns, rows, 2, pair, rows, width))
    by_column = parts.reshape(2, columns, pair, width).transpose(1, 0, 2, 3)
    for h in range(rows):
        table[:, h, :, :, h, :] = by_column
    return table.reshape(columns * rows * 2 * pair, rows * width)


def column_matrix(height, pair):
    angles = 2.0 * math.pi * (np.outer(np.arange(height), np.arange(height)) % height) / height
    scale = 1.0 / math.sqrt(height)
    cosines, sines = np.cos(angles) * scale, np.sin(angles) * scale
    table = np.zeros((2, pair, height, height, 2, pair))
    for k in range(pair):
        table[0, k, :, :, 0, k] = cosines
        table[0, k, :, :, 1, k] = sines
        table[1, k, :, :, 1, k] = cosines
        table[1, k, :, :, 0, k] = -sines
    return table.reshape(2 * pair * height, 2 * pair * height)


def fold_matrices(height, pair):
    size = 2 * pair * height
    plain = np.eye(size)
    folded = np.eye(size).reshape(2, pair, height, 2, pair, height)
    eye = np.eye(height)
    flip = eye[(-np.arange(height)) % height]
    folded[0, 0, :, 0, 0, :] = 0.5 * (eye + flip)
    folded[1, 0, :, 1, 0, :] = 0.5 * (eye - flip)
    return np.stack([plain, folded.reshape(size, size)]).astype(np.float32).astype(BF16)


def dot(left, right):
    return jnp.dot(left, right, preferred_element_type=F32)


def dot_t(left, right):
    return lax.dot_general(left, right, (((1,), (1,)), ((), ())), preferred_element_type=F32)


def gelu_slope(values):
    return (
        0.5 * (1.0 + lax.erf(values * 0.7071067811865476))
        + values * jnp.exp(-0.5 * values * values) * 0.3989422804014327
    )


def twice(table_ref, operand):
    depth = operand.shape[0]
    return dot(table_ref[:, :depth], operand) + dot(table_ref[:, depth:], operand)


def prologue_kernel(table_ref, act_ref, cot_ref, first_ref, second_ref, bias_ref, *rest):
    pieces, rows_ref, cots = rest[:Y], rest[Y], rest[Y + 1 : Y + 1 + Z]
    cot_buf, held, found, sems, cot_sem = rest[Y + 1 + Z :]
    size = cot_buf.shape[1] // 2
    y, core, x, z = (lax.axis_index(name) for name in ("y", "core", "x", "z"))
    odd = x & 1
    cot_copy = pltpu.make_async_copy(cot_ref.at[:, pl.ds(y * 2 * size, 2 * size)], cot_buf, cot_sem)
    cot_copy.start()
    loads = []
    for d in range(Y):
        block = ((y + d) & (Y - 1)) * 2 + odd
        for i in range(2):
            for j, ref in enumerate((first_ref, second_ref)):
                copy = pltpu.make_async_copy(
                    ref.at[0, i, block],
                    held.at[d, pl.ds((2 * j + i) * size, size)],
                    sems.at[d, 2 * j + i],
                )
                copy.start()
                loads.append(copy)

    count = table_ref.shape[0]
    line = lax.broadcasted_iota(jnp.int32, (count, size), 0)
    factor = jnp.where(jnp.logical_and(line < 8, (line & 1) == 0), 1.0, 2.0).astype(F32)
    cot_copy.wait()
    for k in range(2):
        spectrum = (twice(table_ref, cot_buf[:, k * size : (k + 1) * size]) * factor).astype(BF16)
        found[k] = spectrum.reshape(Z, 2, 2, 8, size)
    for d in range(Z):
        to = (z + d) & (Z - 1)
        for k in range(X):
            cots[d][k] = found[k & 1, to, core, k >> 1]

    for d in range(Y):
        block = ((y + d) & (Y - 1)) * 2 + odd
        bias = bias_ref[0, :, pl.ds(block * size, size)]
        high = bias.astype(BF16).astype(F32)
        middle = (bias - high).astype(BF16).astype(F32)
        low = bias - high - middle
        packed = jnp.concatenate([high, middle, low, jnp.zeros((10, size), F32)], axis=0)
        held[d, 4 * size : 4 * size + 16] = packed.astype(BF16)
    for copy in loads:
        copy.wait()
    stores = []
    for d in range(Y):
        copy = pltpu.make_async_copy(held.at[d], pieces[d], sems.at[d, 4])
        copy.start()
        stores.append(copy)

    for n in range(2 * Y):
        spectrum = twice(table_ref, act_ref[:, n * size : (n + 1) * size]).astype(BF16)
        rows_ref[:, :, :, n % 2, n // 2] = spectrum.reshape(Z, 2, 2, 8, size)
    for copy in stores:
        copy.wait()


def turn_kernel(*refs):
    arrived, outs = refs[:Z], refs[Z:]
    x = lax.axis_index("x")
    for e in range(X):
        to = (x + e) & (X - 1)
        for d in range(Z):
            outs[e][d] = arrived[d][to]


def inverse_kernel(table_ref, spec_ref, cot_ref, out_ref, result, sems):
    rows = table_ref.shape[0]
    size = spec_ref.shape[6]
    copies = []
    for n in range(2 * Y):
        block = slice(n * size, (n + 1) * size)
        field = twice(table_ref, spec_ref[:, :, :, n % 2, n // 2].reshape(rows, size))
        result[:, block] = (field + cot_ref[:, block].astype(F32)).astype(BF16)
        copy = pltpu.make_async_copy(result.at[:, block], out_ref.at[:, block], sems.at[n])
        copy.start()
        copies.append(copy)
    for copy in copies:
        copy.wait()


def chain_kernel(act_ref, col_ref, inv_ref, fold_ref, *rest):
    sections = 2 * Y
    cots, weights = rest[:X], rest[X : X + sections]
    out_ref, held, found, sems = rest[X + sections :]
    size = act_ref.shape[6]
    half = col_ref.shape[0] // 2
    y, core, x, z = (lax.axis_index(name) for name in ("y", "core", "x", "z"))
    copies = []
    for d in range(Y):
        for i in range(2):
            slot = ((y - d) & (Y - 1)) * 2 + (core if i == 0 else 1 - core)
            copy = pltpu.make_async_copy(weights[2 * d + i], held.at[slot], sems.at[2 * d + i])
            copy.start()
            copies.append(copy)
    for e in range(X):
        for d in range(Z):
            found[(z - d) & (Z - 1), (x - e) & (X - 1)] = cots[e][d]
    has_zero = jnp.logical_and(jnp.logical_and(core == 0, x < 2), z == 0)
    fold = jnp.where(has_zero, 1, 0)

    base = twice(col_ref, found[...].reshape(2 * half, size))
    total = jnp.zeros_like(base)
    height_total = jnp.zeros_like(base)
    grad = base.astype(BF16)
    spectra = []
    for p in range(sections):
        columns = act_ref[:, p % 2, :, :, p // 2].reshape(2 * half, size)
        spectra.append(twice(col_ref, columns).astype(BF16))
    for copy in copies:
        copy.wait()

    for p in range(sections - 1, -1, -1):
        a_re, a_im = held[p, 0:size], held[p, size : 2 * size]
        b_re, b_im = held[p, 2 * size : 3 * size], held[p, 3 * size : 4 * size]
        bias = held[p, 4 * size : 4 * size + 16].astype(F32)
        bias_re = bias[0:1] + bias[2:3] + bias[4:5]
        bias_im = bias[1:2] + bias[3:4] + bias[5:6]
        s = spectra[p]
        s_turned = jnp.concatenate([-s[half:], s[:half]], axis=0)
        z_both = dot(s, a_re) + dot(s_turned, a_im)
        slope = gelu_slope(jnp.concatenate([z_both[:half] + bias_re, z_both[half:] + bias_im], axis=0))
        g_turned = jnp.concatenate([grad[half:], -grad[:half]], axis=0)
        u = dot_t(grad, b_re) + dot_t(g_turned, b_im)
        q = (u * slope).astype(BF16)
        q_turned = jnp.concatenate([q[half:], -q[:half]], axis=0)
        e = (dot_t(q, a_re) + dot_t(q_turned, a_im)).astype(BF16)
        height_total = height_total + twice(inv_ref, e)
        out_ref[:, p % 2, :, :, p // 2] = height_total.astype(BF16).reshape(Z, 2, 2, 8, size)
        if p > 0:
            total = total + dot(fold_ref[fold], e)
            grad = (base + total).astype(BF16)


def body(activations, cotangent, w_first, w_second, b_first):
    sections, columns = 2 * Y, X * Z
    _, rows, width, channels = activations.shape
    size = w_first.shape[3]
    height = rows * columns
    pair = width // 2 // columns
    count = rows * width
    tile = 2 * rows * pair
    row_table = row_matrix(rows, width, columns)
    row_table = row_table.reshape(2, 2, Z, -1).transpose(2, 0, 1, 3).reshape(row_table.shape)
    forward_rows, inverse_rows = two_parts(row_table), two_parts(row_table.T)
    column_table = column_matrix(height, pair)
    column_table = column_table.reshape(-1, X, Z, tile).transpose(0, 2, 1, 3).reshape(column_table.shape)
    forward_columns, inverse_columns = two_parts(column_table), two_parts(column_table.T)
    folds = fold_matrices(height, pair)

    vmem = pl.BlockSpec(memory_space=pltpu.VMEM)
    hbm = pl.BlockSpec(memory_space=pl.ANY)
    blocks = (Z, 2, 2, 2, Y, tile, size)

    def shaped(*dims):
        return jax.ShapeDtypeStruct(dims, BF16)

    def exchange(value):
        flat = value.reshape(sections * columns, tile, size)
        return lax.all_to_all(flat, EVERYONE, split_axis=0, concat_axis=0, tiled=True).reshape(blocks)

    def shifted(value, axis, distance):
        size = lax.axis_size(axis)
        return lax.ppermute(value, axis, [(i, (i + distance) % size) for i in range(size)])

    flat_cot = cotangent.reshape(count, channels)
    made = pl.pallas_call(
        prologue_kernel,
        in_specs=[vmem, vmem, hbm, hbm, hbm, vmem],
        out_specs=[hbm] * Y + [vmem] * (1 + Z),
        out_shape=[shaped(4 * size + 16, size)] * Y + [shaped(*blocks)] + [shaped(X, tile, size)] * Z,
        scratch_shapes=[
            pltpu.VMEM((count, 2 * size), BF16),
            pltpu.VMEM((Y, 4 * size + 16, size), BF16),
            pltpu.VMEM((2, Z, 2, 2, tile, size), BF16),
            pltpu.SemaphoreType.DMA((Y, 5)),
            pltpu.SemaphoreType.DMA(()),
        ],
        name="prologue",
    )(forward_rows, activations.reshape(count, channels), flat_cot, w_first, w_second, b_first)
    pieces, act_rows, cot_rows = made[:Y], made[Y], made[Y + 1 :]

    arrived = [cot_rows[0]]
    arrived += [shifted(cot_rows[d], "z", d) for d in range(1, Z)]
    weights = []
    for d in range(Y):
        piece = shifted(pieces[d], "y", d) if d else pieces[0]
        weights += [piece, shifted(piece, "core", 1)]
    act_columns = exchange(act_rows)
    turned = pl.pallas_call(
        turn_kernel,
        in_specs=[vmem] * Z,
        out_specs=[vmem] * X,
        out_shape=[shaped(Z, tile, size)] * X,
        name="turn",
    )(*arrived)
    cots = [turned[0]] + [shifted(turned[e], "x", e) for e in range(1, X)]

    back = pl.pallas_call(
        chain_kernel,
        in_specs=[vmem] * (4 + X) + [hbm] * sections,
        out_specs=vmem,
        out_shape=shaped(*blocks),
        scratch_shapes=[
            pltpu.VMEM((sections, 4 * size + 16, size), BF16),
            pltpu.VMEM((Z, X, tile, size), BF16),
            pltpu.SemaphoreType.DMA((sections,)),
        ],
        name="chain",
    )(act_columns, forward_columns, inverse_columns, folds, *cots, *weights)
    grads = pl.pallas_call(
        inverse_kernel,
        in_specs=[vmem] * 3,
        out_specs=hbm,
        out_shape=shaped(count, channels),
        scratch_shapes=[pltpu.VMEM((count, channels), BF16), pltpu.SemaphoreType.DMA((sections,))],
        name="inverse_rows",
    )(inverse_rows, exchange(back), flat_cot)
    return grads.reshape(1, rows, width, channels)


def solution(mesh):
    chips = Mesh(mesh.devices.reshape(Y, 2, X, Z), ("y", "core", "x", "z"))
    pipe, space = ("y", "core"), ("x", "z")
    in_specs = (
        P(pipe, space, None, None),
        P(space, None, None),
        P(pipe, None, None, None, None),
        P(pipe, None, None, None, None),
        P(pipe, None, None),
    )
    out_specs = P(pipe, space, None, None)
    return jax.shard_map(body, mesh=chips, in_specs=in_specs, out_specs=out_specs, check_vma=False)
```

time: 237 us -> 172 us (0.73)
  Pallas kernels: 83.3 us -> 20.8 us
  blocking collectives: 50.7 us -> 48.3 us
    pallas_call x4, Pallas kernels: 83.3 us -> 20.8 us  [the longest x1 10.4 us: body(): pl.pallas_call(chain_kernel, in_specs=[vmem] * (4 + X) + [hbm] * sections...]
    all_to_all x1, blocking collectives: 50.7 us -> 48.3 us  [exchange(): lax.all_to_all(flat, EVERYONE, split_axis=0, concat_axis=0, tiled=True)]
where the time goes in v1:
time: 172 us
  waiting for transfers between devices  59 us (34%)
  blocking collectives  48.3 us (28%)
  starting transfers between devices  41.5 us (24%)
  Pallas kernels  20.8 us (12%)
    ppermute x17, waiting for transfers between devices, shifted(): lax.ppermute(value, axis, [(i, (i + distance) % size) for i in range(size)])  59 us
    all_to_all x1, blocking collectives, exchange(): lax.all_to_all(flat, EVERYONE, split_axis=0, concat_axis=0, tiled=True)  48.3 us
    ppermute x17, starting transfers between devices, shifted(): lax.ppermute(value, axis, [(i, (i + distance) % size) for i in range(size)])  25.9 us
    all_to_all x1, starting transfers between devices, exchange(): lax.all_to_all(flat, EVERYONE, split_axis=0, concat_axis=0, tiled=True)  15.7 us
    pallas_call x1, Pallas kernels, body(): pl.pallas_call(chain_kernel, in_specs=[vmem] * (4 + X) + [hbm] * sections...  10.4 us
    pallas_call x1, Pallas kernels, body(): pl.pallas_call(prologue_kernel, in_specs=[vmem, vmem, hbm, hbm, hbm, vmem...  5.77 us
  transfers between devices with their start and end apart: 18, of which 12 were waited for; matrix products, arithmetic and copies ran while one was open for 0% of the time, Pallas kernels for 1%

profile of v1, /device:TPU:1, one launch (start us, length us, event | category | flops | bytes accessed | tf_op | source)
XLA Modules:
  0.0 171.5 jit_solution(17350507051440541179)
XLA Ops:
  0.0 5.8 %prologue.1 = (bf16[1040,256]{1,0:T(8,128)(2,1)}, bf16[1040,256]{1,0:T(8,128)(2,1)}, bf16[1040,256]{1,0:T(8,128)(2,1)}, bf16[1040,256]{1,0:T(8,128)(2,1)}, bf16[...) custom-call(bf16[256,512]{1,0:T(8,128)(2,1)} %constant.10.clone.tabl, ...), custom_call_target="tpu_custom_call" | custom-call | tf_op jit(solution)/shard_map/prologue/pallas_call | solution.py:247
  5.9 15.7 %all-to-all-start = ((bf16[256,8,256]{2,1,0:T(8,128)(2,1)}), bf16[256,8,256]{2,1,0:T(8,128)(2,1)S(1)}, u32[]{:S(2)}, u32[]{:S(2)}) async-start(bf16[256,8,256]{2,1,0:T(8,128)(2,1)} %bitcast.13), calls=%async_computation | async-start | bytes 2097152 | tf_op jit(solution)/shard_map/all_to_all | solution.py:240
  21.5 1.4 collective-permute-start.11
  23.0 2.5 %collective-permute-start.13 = (bf16[1040,256]{1,0:T(8,128)(2,1)}, bf16[1040,256]{1,0:T(8,128)(2,1)S(1)}, u32[]{:S(2)}, u32[]{:S(2)}) collective-permute-start(bf16[1040,256]{1,0:T(8,128)(2,1)} %get-tuple-element.37), channel_id=1, source_target_pairs={{0,128},{64,192},{128,0},{192,64},{1,129},{65,193},{129,1},{193,65... | collective-permute-start | bytes 1597448 | tf_op jit(solution)/shard_map/ppermute | solution.py:244
  27.8 15.3 %collective-permute-done.11.rest_6_ = bf16[1040,256]{1,0:T(8,128)(2,1)S(1)} collective-permute-done((bf16[1040,256]{1,0:T(8,128)(2,1)}, bf16[1040,256]{1,0:T(8,128)(2,1)S(1)}, u32[]{:S(2)}, u32[]{:S(2)}) %collective-permute-start.11) | collective-permute-done | bytes 532512 | tf_op jit(solution)/shard_map/ppermute | solution.py:244
  43.1 3.1 %collective-permute-start.12 = (bf16[1040,256]{1,0:T(8,128)(2,1)S(1)}, bf16[1040,256]{1,0:T(8,128)(2,1)}, u32[]{:S(2)}, u32[]{:S(2)}) collective-permute-start(bf16[1040,256]{1,0:T(8,128)(2,1)S(1)} %collective-permute-done.11.rest_6_), channel_id=1, source_target_pairs={{0,32},{32,0},{1,33},{33,1},{2,34},{34,2},{3,35},{35,3},{4,36},{36... | collective-permute-start | bytes 1597448 | tf_op jit(solution)/shard_map/ppermute | solution.py:244
  46.2 13.4 %collective-permute-done.13.rest_8_ = bf16[1040,256]{1,0:T(8,128)(2,1)S(1)} collective-permute-done((bf16[1040,256]{1,0:T(8,128)(2,1)}, bf16[1040,256]{1,0:T(8,128)(2,1)S(1)}, u32[]{:S(2)}, u32[]{:S(2)}) %collective-permute-start.13) | collective-permute-done | bytes 532512 | tf_op jit(solution)/shard_map/ppermute | solution.py:244
  60.6 1.3 collective-permute-start
  61.9 3.4 %collective-permute-done.refs_1_ = bf16[4,8,256]{2,1,0:T(8,128)(2,1)S(1)} collective-permute-done((bf16[4,8,256]{2,1,0:T(8,128)(2,1)S(1)}, bf16[4,8,256]{2,1,0:T(8,128)(2,1)S(1)}, u32[]{:S(2)}, u32[]{:S(2)}) %collective-permute-start) | collective-permute-done | bytes 16416 | tf_op jit(solution)/shard_map/ppermute | solution.py:244
  65.5 4.7 %collective-permute-done.1.refs_2_ = bf16[4,8,256]{2,1,0:T(8,128)(2,1)S(1)} collective-permute-done((bf16[4,8,256]{2,1,0:T(8,128)(2,1)S(1)}, bf16[4,8,256]{2,1,0:T(8,128)(2,1)S(1)}, u32[]{:S(2)}, u32[]{:S(2)}) %collective-permute-start.1) | collective-permute-done | bytes 16416 | tf_op jit(solution)/shard_map/ppermute | solution.py:244
  70.7 5.2 %collective-permute-done.2.refs_3_ = bf16[4,8,256]{2,1,0:T(8,128)(2,1)S(1)} collective-permute-done((bf16[4,8,256]{2,1,0:T(8,128)(2,1)S(1)}, bf16[4,8,256]{2,1,0:T(8,128)(2,1)S(1)}, u32[]{:S(2)}, u32[]{:S(2)}) %collective-permute-start.2) | collective-permute-done | bytes 16416 | tf_op jit(solution)/shard_map/ppermute | solution.py:244
  76.0 4.4 %collective-permute-start.3 = (bf16[4,8,256]{2,1,0:T(8,128)(2,1)S(1)}, bf16[4,8,256]{2,1,0:T(8,128)(2,1)S(1)}, u32[]{:S(2)}, u32[]{:S(2)}) collective-permute-start(bf16[4,8,256]{2,1,0:T(8,128)(2,1)S(1)} %copy-done.18), channel_id=1, source_target_pairs={{0,4},{1,5},{2,6},{3,7},{4,0},{5,1},{6,2},{7,3},{8,12},{9,13},{10,... | collective-permute-start | bytes 49160 | tf_op jit(solution)/shard_map/ppermute | solution.py:244
  80.3 2.1 %collective-permute-done.3.refs_4_ = bf16[4,8,256]{2,1,0:T(8,128)(2,1)S(1)} collective-permute-done((bf16[4,8,256]{2,1,0:T(8,128)(2,1)S(1)}, bf16[4,8,256]{2,1,0:T(8,128)(2,1)S(1)}, u32[]{:S(2)}, u32[]{:S(2)}) %collective-permute-start.3) | collective-permute-done | bytes 16416 | tf_op jit(solution)/shard_map/ppermute | solution.py:244
  82.5 2.5 %collective-permute-start.4 = (bf16[4,8,256]{2,1,0:T(8,128)(2,1)S(1)}, bf16[4,8,256]{2,1,0:T(8,128)(2,1)S(1)}, u32[]{:S(2)}, u32[]{:S(2)}) collective-permute-start(bf16[4,8,256]{2,1,0:T(8,128)(2,1)S(1)} %copy-done.17), channel_id=1, source_target_pairs={{0,5},{1,6},{2,7},{3,0},{4,1},{5,2},{6,3},{7,4},{8,13},{9,14},{10,... | collective-permute-start | bytes 49160 | tf_op jit(solution)/shard_map/ppermute | solution.py:244
  84.9 1.9 %collective-permute-done.4.refs_5_ = bf16[4,8,256]{2,1,0:T(8,128)(2,1)S(1)} collective-permute-done((bf16[4,8,256]{2,1,0:T(8,128)(2,1)S(1)}, bf16[4,8,256]{2,1,0:T(8,128)(2,1)S(1)}, u32[]{:S(2)}, u32[]{:S(2)}) %collective-permute-start.4) | collective-permute-done | bytes 16416 | tf_op jit(solution)/shard_map/ppermute | solution.py:244
  86.9 2.3 %collective-permute-start.5 = (bf16[4,8,256]{2,1,0:T(8,128)(2,1)S(1)}, bf16[4,8,256]{2,1,0:T(8,128)(2,1)S(1)}, u32[]{:S(2)}, u32[]{:S(2)}) collective-permute-start(bf16[4,8,256]{2,1,0:T(8,128)(2,1)S(1)} %copy-done.16), channel_id=1, source_target_pairs={{0,6},{1,7},{2,0},{3,1},{4,2},{5,3},{6,4},{7,5},{8,14},{9,15},{10,... | collective-permute-start | bytes 49160 | tf_op jit(solution)/shard_map/ppermute | solution.py:244
  90.3 3.2 %collective-permute-start.6 = (bf16[4,8,256]{2,1,0:T(8,128)(2,1)S(1)}, bf16[4,8,256]{2,1,0:T(8,128)(2,1)S(1)}, u32[]{:S(2)}, u32[]{:S(2)}) collective-permute-start(bf16[4,8,256]{2,1,0:T(8,128)(2,1)S(1)} %copy-done.15), channel_id=1, source_target_pairs={{0,7},{1,0},{2,1},{3,2},{4,3},{5,4},{6,5},{7,6},{8,15},{9,8},{10,9... | collective-permute-start | bytes 49160 | tf_op jit(solution)/shard_map/ppermute | solution.py:244
  95.1 1.5 turn.1
  97.3 3.5 %collective-permute-done.7.rest_1_ = bf16[8,8,256]{2,1,0:T(8,128)(2,1)S(1)} collective-permute-done((bf16[8,8,256]{2,1,0:T(8,128)(2,1)}, bf16[8,8,256]{2,1,0:T(8,128)(2,1)S(1)}, u32[]{:S(2)}, u32[]{:S(2)}) %collective-permute-start.7) | collective-permute-done | bytes 32800 | tf_op jit(solution)/shard_map/ppermute | solution.py:244
  100.9 4.3 %collective-permute-done.8.rest_2_ = bf16[8,8,256]{2,1,0:T(8,128)(2,1)S(1)} collective-permute-done((bf16[8,8,256]{2,1,0:T(8,128)(2,1)}, bf16[8,8,256]{2,1,0:T(8,128)(2,1)S(1)}, u32[]{:S(2)}, u32[]{:S(2)}) %collective-permute-start.8) | collective-permute-done | bytes 32800 | tf_op jit(solution)/shard_map/ppermute | solution.py:244
  105.5 3.0 %collective-permute-done.9.rest_3_ = bf16[8,8,256]{2,1,0:T(8,128)(2,1)S(1)} collective-permute-done((bf16[8,8,256]{2,1,0:T(8,128)(2,1)}, bf16[8,8,256]{2,1,0:T(8,128)(2,1)S(1)}, u32[]{:S(2)}, u32[]{:S(2)}) %collective-permute-start.9) | collective-permute-done | bytes 32800 | tf_op jit(solution)/shard_map/ppermute | solution.py:244
  109.5 10.4 %chain.1 = bf16[8,2,2,2,4,8,256]{6,5,4,3,2,1,0:T(8,128)(2,1)} custom-call(bf16[8,2,2,2,4,8,256]{6,5,4,3,2,1,0:T(8,128)(2,1)} %bitcast.9, bf16[256,512]{1,0:T(8,128)(2,1)} %constant.11.clone.col_ref, bf16[256,512]{1,0:T(8,128)(2,1)} %constant.12.clone.inv_ref, bf16[2,256,256]{2,1,0:T(8,128)(2,1)} %constant.13.clone.fold_ref, ...), custom_call_target="tpu_custom_call" | custom-call | tf_op jit(solution)/shard_map/chain/pallas_call | solution.py:279
  119.9 48.3 %all_to_all.10 = bf16[256,8,256]{2,1,0:T(8,128)(2,1)} all-to-all(bf16[256,8,256]{2,1,0:T(8,128)(2,1)} %bitcast.10), channel_id=1, replica_groups=mesh['y'=4,'core'=2,'x'=4,'z'=8] {'z','core','x','y'}, dimensions={0} | all-to-all | bytes 2097152 | tf_op jit(solution)/shard_map/all_to_all | solution.py:240
  168.2 3.2 %inverse_rows.1 = bf16[256,2048]{1,0:T(8,128)(2,1)} custom-call(bf16[256,512]{1,0:T(8,128)(2,1)} %constant.14.clone.table_ref, bf16[8,2,2,2,4,8,256]{6,5,4,3,2,1,0:T(8,128)(2,1)} %bitcast.11, bf16[256,2048]{1,0:T(8,128)(2,1)} %bitcast.8), custom_call_target="tpu_custom_call" | custom-call | tf_op jit(solution)/shard_map/inverse_rows/pallas_call | solution.py:291
  (61 shorter events, 8.9 us)
Async XLA Ops:
  5.8 64.4 %copy-start.19 = (bf16[4,8,256]{2,1,0:T(8,128)(2,1)S(1)}, bf16[4,8,256]{2,1,0:T(8,128)(2,1)}, u32[]{:S(2)}) copy-start(bf16[4,8,256]{2,1,0:T(8,128)(2,1)} %get-tuple-element.26) | copy-start | bytes 49156
  5.8 70.1 %copy-start.18 = (bf16[4,8,256]{2,1,0:T(8,128)(2,1)S(1)}, bf16[4,8,256]{2,1,0:T(8,128)(2,1)}, u32[]{:S(2)}) copy-start(bf16[4,8,256]{2,1,0:T(8,128)(2,1)} %get-tuple-element.27) | copy-start | bytes 49156
  5.8 76.6 %copy-start.17 = (bf16[4,8,256]{2,1,0:T(8,128)(2,1)S(1)}, bf16[4,8,256]{2,1,0:T(8,128)(2,1)}, u32[]{:S(2)}) copy-start(bf16[4,8,256]{2,1,0:T(8,128)(2,1)} %get-tuple-element.28) | copy-start | bytes 49156
  5.8 81.0 %copy-start.16 = (bf16[4,8,256]{2,1,0:T(8,128)(2,1)S(1)}, bf16[4,8,256]{2,1,0:T(8,128)(2,1)}, u32[]{:S(2)}) copy-start(bf16[4,8,256]{2,1,0:T(8,128)(2,1)} %get-tuple-element.29) | copy-start | bytes 49156
  5.8 84.5 %copy-start.15 = (bf16[4,8,256]{2,1,0:T(8,128)(2,1)S(1)}, bf16[4,8,256]{2,1,0:T(8,128)(2,1)}, u32[]{:S(2)}) copy-start(bf16[4,8,256]{2,1,0:T(8,128)(2,1)} %get-tuple-element.30) | copy-start | bytes 49156
  5.9 102.7 %all-to-all-start = ((bf16[256,8,256]{2,1,0:T(8,128)(2,1)}), bf16[256,8,256]{2,1,0:T(8,128)(2,1)S(1)}, u32[]{:S(2)}, u32[]{:S(2)}) async-start(bf16[256,8,256]{2,1,0:T(8,128)(2,1)} %bitcast.13), calls=%async_computation | async-start | bytes 2097152 | tf_op jit(solution)/shard_map/all_to_all | solution.py:240
  21.5 21.5 %collective-permute-start.11 = (bf16[1040,256]{1,0:T(8,128)(2,1)}, bf16[1040,256]{1,0:T(8,128)(2,1)S(1)}, u32[]{:S(2)}, u32[]{:S(2)}) collective-permute-start(bf16[1040,256]{1,0:T(8,128)(2,1)} %get-tuple-element.36), channel_id=1, source_target_pairs={{0,64},{64,128},{128,192},{192,0},{1,65},{65,129},{129,193},{193,1... | collective-permute-start | bytes 1597448 | tf_op jit(solution)/shard_map/ppermute | solution.py:244
  23.0 36.6 %collective-permute-start.13 = (bf16[1040,256]{1,0:T(8,128)(2,1)}, bf16[1040,256]{1,0:T(8,128)(2,1)S(1)}, u32[]{:S(2)}, u32[]{:S(2)}) collective-permute-start(bf16[1040,256]{1,0:T(8,128)(2,1)} %get-tuple-element.37), channel_id=1, source_target_pairs={{0,128},{64,192},{128,0},{192,64},{1,129},{65,193},{129,1},{193,65... | collective-permute-start | bytes 1597448 | tf_op jit(solution)/shard_map/ppermute | solution.py:244
  25.4 35.1 %collective-permute-start.15 = (bf16[1040,256]{1,0:T(8,128)(2,1)}, bf16[1040,256]{1,0:T(8,128)(2,1)S(1)}, u32[]{:S(2)}, u32[]{:S(2)}) collective-permute-start(bf16[1040,256]{1,0:T(8,128)(2,1)} %get-tuple-element.38), channel_id=1, source_target_pairs={{0,192},{64,0},{128,64},{192,128},{1,193},{65,1},{129,65},{193,129... | collective-permute-start | bytes 1597448 | tf_op jit(solution)/shard_map/ppermute | solution.py:244
  26.5 82.0 %collective-permute-start.10 = (bf16[1040,256]{1,0:T(8,128)(2,1)S(1)}, bf16[1040,256]{1,0:T(8,128)(2,1)}, u32[]{:S(2)}, u32[]{:S(2)}) collective-permute-start(bf16[1040,256]{1,0:T(8,128)(2,1)S(1)} %copy-done.1), channel_id=1, source_target_pairs={{0,32},{32,0},{1,33},{33,1},{2,34},{34,2},{3,35},{35,3},{4,36},{36... | collective-permute-start | bytes 1597448 | tf_op jit(solution)/shard_map/ppermute | solution.py:244
  43.1 65.5 %copy-start.2 = (bf16[1040,256]{1,0:T(8,128)(2,1)}, bf16[1040,256]{1,0:T(8,128)(2,1)S(1)}, u32[]{:S(2)}) copy-start(bf16[1040,256]{1,0:T(8,128)(2,1)S(1)} %collective-permute-done.11.rest_6_) | copy-start | bytes 1597444
  43.1 65.4 %collective-permute-start.12 = (bf16[1040,256]{1,0:T(8,128)(2,1)S(1)}, bf16[1040,256]{1,0:T(8,128)(2,1)}, u32[]{:S(2)}, u32[]{:S(2)}) collective-permute-start(bf16[1040,256]{1,0:T(8,128)(2,1)S(1)} %collective-permute-done.11.rest_6_), channel_id=1, source_target_pairs={{0,32},{32,0},{1,33},{33,1},{2,34},{34,2},{3,35},{35,3},{4,36},{36... | collective-permute-start | bytes 1597448 | tf_op jit(solution)/shard_map/ppermute | solution.py:244
  59.5 49.0 %collective-permute-start.14 = (bf16[1040,256]{1,0:T(8,128)(2,1)S(1)}, bf16[1040,256]{1,0:T(8,128)(2,1)}, u32[]{:S(2)}, u32[]{:S(2)}) collective-permute-start(bf16[1040,256]{1,0:T(8,128)(2,1)S(1)} %collective-permute-done.13.rest_8_), channel_id=1, source_target_pairs={{0,32},{32,0},{1,33},{33,1},{2,34},{34,2},{3,35},{35,3},{4,36},{36... | collective-permute-start | bytes 1597448 | tf_op jit(solution)/shard_map/ppermute | solution.py:244
  60.5 48.1 %collective-permute-start.16 = (bf16[1040,256]{1,0:T(8,128)(2,1)S(1)}, bf16[1040,256]{1,0:T(8,128)(2,1)}, u32[]{:S(2)}, u32[]{:S(2)}) collective-permute-start(bf16[1040,256]{1,0:T(8,128)(2,1)S(1)} %collective-permute-done.15.rest_10_), channel_id=1, source_target_pairs={{0,32},{32,0},{1,33},{33,1},{2,34},{34,2},{3,35},{35,3},{4,36},{36... | collective-permute-start | bytes 1597448 | tf_op jit(solution)/shard_map/ppermute | solution.py:244
  60.6 4.7 %collective-permute-start = (bf16[4,8,256]{2,1,0:T(8,128)(2,1)S(1)}, bf16[4,8,256]{2,1,0:T(8,128)(2,1)S(1)}, u32[]{:S(2)}, u32[]{:S(2)}) collective-permute-start(bf16[4,8,256]{2,1,0:T(8,128)(2,1)S(1)} %copy-done.21), channel_id=1, source_target_pairs={{0,1},{1,2},{2,3},{3,4},{4,5},{5,6},{6,7},{7,0},{8,9},{9,10},{10,1... | collective-permute-start | bytes 49160 | tf_op jit(solution)/shard_map/ppermute | solution.py:244
  65.3 4.9 %collective-permute-start.1 = (bf16[4,8,256]{2,1,0:T(8,128)(2,1)S(1)}, bf16[4,8,256]{2,1,0:T(8,128)(2,1)S(1)}, u32[]{:S(2)}, u32[]{:S(2)}) collective-permute-start(bf16[4,8,256]{2,1,0:T(8,128)(2,1)S(1)} %copy-done.20), channel_id=1, source_target_pairs={{0,2},{1,3},{2,4},{3,5},{4,6},{5,7},{6,0},{7,1},{8,10},{9,11},{10,... | collective-permute-start | bytes 49160 | tf_op jit(solution)/shard_map/ppermute | solution.py:244
  70.2 5.8 %collective-permute-start.2 = (bf16[4,8,256]{2,1,0:T(8,128)(2,1)S(1)}, bf16[4,8,256]{2,1,0:T(8,128)(2,1)S(1)}, u32[]{:S(2)}, u32[]{:S(2)}) collective-permute-start(bf16[4,8,256]{2,1,0:T(8,128)(2,1)S(1)} %copy-done.19), channel_id=1, source_target_pairs={{0,3},{1,4},{2,5},{3,6},{4,7},{5,0},{6,1},{7,2},{8,11},{9,12},{10,... | collective-permute-start | bytes 49160 | tf_op jit(solution)/shard_map/ppermute | solution.py:244
  76.0 6.5 %collective-permute-start.3 = (bf16[4,8,256]{2,1,0:T(8,128)(2,1)S(1)}, bf16[4,8,256]{2,1,0:T(8,128)(2,1)S(1)}, u32[]{:S(2)}, u32[]{:S(2)}) collective-permute-start(bf16[4,8,256]{2,1,0:T(8,128)(2,1)S(1)} %copy-done.18), channel_id=1, source_target_pairs={{0,4},{1,5},{2,6},{3,7},{4,0},{5,1},{6,2},{7,3},{8,12},{9,13},{10,... | collective-permute-start | bytes 49160 | tf_op jit(solution)/shard_map/ppermute | solution.py:244
  82.5 4.4 %collective-permute-start.4 = (bf16[4,8,256]{2,1,0:T(8,128)(2,1)S(1)}, bf16[4,8,256]{2,1,0:T(8,128)(2,1)S(1)}, u32[]{:S(2)}, u32[]{:S(2)}) collective-permute-start(bf16[4,8,256]{2,1,0:T(8,128)(2,1)S(1)} %copy-done.17), channel_id=1, source_target_pairs={{0,5},{1,6},{2,7},{3,0},{4,1},{5,2},{6,3},{7,4},{8,13},{9,14},{10,... | collective-permute-start | bytes 49160 | tf_op jit(solution)/shard_map/ppermute | solution.py:244
  86.9 3.5 %collective-permute-start.5 = (bf16[4,8,256]{2,1,0:T(8,128)(2,1)S(1)}, bf16[4,8,256]{2,1,0:T(8,128)(2,1)S(1)}, u32[]{:S(2)}, u32[]{:S(2)}) collective-permute-start(bf16[4,8,256]{2,1,0:T(8,128)(2,1)S(1)} %copy-done.16), channel_id=1, source_target_pairs={{0,6},{1,7},{2,0},{3,1},{4,2},{5,3},{6,4},{7,5},{8,14},{9,15},{10,... | collective-permute-start | bytes 49160 | tf_op jit(solution)/shard_map/ppermute | solution.py:244
  90.3 4.1 %collective-permute-start.6 = (bf16[4,8,256]{2,1,0:T(8,128)(2,1)S(1)}, bf16[4,8,256]{2,1,0:T(8,128)(2,1)S(1)}, u32[]{:S(2)}, u32[]{:S(2)}) collective-permute-start(bf16[4,8,256]{2,1,0:T(8,128)(2,1)S(1)} %copy-done.15), channel_id=1, source_target_pairs={{0,7},{1,0},{2,1},{3,2},{4,3},{5,4},{6,5},{7,6},{8,15},{9,8},{10,9... | collective-permute-start | bytes 49160 | tf_op jit(solution)/shard_map/ppermute | solution.py:244
  96.6 4.2 %collective-permute-start.7 = (bf16[8,8,256]{2,1,0:T(8,128)(2,1)}, bf16[8,8,256]{2,1,0:T(8,128)(2,1)S(1)}, u32[]{:S(2)}, u32[]{:S(2)}) collective-permute-start(bf16[8,8,256]{2,1,0:T(8,128)(2,1)} %get-tuple-element.32), channel_id=1, source_target_pairs={{0,8},{8,16},{16,24},{24,0},{1,9},{9,17},{17,25},{25,1},{2,10},{10... | collective-permute-start | bytes 98312 | tf_op jit(solution)/shard_map/ppermute | solution.py:244
  100.8 4.5 %collective-permute-start.8 = (bf16[8,8,256]{2,1,0:T(8,128)(2,1)}, bf16[8,8,256]{2,1,0:T(8,128)(2,1)S(1)}, u32[]{:S(2)}, u32[]{:S(2)}) collective-permute-start(bf16[8,8,256]{2,1,0:T(8,128)(2,1)} %get-tuple-element.33), channel_id=1, source_target_pairs={{0,16},{8,24},{16,0},{24,8},{1,17},{9,25},{17,1},{25,9},{2,18},{10... | collective-permute-start | bytes 98312 | tf_op jit(solution)/shard_map/ppermute | solution.py:244
  105.2 3.3 %collective-permute-start.9 = (bf16[8,8,256]{2,1,0:T(8,128)(2,1)}, bf16[8,8,256]{2,1,0:T(8,128)(2,1)S(1)}, u32[]{:S(2)}, u32[]{:S(2)}) collective-permute-start(bf16[8,8,256]{2,1,0:T(8,128)(2,1)} %get-tuple-element.34), channel_id=1, source_target_pairs={{0,24},{8,0},{16,8},{24,16},{1,25},{9,1},{17,9},{25,17},{2,26},{10... | collective-permute-start | bytes 98312 | tf_op jit(solution)/shard_map/ppermute | solution.py:244
  (16 other events, 341.4 us)

commit v2 on v1

--- a/solution.py
+++ b/solution.py
@@ -79,14 +79,36 @@
     return dot(table_ref[:, :depth], operand) + dot(table_ref[:, depth:], operand)
 
 
-def prologue_kernel(table_ref, act_ref, cot_ref, first_ref, second_ref, bias_ref, *rest):
-    pieces, rows_ref, cots = rest[:Y], rest[Y], rest[Y + 1 : Y + 1 + Z]
-    cot_buf, held, found, sems, cot_sem = rest[Y + 1 + Z :]
-    size = cot_buf.shape[1] // 2
-    y, core, x, z = (lax.axis_index(name) for name in ("y", "core", "x", "z"))
-    odd = x & 1
-    cot_copy = pltpu.make_async_copy(cot_ref.at[:, pl.ds(y * 2 * size, 2 * size)], cot_buf, cot_sem)
-    cot_copy.start()
+def cot_kernel(table_ref, cot_ref, out_ref, table, field, sems):
+    size = out_ref.shape[3]
+    depth = table.shape[2] // 2
+    y, core = lax.axis_index("y"), lax.axis_index("core")
+    copies = [
+        pltpu.make_async_copy(table_ref.at[:, core], table, sems.at[0]),
+        pltpu.make_async_copy(cot_ref.at[:, pl.ds(y * 2 * size, 2 * size)], field, sems.at[1]),
+    ]
+    for copy in copies:
+        copy.start()
+    half = Z * table.shape[1]
+    line = lax.broadcasted_iota(jnp.int32, (half, size), 0)
+    zero_mode = jnp.logical_and(jnp.logical_and(line < 8, (line & 1) == 0), core == 0)
+    factor = jnp.where(zero_mode, 1.0, 2.0).astype(F32)
+    for copy in copies:
+        copy.wait()
+    high = table[:, :, :depth].reshape(half, depth)
+    low = table[:, :, depth:].reshape(half, depth)
+    for k in range(2):
+        part = field[:, k * size : (k + 1) * size]
+        spectrum = ((dot(high, part) + dot(low, part)) * factor).astype(BF16).reshape(Z, 2, 8, size)
+        for m in range(2):
+            out_ref[:, 2 * m + k] = spectrum[:, m]
+
+
+def prologue_kernel(table_ref, act_ref, first_ref, second_ref, bias_ref, *rest):
+    pieces = rest[:Y]
+    rows_ref, held, sems = rest[Y:]
+    size = held.shape[2]
+    y, odd = lax.axis_index("y"), lax.axis_index("x") & 1
     loads = []
     for d in range(Y):
         block = ((y + d) & (Y - 1)) * 2 + odd
@@ -99,49 +121,32 @@
                 )
                 copy.start()
                 loads.append(copy)
-
-    count = table_ref.shape[0]
-    line = lax.broadcasted_iota(jnp.int32, (count, size), 0)
-    factor = jnp.where(jnp.logical_and(line < 8, (line & 1) == 0), 1.0, 2.0).astype(F32)
-    cot_copy.wait()
-    for k in range(2):
-        spectrum = (twice(table_ref, cot_buf[:, k * size : (k + 1) * size]) * factor).astype(BF16)
-        found[k] = spectrum.reshape(Z, 2, 2, 8, size)
-    for d in range(Z):
-        to = (z + d) & (Z - 1)
-        for k in range(X):
-            cots[d][k] = found[k & 1, to, core, k >> 1]
-
-    for d in range(Y):
-        block = ((y + d) & (Y - 1)) * 2 + odd
         bias = bias_ref[0, :, pl.ds(block * size, size)]
         high = bias.astype(BF16).astype(F32)
         middle = (bias - high).astype(BF16).astype(F32)
         low = bias - high - middle
         packed = jnp.concatenate([high, middle, low, jnp.zeros((10, size), F32)], axis=0)
         held[d, 4 * size : 4 * size + 16] = packed.astype(BF16)
-    for copy in loads:
-        copy.wait()
+
     stores = []
-    for d in range(Y):
-        copy = pltpu.make_async_copy(held.at[d], pieces[d], sems.at[d, 4])
-        copy.start()
-        stores.append(copy)
-
     for n in range(2 * Y):
+        if n == 2:
+            for copy in loads:
+                copy.wait()
+            for d in range(Y):
+                copy = pltpu.make_async_copy(held.at[d], pieces[d], sems.at[d, 4])
+                copy.start()
+                stores.append(copy)
         spectrum = twice(table_ref, act_ref[:, n * size : (n + 1) * size]).astype(BF16)
         rows_ref[:, :, :, n % 2, n // 2] = spectrum.reshape(Z, 2, 2, 8, size)
     for copy in stores:
         copy.wait()
 
 
-def turn_kernel(*refs):
-    arrived, outs = refs[:Z], refs[Z:]
+def turn_kernel(arrived_ref, *outs):
     x = lax.axis_index("x")
     for e in range(X):
-        to = (x + e) & (X - 1)
-        for d in range(Z):
-            outs[e][d] = arrived[d][to]
+        outs[e][...] = arrived_ref[:, (x + e) & (X - 1)]
 
 
 def inverse_kernel(table_ref, spec_ref, cot_ref, out_ref, result, sems):
@@ -174,8 +179,7 @@
             copy.start()
             copies.append(copy)
     for e in range(X):
-        for d in range(Z):
-            found[(z - d) & (Z - 1), (x - e) & (X - 1)] = cots[e][d]
+        found[:, (x - e) & (X - 1)] = cots[e][...]
     has_zero = jnp.logical_and(jnp.logical_and(core == 0, x < 2), z == 0)
     fold = jnp.where(has_zero, 1, 0)
 
@@ -244,24 +248,34 @@
         return lax.ppermute(value, axis, [(i, (i + distance) % size) for i in range(size)])
 
     flat_cot = cotangent.reshape(count, channels)
+    cot_rows = pl.pallas_call(
+        cot_kernel,
+        in_specs=[hbm, hbm],
+        out_specs=vmem,
+        out_shape=shaped(Z, X, tile, size),
+        scratch_shapes=[
+            pltpu.VMEM((Z, 2 * tile, 2 * count), BF16),
+            pltpu.VMEM((count, 2 * size), BF16),
+            pltpu.SemaphoreType.DMA((2,)),
+        ],
+        name="cot_rows",
+    )(forward_rows.reshape(Z, 2, 2 * tile, 2 * count), flat_cot)
+    cot_blocks = lax.all_to_all(
+        cot_rows.reshape(Z, X * tile, size), "z", split_axis=0, concat_axis=0, tiled=True
+    ).reshape(cot_rows.shape)
     made = pl.pallas_call(
         prologue_kernel,
-        in_specs=[vmem, vmem, hbm, hbm, hbm, vmem],
-        out_specs=[hbm] * Y + [vmem] * (1 + Z),
-        out_shape=[shaped(4 * size + 16, size)] * Y + [shaped(*blocks)] + [shaped(X, tile, size)] * Z,
+        in_specs=[vmem, vmem, hbm, hbm, vmem],
+        out_specs=[hbm] * Y + [vmem],
+        out_shape=[shaped(4 * size + 16, size)] * Y + [shaped(*blocks)],
         scratch_shapes=[
-            pltpu.VMEM((count, 2 * size), BF16),
             pltpu.VMEM((Y, 4 * size + 16, size), BF16),
-            pltpu.VMEM((2, Z, 2, 2, tile, size), BF16),
             pltpu.SemaphoreType.DMA((Y, 5)),
-            pltpu.SemaphoreType.DMA(()),
         ],
         name="prologue",
-    )(forward_rows, activations.reshape(count, channels), flat_cot, w_first, w_second, b_first)
-    pieces, act_rows, cot_rows = made[:Y], made[Y], made[Y + 1 :]
-
-    arrived = [cot_rows[0]]
-    arrived += [shifted(cot_rows[d], "z", d) for d in range(1, Z)]
+    )(forward_rows, activations.reshape(count, channels), w_first, w_second, b_first)
+    pieces, act_rows = made[:Y], made[Y]
+
     weights = []
     for d in range(Y):
         piece = shifted(pieces[d], "y", d) if d else pieces[0]
@@ -269,11 +283,11 @@
     act_columns = exchange(act_rows)
     turned = pl.pallas_call(
         turn_kernel,
-        in_specs=[vmem] * Z,
+        in_specs=[vmem],
         out_specs=[vmem] * X,
         out_shape=[shaped(Z, tile, size)] * X,
         name="turn",
-    )(*arrived)
+    )(cot_blocks)
     cots = [turned[0]] + [shifted(turned[e], "x", e) for e in range(1, X)]
 
     back = pl.pallas_call(

time: 172 us -> 141 us (0.82)
  waiting for transfers between devices: 59 us -> 40.7 us
  starting transfers between devices: 41.5 us -> 32.9 us
  blocking collectives: 48.3 us -> 43.3 us
    ppermute x17 -> x10, waiting for transfers between devices: 59 us -> 38.4 us  [shifted(): lax.ppermute(value, axis, [(i, (i + distance) % size) for i in range(size)])]
    ppermute x17 -> x10, starting transfers between devices: 25.9 us -> 12.3 us  [shifted(): lax.ppermute(value, axis, [(i, (i + distance) % size) for i in range(size)])]
    all_to_all x0 -> x1, starting transfers between devices: none -> 9.01 us  [body(): lax.all_to_all(cot_rows.reshape(Z, X * tile, size), 'z', split_axis=0, co...]
    all_to_all x1, blocking collectives: 48.3 us -> 43.3 us  [exchange(): lax.all_to_all(flat, EVERYONE, split_axis=0, concat_axis=0, tiled=True)]
    all_to_all x1, starting transfers between devices: 15.7 us -> 11.6 us  [exchange(): lax.all_to_all(flat, EVERYONE, split_axis=0, concat_axis=0, tiled=True)]
    all_to_all x0 -> x1, waiting for transfers between devices: none -> 2.33 us  [body(): lax.all_to_all(cot_rows.reshape(Z, X * tile, size), 'z', split_axis=0, co...]
    pallas_call x2 -> x3, Pallas kernels: 7.28 us -> 9.02 us  [the longest x1 5.41 us: body(): pl.pallas_call(prologue_kernel, in_specs=[vmem, vmem, hbm, hbm, vmem], ou...]
  transfers between devices with their start and end apart: 18 -> 12, of which waited for: 12 -> 6; matrix products, arithmetic and copies ran while one was open for 0% -> 0% of each run, Pallas kernels for 1% -> 5%
where the time goes in v2:
time: 141 us
  blocking collectives  43.3 us (31%)
  waiting for transfers between devices  40.7 us (29%)
  starting transfers between devices  32.9 us (23%)
  Pallas kernels  22.5 us (16%)
    all_to_all x1, blocking collectives, exchange(): lax.all_to_all(flat, EVERYONE, split_axis=0, concat_axis=0, tiled=True)  43.3 us
    ppermute x10, waiting for transfers between devices, shifted(): lax.ppermute(value, axis, [(i, (i + distance) % size) for i in range(size)])  38.4 us
    ppermute x10, starting transfers between devices, shifted(): lax.ppermute(value, axis, [(i, (i + distance) % size) for i in range(size)])  12.3 us
    all_to_all x1, starting transfers between devices, exchange(): lax.all_to_all(flat, EVERYONE, split_axis=0, concat_axis=0, tiled=True)  11.6 us
    pallas_call x1, Pallas kernels, body(): pl.pallas_call(chain_kernel, in_specs=[vmem] * (4 + X) + [hbm] * sections...  10.4 us
    all_to_all x1, starting transfers between devices, body(): lax.all_to_all(cot_rows.reshape(Z, X * tile, size), 'z', split_axis=0, co...  9.01 us
    pallas_call x1, Pallas kernels, body(): pl.pallas_call(prologue_kernel, in_specs=[vmem, vmem, hbm, hbm, vmem], ou...  5.41 us
    pallas_call x1, Pallas kernels, body(): pl.pallas_call(inverse_kernel, in_specs=[vmem] * 3, out_specs=hbm, out_sh...  3.15 us
  transfers between devices with their start and end apart: 12, of which 6 were waited for; matrix products, arithmetic and copies ran while one was open for 0% of the time, Pallas kernels for 5%

profile of v2, /device:TPU:1, one launch (start us, length us, event | category | flops | bytes accessed | tf_op | source)
XLA Modules:
  0.0 140.6 jit_solution(17698660294660756544)
XLA Ops:
  0.0 1.9 %cot_rows.1 = bf16[8,4,8,256]{3,2,1,0:T(8,128)(2,1)} custom-call(bf16[8,2,16,512]{3,2,1,0:T(8,128)(2,1)} %constant.12.clone.table_ref, bf16[256,2048]{1,0:T(8,128)(2,1)} %bitcast.11), custom_call_target="tpu_custom_call" | custom-call | tf_op jit(solution)/shard_map/cot_rows/pallas_call | solution.py:251
  1.9 9.0 %all-to-all-start.1 = ((bf16[8,32,256]{2,1,0:T(8,128)(2,1)}), bf16[8,32,256]{2,1,0:T(8,128)(2,1)S(1)}, u32[]{:S(2)}, u32[]{:S(2)}) async-start(bf16[8,32,256]{2,1,0:T(8,128)(2,1)} %bitcast.17), calls=%async_computation.1 | async-start | bytes 262144 | tf_op jit(solution)/shard_map/all_to_all | solution.py:263
  10.9 5.4 %prologue.1 = (bf16[1040,256]{1,0:T(8,128)(2,1)}, bf16[1040,256]{1,0:T(8,128)(2,1)}, bf16[1040,256]{1,0:T(8,128)(2,1)}, bf16[1040,256]{1,0:T(8,128)(2,1)}, bf16[8,2,2,2,4,8,256]{6,5,4,3,2,1,0:T(8,128)(2,1)}) custom-call(bf16[256,512]{1,0:T(8,128)(2,1)} %constant.13.clone.table_ref, bf16[256,2048]{1,0:T(8,128)(2,1)} %bitcast.15, ...), custom_call_target="tpu_custom_call" | custom-call | tf_op jit(solution)/shard_map/prologue/pallas_call | solution.py:266
  16.4 2.3 %all-to-all-done.1 = bf16[8,32,256]{2,1,0:T(8,128)(2,1)S(1)} async-done(((bf16[8,32,256]{2,1,0:T(8,128)(2,1)}), bf16[8,32,256]{2,1,0:T(8,128)(2,1)S(1)}, u32[]{:S(2)}, u32[]{:S(2)}) %all-to-all-start.1) | async-done | bytes 131104 | tf_op jit(solution)/shard_map/all_to_all | solution.py:263
  18.7 11.6 %all-to-all-start = ((bf16[256,8,256]{2,1,0:T(8,128)(2,1)}), bf16[256,8,256]{2,1,0:T(8,128)(2,1)S(1)}, u32[]{:S(2)}, u32[]{:S(2)}) async-start(bf16[256,8,256]{2,1,0:T(8,128)(2,1)} %bitcast.14), calls=%async_computation | async-start | bytes 2097152 | tf_op jit(solution)/shard_map/all_to_all | solution.py:244
  30.3 1.4 %collective-permute-start.4 = (bf16[1040,256]{1,0:T(8,128)(2,1)}, bf16[1040,256]{1,0:T(8,128)(2,1)S(1)}, u32[]{:S(2)}, u32[]{:S(2)}) collective-permute-start(bf16[1040,256]{1,0:T(8,128)(2,1)} %get-tuple-element.20), channel_id=1, source_target_pairs={{0,64},{64,128},{128,192},{192,0},{1,65},{65,129},{129,193},{193,1... | collective-permute-start | bytes 1597448 | tf_op jit(solution)/shard_map/ppermute | solution.py:248
  31.7 2.5 %collective-permute-start.6 = (bf16[1040,256]{1,0:T(8,128)(2,1)}, bf16[1040,256]{1,0:T(8,128)(2,1)S(1)}, u32[]{:S(2)}, u32[]{:S(2)}) collective-permute-start(bf16[1040,256]{1,0:T(8,128)(2,1)} %get-tuple-element.21), channel_id=1, source_target_pairs={{0,128},{64,192},{128,0},{192,64},{1,129},{65,193},{129,1},{193,65... | collective-permute-start | bytes 1597448 | tf_op jit(solution)/shard_map/ppermute | solution.py:248
  34.1 1.1 collective-permute-start.8
  35.3 1.2 collective-permute-start.3
  36.5 15.3 %collective-permute-done.4.rest_6_ = bf16[1040,256]{1,0:T(8,128)(2,1)S(1)} collective-permute-done((bf16[1040,256]{1,0:T(8,128)(2,1)}, bf16[1040,256]{1,0:T(8,128)(2,1)S(1)}, u32[]{:S(2)}, u32[]{:S(2)}) %collective-permute-start.4) | collective-permute-done | bytes 532512 | tf_op jit(solution)/shard_map/ppermute | solution.py:248
  51.8 3.1 %collective-permute-start.5 = (bf16[1040,256]{1,0:T(8,128)(2,1)S(1)}, bf16[1040,256]{1,0:T(8,128)(2,1)}, u32[]{:S(2)}, u32[]{:S(2)}) collective-permute-start(bf16[1040,256]{1,0:T(8,128)(2,1)S(1)} %collective-permute-done.4.rest_6_), channel_id=1, source_target_pairs={{0,32},{32,0},{1,33},{33,1},{2,34},{34,2},{3,35},{35,3},{4,36},{36... | collective-permute-start | bytes 1597448 | tf_op jit(solution)/shard_map/ppermute | solution.py:248
  54.9 13.4 %collective-permute-done.6.rest_8_ = bf16[1040,256]{1,0:T(8,128)(2,1)S(1)} collective-permute-done((bf16[1040,256]{1,0:T(8,128)(2,1)}, bf16[1040,256]{1,0:T(8,128)(2,1)S(1)}, u32[]{:S(2)}, u32[]{:S(2)}) %collective-permute-start.6) | collective-permute-done | bytes 532512 | tf_op jit(solution)/shard_map/ppermute | solution.py:248
  68.3 0.9 collective-permute-start.7
  69.3 1.7 %turn.1 = (bf16[8,8,256]{2,1,0:T(8,128)(2,1)}, bf16[8,8,256]{2,1,0:T(8,128)(2,1)}, bf16[8,8,256]{2,1,0:T(8,128)(2,1)}, bf16[8,8,256]{2,1,0:T(8,128)(2,1)}) custom-call(bf16[8,4,8,256]{3,2,1,0:T(8,128)(2,1)} %bitcast.16), custom_call_target="tpu_custom_call" | custom-call | tf_op jit(solution)/shard_map/turn/pallas_call | solution.py:284
  71.0 0.6 collective-permute-start
  71.6 3.6 %collective-permute-done.rest_1_ = bf16[8,8,256]{2,1,0:T(8,128)(2,1)S(1)} collective-permute-done((bf16[8,8,256]{2,1,0:T(8,128)(2,1)}, bf16[8,8,256]{2,1,0:T(8,128)(2,1)S(1)}, u32[]{:S(2)}, u32[]{:S(2)}) %collective-permute-start) | collective-permute-done | bytes 32800 | tf_op jit(solution)/shard_map/ppermute | solution.py:248
  75.2 0.8 collective-permute-start.1
  76.0 3.7 %collective-permute-done.1.rest_2_ = bf16[8,8,256]{2,1,0:T(8,128)(2,1)S(1)} collective-permute-done((bf16[8,8,256]{2,1,0:T(8,128)(2,1)}, bf16[8,8,256]{2,1,0:T(8,128)(2,1)S(1)}, u32[]{:S(2)}, u32[]{:S(2)}) %collective-permute-start.1) | collective-permute-done | bytes 32800 | tf_op jit(solution)/shard_map/ppermute | solution.py:248
  79.7 0.5 collective-permute-start.2
  80.2 2.4 %collective-permute-done.2.rest_3_ = bf16[8,8,256]{2,1,0:T(8,128)(2,1)S(1)} collective-permute-done((bf16[8,8,256]{2,1,0:T(8,128)(2,1)}, bf16[8,8,256]{2,1,0:T(8,128)(2,1)S(1)}, u32[]{:S(2)}, u32[]{:S(2)}) %collective-permute-start.2) | collective-permute-done | bytes 32800 | tf_op jit(solution)/shard_map/ppermute | solution.py:248
  82.8 0.5 copy-done.8
  83.7 10.4 %chain.1 = bf16[8,2,2,2,4,8,256]{6,5,4,3,2,1,0:T(8,128)(2,1)} custom-call(bf16[8,2,2,2,4,8,256]{6,5,4,3,2,1,0:T(8,128)(2,1)} %bitcast.9, bf16[256,512]{1,0:T(8,128)(2,1)} %constant.14.clone.col_ref, bf16[256,512]{1,0:T(8,128)(2,1)} %constant.15.clone.inv_ref, bf16[2,256,256]{2,1,0:T(8,128)(2,1)} %constant.16.clone.fold_ref, ...), custom_call_target="tpu_custom_call" | custom-call | tf_op jit(solution)/shard_map/chain/pallas_call | solution.py:293
  94.0 43.3 %all_to_all.15 = bf16[256,8,256]{2,1,0:T(8,128)(2,1)} all-to-all(bf16[256,8,256]{2,1,0:T(8,128)(2,1)} %bitcast.10), channel_id=1, replica_groups=mesh['y'=4,'core'=2,'x'=4,'z'=8] {'z','core','x','y'}, dimensions={0} | all-to-all | bytes 2097152 | tf_op jit(solution)/shard_map/all_to_all | solution.py:244
  137.3 3.1 %inverse_rows.1 = bf16[256,2048]{1,0:T(8,128)(2,1)} custom-call(bf16[256,512]{1,0:T(8,128)(2,1)} %constant.17.clone.table_ref, bf16[8,2,2,2,4,8,256]{6,5,4,3,2,1,0:T(8,128)(2,1)} %bitcast.13, bf16[256,2048]{1,0:T(8,128)(2,1)} %bitcast.12), custom_call_target="tpu_custom_call" | custom-call | tf_op jit(solution)/shard_map/inverse_rows/pallas_call | solution.py:305
  (24 shorter events, 0.5 us)
Async XLA Ops:
  1.9 16.8 %all-to-all-start.1 = ((bf16[8,32,256]{2,1,0:T(8,128)(2,1)}), bf16[8,32,256]{2,1,0:T(8,128)(2,1)S(1)}, u32[]{:S(2)}, u32[]{:S(2)}) async-start(bf16[8,32,256]{2,1,0:T(8,128)(2,1)} %bitcast.17), calls=%async_computation.1 | async-start | bytes 262144 | tf_op jit(solution)/shard_map/all_to_all | solution.py:263
  16.4 18.9 %copy-start.1 = (bf16[1040,256]{1,0:T(8,128)(2,1)S(1)}, bf16[1040,256]{1,0:T(8,128)(2,1)}, u32[]{:S(2)}) copy-start(bf16[1040,256]{1,0:T(8,128)(2,1)} %get-tuple-element.19.rest_4_) | copy-start | bytes 1597444
  18.7 50.6 %copy-start.5 = (bf16[8,32,256]{2,1,0:T(8,128)(2,1)}, bf16[8,32,256]{2,1,0:T(8,128)(2,1)S(1)}, u32[]{:S(2)}) copy-start(bf16[8,32,256]{2,1,0:T(8,128)(2,1)S(1)} %all-to-all-done.1) | copy-start | bytes 393220
  18.7 64.0 %all-to-all-start = ((bf16[256,8,256]{2,1,0:T(8,128)(2,1)}), bf16[256,8,256]{2,1,0:T(8,128)(2,1)S(1)}, u32[]{:S(2)}, u32[]{:S(2)}) async-start(bf16[256,8,256]{2,1,0:T(8,128)(2,1)} %bitcast.14), calls=%async_computation | async-start | bytes 2097152 | tf_op jit(solution)/shard_map/all_to_all | solution.py:244
  30.3 21.5 %collective-permute-start.4 = (bf16[1040,256]{1,0:T(8,128)(2,1)}, bf16[1040,256]{1,0:T(8,128)(2,1)S(1)}, u32[]{:S(2)}, u32[]{:S(2)}) collective-permute-start(bf16[1040,256]{1,0:T(8,128)(2,1)} %get-tuple-element.20), channel_id=1, source_target_pairs={{0,64},{64,128},{128,192},{192,0},{1,65},{65,129},{129,193},{193,1... | collective-permute-start | bytes 1597448 | tf_op jit(solution)/shard_map/ppermute | solution.py:248
  31.7 36.6 %collective-permute-start.6 = (bf16[1040,256]{1,0:T(8,128)(2,1)}, bf16[1040,256]{1,0:T(8,128)(2,1)S(1)}, u32[]{:S(2)}, u32[]{:S(2)}) collective-permute-start(bf16[1040,256]{1,0:T(8,128)(2,1)} %get-tuple-element.21), channel_id=1, source_target_pairs={{0,128},{64,192},{128,0},{192,64},{1,129},{65,193},{129,1},{193,65... | collective-permute-start | bytes 1597448 | tf_op jit(solution)/shard_map/ppermute | solution.py:248
  34.1 35.1 %collective-permute-start.8 = (bf16[1040,256]{1,0:T(8,128)(2,1)}, bf16[1040,256]{1,0:T(8,128)(2,1)S(1)}, u32[]{:S(2)}, u32[]{:S(2)}) collective-permute-start(bf16[1040,256]{1,0:T(8,128)(2,1)} %get-tuple-element.22), channel_id=1, source_target_pairs={{0,192},{64,0},{128,64},{192,128},{1,193},{65,1},{129,65},{193,129... | collective-permute-start | bytes 1597448 | tf_op jit(solution)/shard_map/ppermute | solution.py:248
  35.3 47.4 %collective-permute-start.3 = (bf16[1040,256]{1,0:T(8,128)(2,1)S(1)}, bf16[1040,256]{1,0:T(8,128)(2,1)}, u32[]{:S(2)}, u32[]{:S(2)}) collective-permute-start(bf16[1040,256]{1,0:T(8,128)(2,1)S(1)} %copy-done.1), channel_id=1, source_target_pairs={{0,32},{32,0},{1,33},{33,1},{2,34},{34,2},{3,35},{35,3},{4,36},{36... | collective-permute-start | bytes 1597448 | tf_op jit(solution)/shard_map/ppermute | solution.py:248
  51.8 30.9 %copy-start.2 = (bf16[1040,256]{1,0:T(8,128)(2,1)}, bf16[1040,256]{1,0:T(8,128)(2,1)S(1)}, u32[]{:S(2)}) copy-start(bf16[1040,256]{1,0:T(8,128)(2,1)S(1)} %collective-permute-done.4.rest_6_) | copy-start | bytes 1597444
  51.8 30.8 %collective-permute-start.5 = (bf16[1040,256]{1,0:T(8,128)(2,1)S(1)}, bf16[1040,256]{1,0:T(8,128)(2,1)}, u32[]{:S(2)}, u32[]{:S(2)}) collective-permute-start(bf16[1040,256]{1,0:T(8,128)(2,1)S(1)} %collective-permute-done.4.rest_6_), channel_id=1, source_target_pairs={{0,32},{32,0},{1,33},{33,1},{2,34},{34,2},{3,35},{35,3},{4,36},{36... | collective-permute-start | bytes 1597448 | tf_op jit(solution)/shard_map/ppermute | solution.py:248
  68.3 14.4 %copy-start.3 = (bf16[1040,256]{1,0:T(8,128)(2,1)}, bf16[1040,256]{1,0:T(8,128)(2,1)S(1)}, u32[]{:S(2)}) copy-start(bf16[1040,256]{1,0:T(8,128)(2,1)S(1)} %collective-permute-done.6.rest_8_) | copy-start | bytes 1597444
  68.3 14.4 %collective-permute-start.7 = (bf16[1040,256]{1,0:T(8,128)(2,1)S(1)}, bf16[1040,256]{1,0:T(8,128)(2,1)}, u32[]{:S(2)}, u32[]{:S(2)}) collective-permute-start(bf16[1040,256]{1,0:T(8,128)(2,1)S(1)} %collective-permute-done.6.rest_8_), channel_id=1, source_target_pairs={{0,32},{32,0},{1,33},{33,1},{2,34},{34,2},{3,35},{35,3},{4,36},{36... | collective-permute-start | bytes 1597448 | tf_op jit(solution)/shard_map/ppermute | solution.py:248
  69.2 13.5 %copy-start.4 = (bf16[1040,256]{1,0:T(8,128)(2,1)}, bf16[1040,256]{1,0:T(8,128)(2,1)S(1)}, u32[]{:S(2)}) copy-start(bf16[1040,256]{1,0:T(8,128)(2,1)S(1)} %collective-permute-done.8.rest_10_) | copy-start | bytes 1597444
  69.2 13.5 %collective-permute-start.9 = (bf16[1040,256]{1,0:T(8,128)(2,1)S(1)}, bf16[1040,256]{1,0:T(8,128)(2,1)}, u32[]{:S(2)}, u32[]{:S(2)}) collective-permute-start(bf16[1040,256]{1,0:T(8,128)(2,1)S(1)} %collective-permute-done.8.rest_10_), channel_id=1, source_target_pairs={{0,32},{32,0},{1,33},{33,1},{2,34},{34,2},{3,35},{35,3},{4,36},{36... | collective-permute-start | bytes 1597448 | tf_op jit(solution)/shard_map/ppermute | solution.py:248
  71.0 4.2 %collective-permute-start = (bf16[8,8,256]{2,1,0:T(8,128)(2,1)}, bf16[8,8,256]{2,1,0:T(8,128)(2,1)S(1)}, u32[]{:S(2)}, u32[]{:S(2)}) collective-permute-start(bf16[8,8,256]{2,1,0:T(8,128)(2,1)} %get-tuple-element.16), channel_id=1, source_target_pairs={{0,8},{8,16},{16,24},{24,0},{1,9},{9,17},{17,25},{25,1},{2,10},{10... | collective-permute-start | bytes 98312 | tf_op jit(solution)/shard_map/ppermute | solution.py:248
  75.2 7.5 %copy-start.6 = (bf16[8,8,256]{2,1,0:T(8,128)(2,1)}, bf16[8,8,256]{2,1,0:T(8,128)(2,1)S(1)}, u32[]{:S(2)}) copy-start(bf16[8,8,256]{2,1,0:T(8,128)(2,1)S(1)} %collective-permute-done.rest_1_) | copy-start | bytes 98308
  75.2 4.5 %collective-permute-start.1 = (bf16[8,8,256]{2,1,0:T(8,128)(2,1)}, bf16[8,8,256]{2,1,0:T(8,128)(2,1)S(1)}, u32[]{:S(2)}, u32[]{:S(2)}) collective-permute-start(bf16[8,8,256]{2,1,0:T(8,128)(2,1)} %get-tuple-element.17), channel_id=1, source_target_pairs={{0,16},{8,24},{16,0},{24,8},{1,17},{9,25},{17,1},{25,9},{2,18},{10... | collective-permute-start | bytes 98312 | tf_op jit(solution)/shard_map/ppermute | solution.py:248
  79.7 3.1 %copy-start.7 = (bf16[8,8,256]{2,1,0:T(8,128)(2,1)}, bf16[8,8,256]{2,1,0:T(8,128)(2,1)S(1)}, u32[]{:S(2)}) copy-start(bf16[8,8,256]{2,1,0:T(8,128)(2,1)S(1)} %collective-permute-done.1.rest_2_) | copy-start | bytes 98308
  79.7 3.0 %collective-permute-start.2 = (bf16[8,8,256]{2,1,0:T(8,128)(2,1)}, bf16[8,8,256]{2,1,0:T(8,128)(2,1)S(1)}, u32[]{:S(2)}, u32[]{:S(2)}) collective-permute-start(bf16[8,8,256]{2,1,0:T(8,128)(2,1)} %get-tuple-element.18), channel_id=1, source_target_pairs={{0,24},{8,0},{16,8},{24,16},{1,25},{9,1},{17,9},{25,17},{2,26},{10... | collective-permute-start | bytes 98312 | tf_op jit(solution)/shard_map/ppermute | solution.py:248
  82.6 0.6 copy-start.8
  82.7 1.0 copy-start

commit v3 on v2

--- a/solution.py
+++ b/solution.py
@@ -13,6 +13,7 @@
 BF16 = jnp.bfloat16
 F32 = jnp.float32
 X, Y, Z = 4, 4, 8
+SMALL = pltpu.CompilerParams(vmem_limit_bytes=20 << 20)
 EVERYONE = ("z", "core", "x", "y")
 
 
@@ -79,16 +80,37 @@
     return dot(table_ref[:, :depth], operand) + dot(table_ref[:, depth:], operand)
 
 
-def cot_kernel(table_ref, cot_ref, out_ref, table, field, sems):
+def first_kernel(table_ref, cot_ref, first_ref, second_ref, bias_ref, *rest):
+    pieces = rest[:Y]
+    out_ref, table, field, sems, cot_sems = rest[Y:]
     size = out_ref.shape[3]
     depth = table.shape[2] // 2
-    y, core = lax.axis_index("y"), lax.axis_index("core")
+    y, core, odd = lax.axis_index("y"), lax.axis_index("core"), lax.axis_index("x") & 1
     copies = [
-        pltpu.make_async_copy(table_ref.at[:, core], table, sems.at[0]),
-        pltpu.make_async_copy(cot_ref.at[:, pl.ds(y * 2 * size, 2 * size)], field, sems.at[1]),
+        pltpu.make_async_copy(table_ref.at[:, core], table, cot_sems.at[0]),
+        pltpu.make_async_copy(cot_ref.at[:, pl.ds(y * 2 * size, 2 * size)], field, cot_sems.at[1]),
     ]
     for copy in copies:
         copy.start()
+    loads = []
+    for d in range(Y):
+        block = ((y + d) & (Y - 1)) * 2 + odd
+        for i in range(2):
+            for j, ref in enumerate((first_ref, second_ref)):
+                copy = pltpu.make_async_copy(
+                    ref.at[0, i, block],
+                    pieces[d].at[pl.ds((2 * j + i) * size, size)],
+                    sems.at[d, 2 * j + i],
+                )
+                copy.start()
+                loads.append(copy)
+        bias = bias_ref[0, :, pl.ds(block * size, size)]
+        high = bias.astype(BF16).astype(F32)
+        middle = (bias - high).astype(BF16).astype(F32)
+        low = bias - high - middle
+        packed = jnp.concatenate([high, middle, low, jnp.zeros((10, size), F32)], axis=0)
+        pieces[d][4 * size : 4 * size + 16] = packed.astype(BF16)
+
     half = Z * table.shape[1]
     line = lax.broadcasted_iota(jnp.int32, (half, size), 0)
     zero_mode = jnp.logical_and(jnp.logical_and(line < 8, (line & 1) == 0), core == 0)
@@ -102,45 +124,15 @@
         spectrum = ((dot(high, part) + dot(low, part)) * factor).astype(BF16).reshape(Z, 2, 8, size)
         for m in range(2):
             out_ref[:, 2 * m + k] = spectrum[:, m]
-
-
-def prologue_kernel(table_ref, act_ref, first_ref, second_ref, bias_ref, *rest):
-    pieces = rest[:Y]
-    rows_ref, held, sems = rest[Y:]
-    size = held.shape[2]
-    y, odd = lax.axis_index("y"), lax.axis_index("x") & 1
-    loads = []
-    for d in range(Y):
-        block = ((y + d) & (Y - 1)) * 2 + odd
-        for i in range(2):
-            for j, ref in enumerate((first_ref, second_ref)):
-                copy = pltpu.make_async_copy(
-                    ref.at[0, i, block],
-                    held.at[d, pl.ds((2 * j + i) * size, size)],
-                    sems.at[d, 2 * j + i],
-                )
-                copy.start()
-                loads.append(copy)
-        bias = bias_ref[0, :, pl.ds(block * size, size)]
-        high = bias.astype(BF16).astype(F32)
-        middle = (bias - high).astype(BF16).astype(F32)
-        low = bias - high - middle
-        packed = jnp.concatenate([high, middle, low, jnp.zeros((10, size), F32)], axis=0)
-        held[d, 4 * size : 4 * size + 16] = packed.astype(BF16)
-
-    stores = []
+    for copy in loads:
+        copy.wait()
+
+
+def row_kernel(table_ref, act_ref, rows_ref):
+    size = rows_ref.shape[6]
     for n in range(2 * Y):
-        if n == 2:
-            for copy in loads:
-                copy.wait()
-            for d in range(Y):
-                copy = pltpu.make_async_copy(held.at[d], pieces[d], sems.at[d, 4])
-                copy.start()
-                stores.append(copy)
         spectrum = twice(table_ref, act_ref[:, n * size : (n + 1) * size]).astype(BF16)
         rows_ref[:, :, :, n % 2, n // 2] = spectrum.reshape(Z, 2, 2, 8, size)
-    for copy in stores:
-        copy.wait()
 
 
 def turn_kernel(arrived_ref, *outs):
@@ -167,17 +159,21 @@
 def chain_kernel(act_ref, col_ref, inv_ref, fold_ref, *rest):
     sections = 2 * Y
     cots, weights = rest[:X], rest[X : X + sections]
-    out_ref, held, found, sems = rest[X + sections :]
+    out_ref, found, held, sems = rest[X + sections :]
     size = act_ref.shape[6]
     half = col_ref.shape[0] // 2
     y, core, x, z = (lax.axis_index(name) for name in ("y", "core", "x", "z"))
-    copies = []
-    for d in range(Y):
-        for i in range(2):
-            slot = ((y - d) & (Y - 1)) * 2 + (core if i == 0 else 1 - core)
-            copy = pltpu.make_async_copy(weights[2 * d + i], held.at[slot], sems.at[2 * d + i])
-            copy.start()
-            copies.append(copy)
+
+    def load(p, source):
+        return pltpu.make_async_copy(weights[source], held.at[p], sems.at[p])
+
+    for here in range(sections):
+
+        @pl.when(y * 2 + core == here)
+        def _():
+            for p in range(sections - 1, -1, -1):
+                load(p, 2 * ((here // 2 - p // 2) % Y) + (p % 2 != here % 2)).start()
+
     for e in range(X):
         found[:, (x - e) & (X - 1)] = cots[e][...]
     has_zero = jnp.logical_and(jnp.logical_and(core == 0, x < 2), z == 0)
@@ -191,10 +187,9 @@
     for p in range(sections):
         columns = act_ref[:, p % 2, :, :, p // 2].reshape(2 * half, size)
         spectra.append(twice(col_ref, columns).astype(BF16))
-    for copy in copies:
-        copy.wait()
 
     for p in range(sections - 1, -1, -1):
+        load(p, 0).wait()
         a_re, a_im = held[p, 0:size], held[p, size : 2 * size]
         b_re, b_im = held[p, 2 * size : 3 * size], held[p, 3 * size : 4 * size]
         bias = held[p, 4 * size : 4 * size + 16].astype(F32)
@@ -237,7 +232,13 @@
     blocks = (Z, 2, 2, 2, Y, tile, size)
 
     def shaped(*dims):
-        return jax.ShapeDtypeStruct(dims, BF16)
+        return pltpu.VMEM(dims, BF16)
+
+    def near(*values):
+        return [pltpu.with_memory_space_constraint(value, pltpu.VMEM) for value in values]
+
+    def far(*values):
+        return [pltpu.with_memory_space_constraint(value, pltpu.HBM) for value in values]
 
     def exchange(value):
         flat = value.reshape(sections * columns, tile, size)
@@ -248,33 +249,32 @@
         return lax.ppermute(value, axis, [(i, (i + distance) % size) for i in range(size)])
 
     flat_cot = cotangent.reshape(count, channels)
-    cot_rows = pl.pallas_call(
-        cot_kernel,
-        in_specs=[hbm, hbm],
-        out_specs=vmem,
-        out_shape=shaped(Z, X, tile, size),
+    made = pl.pallas_call(
+        first_kernel,
+        in_specs=[hbm] * 4 + [vmem],
+        out_specs=[vmem] * (Y + 1),
+        out_shape=[shaped(4 * size + 16, size)] * Y + [shaped(Z, X, tile, size)],
         scratch_shapes=[
             pltpu.VMEM((Z, 2 * tile, 2 * count), BF16),
             pltpu.VMEM((count, 2 * size), BF16),
+            pltpu.SemaphoreType.DMA((Y, 4)),
             pltpu.SemaphoreType.DMA((2,)),
         ],
-        name="cot_rows",
-    )(forward_rows.reshape(Z, 2, 2 * tile, 2 * count), flat_cot)
+        compiler_params=SMALL,
+        name="first",
+    )(*far(jnp.asarray(forward_rows.reshape(Z, 2, 2 * tile, -1)), flat_cot, w_first, w_second), b_first)
+    pieces, cot_rows = made[:Y], made[Y]
     cot_blocks = lax.all_to_all(
         cot_rows.reshape(Z, X * tile, size), "z", split_axis=0, concat_axis=0, tiled=True
     ).reshape(cot_rows.shape)
-    made = pl.pallas_call(
-        prologue_kernel,
-        in_specs=[vmem, vmem, hbm, hbm, vmem],
-        out_specs=[hbm] * Y + [vmem],
-        out_shape=[shaped(4 * size + 16, size)] * Y + [shaped(*blocks)],
-        scratch_shapes=[
-            pltpu.VMEM((Y, 4 * size + 16, size), BF16),
-            pltpu.SemaphoreType.DMA((Y, 5)),
-        ],
-        name="prologue",
-    )(forward_rows, activations.reshape(count, channels), w_first, w_second, b_first)
-    pieces, act_rows = made[:Y], made[Y]
+    act_rows = pl.pallas_call(
+        row_kernel,
+        in_specs=[vmem] * 2,
+        out_specs=vmem,
+        out_shape=shaped(*blocks),
+        compiler_params=SMALL,
+        name="act_rows",
+    )(*near(jnp.asarray(forward_rows), activations.reshape(count, channels)))
 
     weights = []
     for d in range(Y):
@@ -286,30 +286,34 @@
         in_specs=[vmem],
         out_specs=[vmem] * X,
         out_shape=[shaped(Z, tile, size)] * X,
+        compiler_params=SMALL,
         name="turn",
-    )(cot_blocks)
+    )(*near(cot_blocks))
     cots = [turned[0]] + [shifted(turned[e], "x", e) for e in range(1, X)]
 
+    tables = [jnp.asarray(table) for table in (forward_columns, inverse_columns, folds)]
     back = pl.pallas_call(
         chain_kernel,
         in_specs=[vmem] * (4 + X) + [hbm] * sections,
         out_specs=vmem,
         out_shape=shaped(*blocks),
         scratch_shapes=[
+            pltpu.VMEM((Z, X, tile, size), BF16),
             pltpu.VMEM((sections, 4 * size + 16, size), BF16),
-            pltpu.VMEM((Z, X, tile, size), BF16),
             pltpu.SemaphoreType.DMA((sections,)),
         ],
+        compiler_params=SMALL,
         name="chain",
-    )(act_columns, forward_columns, inverse_columns, folds, *cots, *weights)
+    )(*near(act_columns, *tables, *cots), *far(*weights))
     grads = pl.pallas_call(
         inverse_kernel,
         in_specs=[vmem] * 3,
         out_specs=hbm,
-        out_shape=shaped(count, channels),
+        out_shape=jax.ShapeDtypeStruct((count, channels), BF16),
         scratch_shapes=[pltpu.VMEM((count, channels), BF16), pltpu.SemaphoreType.DMA((sections,))],
+        compiler_params=SMALL,
         name="inverse_rows",
-    )(inverse_rows, exchange(back), flat_cot)
+    )(*near(jnp.asarray(inverse_rows), exchange(back), flat_cot))
     return grads.reshape(1, rows, width, channels)
 
 

time: 141 us -> 138 us (0.979)
  Pallas kernels: 22.5 us -> 14.6 us
  local copies, waits for them, and re-layouts: 0.94 us -> 4.08 us
  waiting for transfers between devices: 40.7 us -> 43.8 us
  starting transfers between devices: 32.9 us -> 31.2 us
    all_to_all x1, waiting for transfers between devices: 2.33 us -> 6.02 us  [body(): lax.all_to_all(cot_rows.reshape(Z, X * tile, size), 'z', split_axis=0, co...]
    unnamed x18 -> x34, local copies, waits for them, and re-layouts: 0.94 us -> 4.08 us
    pallas_call x2, Pallas kernels: 7.34 us -> 4.56 us  [the longest x1 2.88 us: body(): pl.pallas_call(first_kernel, in_specs=[hbm] * 4 + [vmem], out_specs=[vmem...]
    pallas_call x1, Pallas kernels: 10.4 us -> 8.44 us  [body(): pl.pallas_call(chain_kernel, in_specs=[vmem] * (4 + X) + [hbm] * sections...]
    all_to_all x1, starting transfers between devices: 11.6 us -> 9.83 us  [exchange(): lax.all_to_all(flat, EVERYONE, split_axis=0, concat_axis=0, tiled=True)]
    pallas_call x1, Pallas kernels: 1.69 us -> 0.02 us  [body(): pl.pallas_call(turn_kernel, in_specs=[vmem], out_specs=[vmem] * X, out_sh...]
    pallas_call x1, Pallas kernels: 3.15 us -> 1.54 us  [body(): pl.pallas_call(inverse_kernel, in_specs=[vmem] * 3, out_specs=hbm, out_sh...]
  transfers between devices with their start and end apart: 12 -> 12, of which waited for: 6 -> 6; matrix products, arithmetic and copies ran while one was open for 0% -> 0% of each run, Pallas kernels for 5% -> 1%
where the time goes in v3:
time: 138 us; the launch traced here: 137 us
  waiting for transfers between devices  43.8 us (32%)
  blocking collectives  42.9 us (31%)
  starting transfers between devices  31.2 us (23%)
  Pallas kernels  14.6 us (11%)
  local copies, waits for them, and re-layouts  4.08 us (3%)
    all_to_all x1, blocking collectives, exchange(): lax.all_to_all(flat, EVERYONE, split_axis=0, concat_axis=0, tiled=True)  42.9 us
    ppermute x10, waiting for transfers between devices, shifted(): lax.ppermute(value, axis, [(i, (i + distance) % size) for i in range(size)])  37.8 us
    ppermute x10, starting transfers between devices, shifted(): lax.ppermute(value, axis, [(i, (i + distance) % size) for i in range(size)])  12.4 us
    all_to_all x1, starting transfers between devices, exchange(): lax.all_to_all(flat, EVERYONE, split_axis=0, concat_axis=0, tiled=True)  9.83 us
    all_to_all x1, starting transfers between devices, body(): lax.all_to_all(cot_rows.reshape(Z, X * tile, size), 'z', split_axis=0, co...  9 us
    pallas_call x1, Pallas kernels, body(): pl.pallas_call(chain_kernel, in_specs=[vmem] * (4 + X) + [hbm] * sections...  8.44 us
    all_to_all x1, waiting for transfers between devices, body(): lax.all_to_all(cot_rows.reshape(Z, X * tile, size), 'z', split_axis=0, co...  6.02 us
    unnamed x34, local copies, waits for them, and re-layouts  4.08 us
  transfers between devices with their start and end apart: 12, of which 6 were waited for; matrix products, arithmetic and copies ran while one was open for 0% of the time, Pallas kernels for 1%

profile of v3, /device:TPU:1, one launch (start us, length us, event | category | flops | bytes accessed | tf_op | source)
XLA Modules:
  0.0 136.9 jit_solution(5869314900571030057)
XLA Ops:
  0.7 2.9 %first.1 = (bf16[1040,256]{1,0:T(8,128)(2,1)S(1)}, bf16[1040,256]{1,0:T(8,128)(2,1)S(1)}, bf16[1040,256]{1,0:T(8,128)(2,1)S(1)}, bf16[1040,256]{1,0:T(8,128)(2,1)S(1)}, bf16[8,4,8,256]{3,2,1,0:T(8,128)(2,1)}) custom-call(bf16[8,2,16,512]{3,2,1,0:T(8,128)(2,1)} %constant.12.clone.table_ref, bf16[256,2048]{1,0:T(8,128)(2,1)} %bitcast.12, ...), custom_call_target="tpu_custom_call" | custom-call | tf_op jit(solution)/shard_map/first/pallas_call | solution.py:252
  3.6 0.8 copy-done.9
  4.4 0.8 copy-done.10
  5.2 9.0 %all-to-all-start.1 = ((bf16[8,32,256]{2,1,0:T(8,128)(2,1)}), bf16[8,32,256]{2,1,0:T(8,128)(2,1)S(1)}, u32[]{:S(2)}, u32[]{:S(2)}) async-start(bf16[8,32,256]{2,1,0:T(8,128)(2,1)} %bitcast.4), calls=%async_computation.1 | async-start | bytes 262144 | tf_op jit(solution)/shard_map/all_to_all | solution.py:267
  14.3 1.7 %act_rows.1 = bf16[8,2,2,2,4,8,256]{6,5,4,3,2,1,0:T(8,128)(2,1)} custom-call(bf16[256,512]{1,0:T(8,128)(2,1)S(1)} %copy-done.6, bf16[256,2048]{1,0:T(8,128)(2,1)S(1)} %bitcast.14), custom_call_target="tpu_custom_call" | custom-call | tf_op jit(solution)/shard_map/act_rows/pallas_call | solution.py:270
  16.0 6.0 %all-to-all-done.1 = bf16[8,32,256]{2,1,0:T(8,128)(2,1)S(1)} async-done(((bf16[8,32,256]{2,1,0:T(8,128)(2,1)}), bf16[8,32,256]{2,1,0:T(8,128)(2,1)S(1)}, u32[]{:S(2)}, u32[]{:S(2)}) %all-to-all-start.1) | async-done | bytes 131104 | tf_op jit(solution)/shard_map/all_to_all | solution.py:267
  22.0 9.8 %all-to-all-start = ((bf16[256,8,256]{2,1,0:T(8,128)(2,1)}), bf16[256,8,256]{2,1,0:T(8,128)(2,1)S(1)}, u32[]{:S(2)}, u32[]{:S(2)}) async-start(bf16[256,8,256]{2,1,0:T(8,128)(2,1)} %bitcast.1), calls=%async_computation | async-start | bytes 2097152 | tf_op jit(solution)/shard_map/all_to_all | solution.py:245
  31.8 1.4 %collective-permute-start.4 = (bf16[1040,256]{1,0:T(8,128)(2,1)}, bf16[1040,256]{1,0:T(8,128)(2,1)S(1)}, u32[]{:S(2)}, u32[]{:S(2)}) collective-permute-start(bf16[1040,256]{1,0:T(8,128)(2,1)} %copy-done.10), channel_id=1, source_target_pairs={{0,64},{64,128},{128,192},{192,0},{1,65},{65,129},{129,193},{193,1... | collective-permute-start | bytes 1597448 | tf_op jit(solution)/shard_map/ppermute | solution.py:249
  33.2 2.5 %collective-permute-start.6 = (bf16[1040,256]{1,0:T(8,128)(2,1)}, bf16[1040,256]{1,0:T(8,128)(2,1)S(1)}, u32[]{:S(2)}, u32[]{:S(2)}) collective-permute-start(bf16[1040,256]{1,0:T(8,128)(2,1)} %copy-done.9), channel_id=1, source_target_pairs={{0,128},{64,192},{128,0},{192,64},{1,129},{65,193},{129,1},{193,65... | collective-permute-start | bytes 1597448 | tf_op jit(solution)/shard_map/ppermute | solution.py:249
  35.7 1.1 collective-permute-start.8
  36.8 1.2 collective-permute-start.3
  38.1 15.3 %collective-permute-done.4.rest_6_ = bf16[1040,256]{1,0:T(8,128)(2,1)S(1)} collective-permute-done((bf16[1040,256]{1,0:T(8,128)(2,1)}, bf16[1040,256]{1,0:T(8,128)(2,1)S(1)}, u32[]{:S(2)}, u32[]{:S(2)}) %collective-permute-start.4) | collective-permute-done | bytes 532512 | tf_op jit(solution)/shard_map/ppermute | solution.py:249
  53.4 3.1 %collective-permute-start.5 = (bf16[1040,256]{1,0:T(8,128)(2,1)S(1)}, bf16[1040,256]{1,0:T(8,128)(2,1)S(1)}, u32[]{:S(2)}, u32[]{:S(2)}) collective-permute-start(bf16[1040,256]{1,0:T(8,128)(2,1)S(1)} %collective-permute-done.4.rest_6_), channel_id=1, source_target_pairs={{0,32},{32,0},{1,33},{33,1},{2,34},{34,2},{3,35},{35,3},{4,36},{36... | collective-permute-start | bytes 1597448 | tf_op jit(solution)/shard_map/ppermute | solution.py:249
  56.4 13.4 %collective-permute-done.6.rest_8_ = bf16[1040,256]{1,0:T(8,128)(2,1)S(1)} collective-permute-done((bf16[1040,256]{1,0:T(8,128)(2,1)}, bf16[1040,256]{1,0:T(8,128)(2,1)S(1)}, u32[]{:S(2)}, u32[]{:S(2)}) %collective-permute-start.6) | collective-permute-done | bytes 532512 | tf_op jit(solution)/shard_map/ppermute | solution.py:249
  69.8 0.9 collective-permute-start.7
  71.6 3.4 %collective-permute-done.rest_1_ = bf16[8,8,256]{2,1,0:T(8,128)(2,1)S(1)} collective-permute-done((bf16[8,8,256]{2,1,0:T(8,128)(2,1)S(1)}, bf16[8,8,256]{2,1,0:T(8,128)(2,1)S(1)}, u32[]{:S(2)}, u32[]{:S(2)}) %collective-permute-start) | collective-permute-done | bytes 32800 | tf_op jit(solution)/shard_map/ppermute | solution.py:249
  74.9 0.8 collective-permute-start.1
  75.7 3.5 %collective-permute-done.1.rest_2_ = bf16[8,8,256]{2,1,0:T(8,128)(2,1)S(1)} collective-permute-done((bf16[8,8,256]{2,1,0:T(8,128)(2,1)S(1)}, bf16[8,8,256]{2,1,0:T(8,128)(2,1)S(1)}, u32[]{:S(2)}, u32[]{:S(2)}) %collective-permute-start.1) | collective-permute-done | bytes 32800 | tf_op jit(solution)/shard_map/ppermute | solution.py:249
  79.8 2.2 %collective-permute-done.2.rest_3_ = bf16[8,8,256]{2,1,0:T(8,128)(2,1)S(1)} collective-permute-done((bf16[8,8,256]{2,1,0:T(8,128)(2,1)S(1)}, bf16[8,8,256]{2,1,0:T(8,128)(2,1)S(1)}, u32[]{:S(2)}, u32[]{:S(2)}) %collective-permute-start.2) | collective-permute-done | bytes 32800 | tf_op jit(solution)/shard_map/ppermute | solution.py:249
  82.0 0.7 copy-done.14
  82.9 0.8 copy-done.16
  83.8 8.4 %chain.1 = bf16[8,2,2,2,4,8,256]{6,5,4,3,2,1,0:T(8,128)(2,1)S(1)} custom-call(bf16[8,2,2,2,4,8,256]{6,5,4,3,2,1,0:T(8,128)(2,1)S(1)} %bitcast.9, bf16[256,512]{1,0:T(8,128)(2,1)S(1)} %copy-done.5, bf16[256,512]{1,0:T(8,128)(2,1)S(1)} %copy-done.4, bf16[2,256,256]{2,1,0:T(8,128)(2,1)S(1)} %copy-done.3, bf16[8,8,256]{2,1,0:T(8,128)(2,1)S(1)} %get-tuple-element.15.rest_0_, ...), custom_call_target="tpu_custom_call" | custom-call | tf_op jit(solution)/shard_map/chain/pallas_call | solution.py:295
  92.2 42.9 %all_to_all.15 = bf16[256,8,256]{2,1,0:T(8,128)(2,1)S(1)} all-to-all(bf16[256,8,256]{2,1,0:T(8,128)(2,1)S(1)} %bitcast.10), channel_id=1, replica_groups=mesh['y'=4,'core'=2,'x'=4,'z'=8] {'z','core','x','y'}, dimensions={0} | all-to-all | bytes 2097152 | tf_op jit(solution)/shard_map/all_to_all | solution.py:245
  135.2 1.5 %inverse_rows.1 = bf16[256,2048]{1,0:T(8,128)(2,1)} custom-call(bf16[256,512]{1,0:T(8,128)(2,1)S(1)} %copy-done.7, bf16[8,2,2,2,4,8,256]{6,5,4,3,2,1,0:T(8,128)(2,1)S(1)} %bitcast.11, bf16[256,2048]{1,0:T(8,128)(2,1)S(1)} %bitcast.13), custom_call_target="tpu_custom_call" | custom-call | tf_op jit(solution)/shard_map/inverse_rows/pallas_call | solution.py:308
  (40 shorter events, 2.3 us)
Async XLA Ops:
  0.7 13.5 %copy-start.1 = (bf16[1,2,128,2048]{3,2,1,0:T(8,128)(2,1)S(1)}, bf16[1,2,128,2048]{3,2,1,0:T(8,128)(2,1)}, u32[]{:S(2)}) copy-start(bf16[1,2,128,2048]{3,2,1,0:T(8,128)(2,1)} %param.11) | copy-start | bytes 3145732
  0.7 13.5 %copy-start.6 = (bf16[256,512]{1,0:T(8,128)(2,1)S(1)}, bf16[256,512]{1,0:T(8,128)(2,1)}, u32[]{:S(2)}) copy-start(bf16[256,512]{1,0:T(8,128)(2,1)} %constant.13.clone.table_ref) | copy-start | bytes 786436
  5.2 31.6 %copy-start.2 = (bf16[1040,256]{1,0:T(8,128)(2,1)}, bf16[1040,256]{1,0:T(8,128)(2,1)S(1)}, u32[]{:S(2)}) copy-start(bf16[1040,256]{1,0:T(8,128)(2,1)S(1)} %get-tuple-element.19.rest_4_) | copy-start | bytes 1597444
  5.2 16.8 %all-to-all-start.1 = ((bf16[8,32,256]{2,1,0:T(8,128)(2,1)}), bf16[8,32,256]{2,1,0:T(8,128)(2,1)S(1)}, u32[]{:S(2)}, u32[]{:S(2)}) async-start(bf16[8,32,256]{2,1,0:T(8,128)(2,1)} %bitcast.4), calls=%async_computation.1 | async-start | bytes 262144 | tf_op jit(solution)/shard_map/all_to_all | solution.py:267
  14.2 69.5 %copy-start.3 = (bf16[2,256,256]{2,1,0:T(8,128)(2,1)S(1)}, bf16[2,256,256]{2,1,0:T(8,128)(2,1)}, u32[]{:S(2)}) copy-start(bf16[2,256,256]{2,1,0:T(8,128)(2,1)} %constant.16.clone.fold_ref) | copy-start | bytes 786436
  14.3 69.5 %copy-start.4 = (bf16[256,512]{1,0:T(8,128)(2,1)S(1)}, bf16[256,512]{1,0:T(8,128)(2,1)}, u32[]{:S(2)}) copy-start(bf16[256,512]{1,0:T(8,128)(2,1)} %constant.15.clone.inv_ref) | copy-start | bytes 786436
  14.3 69.5 %copy-start.5 = (bf16[256,512]{1,0:T(8,128)(2,1)S(1)}, bf16[256,512]{1,0:T(8,128)(2,1)}, u32[]{:S(2)}) copy-start(bf16[256,512]{1,0:T(8,128)(2,1)} %constant.14.clone.col_ref) | copy-start | bytes 786436
  22.0 61.8 %all-to-all-start = ((bf16[256,8,256]{2,1,0:T(8,128)(2,1)}), bf16[256,8,256]{2,1,0:T(8,128)(2,1)S(1)}, u32[]{:S(2)}, u32[]{:S(2)}) async-start(bf16[256,8,256]{2,1,0:T(8,128)(2,1)} %bitcast.1), calls=%async_computation | async-start | bytes 2097152 | tf_op jit(solution)/shard_map/all_to_all | solution.py:245
  31.8 21.5 %collective-permute-start.4 = (bf16[1040,256]{1,0:T(8,128)(2,1)}, bf16[1040,256]{1,0:T(8,128)(2,1)S(1)}, u32[]{:S(2)}, u32[]{:S(2)}) collective-permute-start(bf16[1040,256]{1,0:T(8,128)(2,1)} %copy-done.10), channel_id=1, source_target_pairs={{0,64},{64,128},{128,192},{192,0},{1,65},{65,129},{129,193},{193,1... | collective-permute-start | bytes 1597448 | tf_op jit(solution)/shard_map/ppermute | solution.py:249
  33.2 36.6 %collective-permute-start.6 = (bf16[1040,256]{1,0:T(8,128)(2,1)}, bf16[1040,256]{1,0:T(8,128)(2,1)S(1)}, u32[]{:S(2)}, u32[]{:S(2)}) collective-permute-start(bf16[1040,256]{1,0:T(8,128)(2,1)} %copy-done.9), channel_id=1, source_target_pairs={{0,128},{64,192},{128,0},{192,64},{1,129},{65,193},{129,1},{193,65... | collective-permute-start | bytes 1597448 | tf_op jit(solution)/shard_map/ppermute | solution.py:249
  35.7 35.1 %collective-permute-start.8 = (bf16[1040,256]{1,0:T(8,128)(2,1)S(1)}, bf16[1040,256]{1,0:T(8,128)(2,1)S(1)}, u32[]{:S(2)}, u32[]{:S(2)}) collective-permute-start(bf16[1040,256]{1,0:T(8,128)(2,1)S(1)} %get-tuple-element.22), channel_id=1, source_target_pairs={{0,192},{64,0},{128,64},{192,128},{1,193},{65,1},{129,65},{193,129... | collective-permute-start | bytes 1597448 | tf_op jit(solution)/shard_map/ppermute | solution.py:249
  36.8 45.1 %collective-permute-start.3 = (bf16[1040,256]{1,0:T(8,128)(2,1)S(1)}, bf16[1040,256]{1,0:T(8,128)(2,1)S(1)}, u32[]{:S(2)}, u32[]{:S(2)}) collective-permute-start(bf16[1040,256]{1,0:T(8,128)(2,1)S(1)} %get-tuple-element.19.rest_4_), channel_id=1, source_target_pairs={{0,32},{32,0},{1,33},{33,1},{2,34},{34,2},{3,35},{35,3},{4,36},{36... | collective-permute-start | bytes 1597448 | tf_op jit(solution)/shard_map/ppermute | solution.py:249
  53.4 28.6 %copy-start.11 = (bf16[1040,256]{1,0:T(8,128)(2,1)}, bf16[1040,256]{1,0:T(8,128)(2,1)S(1)}, u32[]{:S(2)}) copy-start(bf16[1040,256]{1,0:T(8,128)(2,1)S(1)} %collective-permute-done.4.rest_6_) | copy-start | bytes 1597444
  53.4 28.6 %collective-permute-start.5 = (bf16[1040,256]{1,0:T(8,128)(2,1)S(1)}, bf16[1040,256]{1,0:T(8,128)(2,1)S(1)}, u32[]{:S(2)}, u32[]{:S(2)}) collective-permute-start(bf16[1040,256]{1,0:T(8,128)(2,1)S(1)} %collective-permute-done.4.rest_6_), channel_id=1, source_target_pairs={{0,32},{32,0},{1,33},{33,1},{2,34},{34,2},{3,35},{35,3},{4,36},{36... | collective-permute-start | bytes 1597448 | tf_op jit(solution)/shard_map/ppermute | solution.py:249
  69.8 12.2 %copy-start.12 = (bf16[1040,256]{1,0:T(8,128)(2,1)}, bf16[1040,256]{1,0:T(8,128)(2,1)S(1)}, u32[]{:S(2)}) copy-start(bf16[1040,256]{1,0:T(8,128)(2,1)S(1)} %collective-permute-done.6.rest_8_) | copy-start | bytes 1597444
  69.8 12.2 %collective-permute-start.7 = (bf16[1040,256]{1,0:T(8,128)(2,1)S(1)}, bf16[1040,256]{1,0:T(8,128)(2,1)S(1)}, u32[]{:S(2)}, u32[]{:S(2)}) collective-permute-start(bf16[1040,256]{1,0:T(8,128)(2,1)S(1)} %collective-permute-done.6.rest_8_), channel_id=1, source_target_pairs={{0,32},{32,0},{1,33},{33,1},{2,34},{34,2},{3,35},{35,3},{4,36},{36... | collective-permute-start | bytes 1597448 | tf_op jit(solution)/shard_map/ppermute | solution.py:249
  70.8 11.3 %copy-start.13 = (bf16[1040,256]{1,0:T(8,128)(2,1)}, bf16[1040,256]{1,0:T(8,128)(2,1)S(1)}, u32[]{:S(2)}) copy-start(bf16[1040,256]{1,0:T(8,128)(2,1)S(1)} %collective-permute-done.8.rest_10_) | copy-start | bytes 1597444
  70.8 13.0 %collective-permute-start.9 = (bf16[1040,256]{1,0:T(8,128)(2,1)S(1)}, bf16[1040,256]{1,0:T(8,128)(2,1)}, u32[]{:S(2)}, u32[]{:S(2)}) collective-permute-start(bf16[1040,256]{1,0:T(8,128)(2,1)S(1)} %collective-permute-done.8.rest_10_), channel_id=1, source_target_pairs={{0,32},{32,0},{1,33},{33,1},{2,34},{34,2},{3,35},{35,3},{4,36},{36... | collective-permute-start | bytes 1597448 | tf_op jit(solution)/shard_map/ppermute | solution.py:249
  70.9 4.1 %collective-permute-start = (bf16[8,8,256]{2,1,0:T(8,128)(2,1)S(1)}, bf16[8,8,256]{2,1,0:T(8,128)(2,1)S(1)}, u32[]{:S(2)}, u32[]{:S(2)}) collective-permute-start(bf16[8,8,256]{2,1,0:T(8,128)(2,1)S(1)} %get-tuple-element.16), channel_id=1, source_target_pairs={{0,8},{8,16},{16,24},{24,0},{1,9},{9,17},{17,25},{25,1},{2,10},{10... | collective-permute-start | bytes 98312 | tf_op jit(solution)/shard_map/ppermute | solution.py:249
  74.9 4.3 %collective-permute-start.1 = (bf16[8,8,256]{2,1,0:T(8,128)(2,1)S(1)}, bf16[8,8,256]{2,1,0:T(8,128)(2,1)S(1)}, u32[]{:S(2)}, u32[]{:S(2)}) collective-permute-start(bf16[8,8,256]{2,1,0:T(8,128)(2,1)S(1)} %get-tuple-element.17), channel_id=1, source_target_pairs={{0,16},{8,24},{16,0},{24,8},{1,17},{9,25},{17,1},{25,9},{2,18},{10... | collective-permute-start | bytes 98312 | tf_op jit(solution)/shard_map/ppermute | solution.py:249
  79.2 2.8 %collective-permute-start.2 = (bf16[8,8,256]{2,1,0:T(8,128)(2,1)S(1)}, bf16[8,8,256]{2,1,0:T(8,128)(2,1)S(1)}, u32[]{:S(2)}, u32[]{:S(2)}) collective-permute-start(bf16[8,8,256]{2,1,0:T(8,128)(2,1)S(1)} %get-tuple-element.18), channel_id=1, source_target_pairs={{0,24},{8,0},{16,8},{24,16},{1,25},{9,1},{17,9},{25,17},{2,26},{10... | collective-permute-start | bytes 98312 | tf_op jit(solution)/shard_map/ppermute | solution.py:249
  82.0 1.0 copy-start.15
  92.2 42.9 %copy-start = (bf16[2,128,2048]{2,1,0:T(8,128)(2,1)S(1)}, bf16[2,128,2048]{2,1,0:T(8,128)(2,1)}, u32[]{:S(2)}) copy-start(bf16[2,128,2048]{2,1,0:T(8,128)(2,1)} %param.12) | copy-start | bytes 3145732
  92.2 42.9 %copy-start.7 = (bf16[256,512]{1,0:T(8,128)(2,1)S(1)}, bf16[256,512]{1,0:T(8,128)(2,1)}, u32[]{:S(2)}) copy-start(bf16[256,512]{1,0:T(8,128)(2,1)} %constant.17.clone.table_ref) | copy-start | bytes 786436
  (5 other events, 3.9 us)

commit v4 on v2

--- a/solution.py
+++ b/solution.py
@@ -13,6 +13,8 @@
 BF16 = jnp.bfloat16
 F32 = jnp.float32
 X, Y, Z = 4, 4, 8
+SMALL = pltpu.CompilerParams(vmem_limit_bytes=20 << 20)
+TIGHT = pltpu.CompilerParams(vmem_limit_bytes=20 << 20)
 EVERYONE = ("z", "core", "x", "y")
 
 
@@ -106,9 +108,11 @@
 
 def prologue_kernel(table_ref, act_ref, first_ref, second_ref, bias_ref, *rest):
     pieces = rest[:Y]
-    rows_ref, held, sems = rest[Y:]
+    rows_ref, held, biases, sems, bias_sem = rest[Y:]
     size = held.shape[2]
     y, odd = lax.axis_index("y"), lax.axis_index("x") & 1
+    bias_copy = pltpu.make_async_copy(bias_ref, biases, bias_sem)
+    bias_copy.start()
     loads = []
     for d in range(Y):
         block = ((y + d) & (Y - 1)) * 2 + odd
@@ -121,24 +125,31 @@
                 )
                 copy.start()
                 loads.append(copy)
-        bias = bias_ref[0, :, pl.ds(block * size, size)]
+
+    def transform(n):
+        spectrum = twice(table_ref, act_ref[:, n * size : (n + 1) * size]).astype(BF16)
+        rows_ref[:, :, :, n % 2, n // 2] = spectrum.reshape(Z, 2, 2, 8, size)
+
+    for n in range(4):
+        transform(n)
+    bias_copy.wait()
+    for d in range(Y):
+        block = ((y + d) & (Y - 1)) * 2 + odd
+        bias = biases[0, :, pl.ds(block * size, size)]
         high = bias.astype(BF16).astype(F32)
         middle = (bias - high).astype(BF16).astype(F32)
         low = bias - high - middle
         packed = jnp.concatenate([high, middle, low, jnp.zeros((10, size), F32)], axis=0)
         held[d, 4 * size : 4 * size + 16] = packed.astype(BF16)
-
+    for copy in loads:
+        copy.wait()
     stores = []
-    for n in range(2 * Y):
-        if n == 2:
-            for copy in loads:
-                copy.wait()
-            for d in range(Y):
-                copy = pltpu.make_async_copy(held.at[d], pieces[d], sems.at[d, 4])
-                copy.start()
-                stores.append(copy)
-        spectrum = twice(table_ref, act_ref[:, n * size : (n + 1) * size]).astype(BF16)
-        rows_ref[:, :, :, n % 2, n // 2] = spectrum.reshape(Z, 2, 2, 8, size)
+    for d in range(Y):
+        copy = pltpu.make_async_copy(held.at[d], pieces[d], sems.at[d, 4])
+        copy.start()
+        stores.append(copy)
+    for n in range(4, 2 * Y):
+        transform(n)
     for copy in stores:
         copy.wait()
 
@@ -167,17 +178,21 @@
 def chain_kernel(act_ref, col_ref, inv_ref, fold_ref, *rest):
     sections = 2 * Y
     cots, weights = rest[:X], rest[X : X + sections]
-    out_ref, held, found, sems = rest[X + sections :]
+    out_ref, found, held, sems = rest[X + sections :]
     size = act_ref.shape[6]
     half = col_ref.shape[0] // 2
     y, core, x, z = (lax.axis_index(name) for name in ("y", "core", "x", "z"))
-    copies = []
-    for d in range(Y):
-        for i in range(2):
-            slot = ((y - d) & (Y - 1)) * 2 + (core if i == 0 else 1 - core)
-            copy = pltpu.make_async_copy(weights[2 * d + i], held.at[slot], sems.at[2 * d + i])
-            copy.start()
-            copies.append(copy)
+
+    def load(p, source):
+        return pltpu.make_async_copy(weights[source], held.at[p], sems.at[p])
+
+    for here in range(sections):
+
+        @pl.when(y * 2 + core == here)
+        def _():
+            for p in range(sections - 1, -1, -1):
+                load(p, 2 * ((here // 2 - p // 2) % Y) + (p % 2 != here % 2)).start()
+
     for e in range(X):
         found[:, (x - e) & (X - 1)] = cots[e][...]
     has_zero = jnp.logical_and(jnp.logical_and(core == 0, x < 2), z == 0)
@@ -191,10 +206,9 @@
     for p in range(sections):
         columns = act_ref[:, p % 2, :, :, p // 2].reshape(2 * half, size)
         spectra.append(twice(col_ref, columns).astype(BF16))
-    for copy in copies:
-        copy.wait()
 
     for p in range(sections - 1, -1, -1):
+        load(p, 0).wait()
         a_re, a_im = held[p, 0:size], held[p, size : 2 * size]
         b_re, b_im = held[p, 2 * size : 3 * size], held[p, 3 * size : 4 * size]
         bias = held[p, 4 * size : 4 * size + 16].astype(F32)
@@ -237,7 +251,13 @@
     blocks = (Z, 2, 2, 2, Y, tile, size)
 
     def shaped(*dims):
-        return jax.ShapeDtypeStruct(dims, BF16)
+        return pltpu.VMEM(dims, BF16)
+
+    def near(*values):
+        return [pltpu.with_memory_space_constraint(value, pltpu.VMEM) for value in values]
+
+    def far(*values):
+        return [pltpu.with_memory_space_constraint(value, pltpu.HBM) for value in values]
 
     def exchange(value):
         flat = value.reshape(sections * columns, tile, size)
@@ -250,7 +270,7 @@
     flat_cot = cotangent.reshape(count, channels)
     cot_rows = pl.pallas_call(
         cot_kernel,
-        in_specs=[hbm, hbm],
+        in_specs=[hbm] * 2,
         out_specs=vmem,
         out_shape=shaped(Z, X, tile, size),
         scratch_shapes=[
@@ -258,22 +278,29 @@
             pltpu.VMEM((count, 2 * size), BF16),
             pltpu.SemaphoreType.DMA((2,)),
         ],
+        compiler_params=SMALL,
         name="cot_rows",
-    )(forward_rows.reshape(Z, 2, 2 * tile, 2 * count), flat_cot)
+    )(*far(jnp.asarray(forward_rows.reshape(Z, 2, 2 * tile, -1)), flat_cot))
     cot_blocks = lax.all_to_all(
         cot_rows.reshape(Z, X * tile, size), "z", split_axis=0, concat_axis=0, tiled=True
     ).reshape(cot_rows.shape)
     made = pl.pallas_call(
         prologue_kernel,
-        in_specs=[vmem, vmem, hbm, hbm, vmem],
+        in_specs=[vmem] * 2 + [hbm] * 3,
         out_specs=[hbm] * Y + [vmem],
-        out_shape=[shaped(4 * size + 16, size)] * Y + [shaped(*blocks)],
+        out_shape=[pltpu.HBM((4 * size + 16, size), BF16)] * Y + [shaped(*blocks)],
         scratch_shapes=[
             pltpu.VMEM((Y, 4 * size + 16, size), BF16),
+            pltpu.VMEM(b_first.shape, F32),
             pltpu.SemaphoreType.DMA((Y, 5)),
+            pltpu.SemaphoreType.DMA(()),
         ],
+        compiler_params=SMALL,
         name="prologue",
-    )(forward_rows, activations.reshape(count, channels), w_first, w_second, b_first)
+    )(
+        *near(jnp.asarray(forward_rows), activations.reshape(count, channels)),
+        *far(w_first, w_second, b_first),
+    )
     pieces, act_rows = made[:Y], made[Y]
 
     weights = []
@@ -286,30 +313,34 @@
         in_specs=[vmem],
         out_specs=[vmem] * X,
         out_shape=[shaped(Z, tile, size)] * X,
+        compiler_params=SMALL,
         name="turn",
-    )(cot_blocks)
+    )(*near(cot_blocks))
     cots = [turned[0]] + [shifted(turned[e], "x", e) for e in range(1, X)]
 
+    tables = [jnp.asarray(table) for table in (forward_columns, inverse_columns, folds)]
     back = pl.pallas_call(
         chain_kernel,
         in_specs=[vmem] * (4 + X) + [hbm] * sections,
         out_specs=vmem,
         out_shape=shaped(*blocks),
         scratch_shapes=[
+            pltpu.VMEM((Z, X, tile, size), BF16),
             pltpu.VMEM((sections, 4 * size + 16, size), BF16),
-            pltpu.VMEM((Z, X, tile, size), BF16),
             pltpu.SemaphoreType.DMA((sections,)),
         ],
+        compiler_params=TIGHT,
         name="chain",
-    )(act_columns, forward_columns, inverse_columns, folds, *cots, *weights)
+    )(*near(act_columns, *tables, *cots), *far(*weights))
     grads = pl.pallas_call(
         inverse_kernel,
         in_specs=[vmem] * 3,
         out_specs=hbm,
-        out_shape=shaped(count, channels),
+        out_shape=jax.ShapeDtypeStruct((count, channels), BF16),
         scratch_shapes=[pltpu.VMEM((count, channels), BF16), pltpu.SemaphoreType.DMA((sections,))],
+        compiler_params=SMALL,
         name="inverse_rows",
-    )(inverse_rows, exchange(back), flat_cot)
+    )(*near(jnp.asarray(inverse_rows), exchange(back), flat_cot))
     return grads.reshape(1, rows, width, channels)
 
 

time: 141 us -> 136 us (0.965)
  Pallas kernels: 22.5 us -> 16.2 us
  local copies, waits for them, and re-layouts: 0.94 us -> 2.76 us
    pallas_call x1, Pallas kernels: 10.4 us -> 8.44 us  [body(): pl.pallas_call(chain_kernel, in_specs=[vmem] * (4 + X) + [hbm] * sections...]
    unnamed x18 -> x28, local copies, waits for them, and re-layouts: 0.94 us -> 2.76 us
    pallas_call x1, Pallas kernels: 1.69 us -> 0.02 us  [body(): pl.pallas_call(turn_kernel, in_specs=[vmem], out_specs=[vmem] * X, out_sh...]
    pallas_call x1, Pallas kernels: 3.15 us -> 1.54 us  [body(): pl.pallas_call(inverse_kernel, in_specs=[vmem] * 3, out_specs=hbm, out_sh...]
  transfers between devices with their start and end apart: 12 -> 12, of which waited for: 6 -> 6; matrix products, arithmetic and copies ran while one was open for 0% -> 0% of each run, Pallas kernels for 5% -> 3%
where the time goes in v4:
time: 136 us; the launch traced here: 135 us
  blocking collectives  42.9 us (32%)
  waiting for transfers between devices  40.3 us (30%)
  starting transfers between devices  32.7 us (24%)
  Pallas kernels  16.2 us (12%)
  local copies, waits for them, and re-layouts  2.76 us (2%)
    all_to_all x1, blocking collectives, exchange(): lax.all_to_all(flat, EVERYONE, split_axis=0, concat_axis=0, tiled=True)  42.9 us
    ppermute x10, waiting for transfers between devices, shifted(): lax.ppermute(value, axis, [(i, (i + distance) % size) for i in range(size)])  37.8 us
    ppermute x10, starting transfers between devices, shifted(): lax.ppermute(value, axis, [(i, (i + distance) % size) for i in range(size)])  12.4 us
    all_to_all x1, starting transfers between devices, exchange(): lax.all_to_all(flat, EVERYONE, split_axis=0, concat_axis=0, tiled=True)  11.3 us
    all_to_all x1, starting transfers between devices, body(): lax.all_to_all(cot_rows.reshape(Z, X * tile, size), 'z', split_axis=0, co...  9.01 us
    pallas_call x1, Pallas kernels, body(): pl.pallas_call(chain_kernel, in_specs=[vmem] * (4 + X) + [hbm] * sections...  8.44 us
    pallas_call x1, Pallas kernels, body(): pl.pallas_call(prologue_kernel, in_specs=[vmem] * 2 + [hbm] * 3, out_spec...  4.18 us
    unnamed x28, local copies, waits for them, and re-layouts  2.76 us
  transfers between devices with their start and end apart: 12, of which 6 were waited for; matrix products, arithmetic and copies ran while one was open for 0% of the time, Pallas kernels for 3%

profile of v4, /device:TPU:1, one launch (start us, length us, event | category | flops | bytes accessed | tf_op | source)
XLA Modules:
  0.0 135.2 jit_solution(1201790352807961401)
XLA Ops:
  0.0 2.0 %cot_rows.1 = bf16[8,4,8,256]{3,2,1,0:T(8,128)(2,1)} custom-call(bf16[8,2,16,512]{3,2,1,0:T(8,128)(2,1)} %constant.12.clone.table_ref, bf16[256,2048]{1,0:T(8,128)(2,1)} %bitcast.11), custom_call_target="tpu_custom_call" | custom-call | tf_op jit(solution)/shard_map/cot_rows/pallas_call | solution.py:271
  2.0 9.0 %all-to-all-start.1 = ((bf16[8,32,256]{2,1,0:T(8,128)(2,1)}), bf16[8,32,256]{2,1,0:T(8,128)(2,1)S(1)}, u32[]{:S(2)}, u32[]{:S(2)}) async-start(bf16[8,32,256]{2,1,0:T(8,128)(2,1)} %bitcast.4), calls=%async_computation.1 | async-start | bytes 262144 | tf_op jit(solution)/shard_map/all_to_all | solution.py:284
  11.0 0.9 copy-done.6
  12.0 4.2 %prologue.1 = (bf16[1040,256]{1,0:T(8,128)(2,1)}, bf16[1040,256]{1,0:T(8,128)(2,1)}, bf16[1040,256]{1,0:T(8,128)(2,1)}, bf16[1040,256]{1,0:T(8,128)(2,1)}, bf16[8,2,2,2,4,8,256]{6,5,4,3,2,1,0:T(8,128)(2,1)}) custom-call(bf16[256,512]{1,0:T(8,128)(2,1)S(1)} %copy-done.6, bf16[256,2048]{1,0:T(8,128)(2,1)S(1)} %bitcast.14, ...), custom_call_target="tpu_custom_call" | custom-call | tf_op jit(solution)/shard_map/prologue/pallas_call | solution.py:287
  16.2 2.6 %all-to-all-done.1 = bf16[8,32,256]{2,1,0:T(8,128)(2,1)S(1)} async-done(((bf16[8,32,256]{2,1,0:T(8,128)(2,1)}), bf16[8,32,256]{2,1,0:T(8,128)(2,1)S(1)}, u32[]{:S(2)}, u32[]{:S(2)}) %all-to-all-start.1) | async-done | bytes 131104 | tf_op jit(solution)/shard_map/all_to_all | solution.py:284
  18.8 11.3 %all-to-all-start = ((bf16[256,8,256]{2,1,0:T(8,128)(2,1)}), bf16[256,8,256]{2,1,0:T(8,128)(2,1)S(1)}, u32[]{:S(2)}, u32[]{:S(2)}) async-start(bf16[256,8,256]{2,1,0:T(8,128)(2,1)} %bitcast.1), calls=%async_computation | async-start | bytes 2097152 | tf_op jit(solution)/shard_map/all_to_all | solution.py:264
  30.1 1.4 %collective-permute-start.4 = (bf16[1040,256]{1,0:T(8,128)(2,1)}, bf16[1040,256]{1,0:T(8,128)(2,1)S(1)}, u32[]{:S(2)}, u32[]{:S(2)}) collective-permute-start(bf16[1040,256]{1,0:T(8,128)(2,1)} %get-tuple-element.20), channel_id=1, source_target_pairs={{0,64},{64,128},{128,192},{192,0},{1,65},{65,129},{129,193},{193,1... | collective-permute-start | bytes 1597448 | tf_op jit(solution)/shard_map/ppermute | solution.py:268
  31.5 2.5 %collective-permute-start.6 = (bf16[1040,256]{1,0:T(8,128)(2,1)}, bf16[1040,256]{1,0:T(8,128)(2,1)S(1)}, u32[]{:S(2)}, u32[]{:S(2)}) collective-permute-start(bf16[1040,256]{1,0:T(8,128)(2,1)} %get-tuple-element.21), channel_id=1, source_target_pairs={{0,128},{64,192},{128,0},{192,64},{1,129},{65,193},{129,1},{193,65... | collective-permute-start | bytes 1597448 | tf_op jit(solution)/shard_map/ppermute | solution.py:268
  34.0 1.1 collective-permute-start.8
  35.1 1.2 collective-permute-start.3
  36.3 15.3 %collective-permute-done.4.rest_6_ = bf16[1040,256]{1,0:T(8,128)(2,1)S(1)} collective-permute-done((bf16[1040,256]{1,0:T(8,128)(2,1)}, bf16[1040,256]{1,0:T(8,128)(2,1)S(1)}, u32[]{:S(2)}, u32[]{:S(2)}) %collective-permute-start.4) | collective-permute-done | bytes 532512 | tf_op jit(solution)/shard_map/ppermute | solution.py:268
  51.6 3.1 %collective-permute-start.5 = (bf16[1040,256]{1,0:T(8,128)(2,1)S(1)}, bf16[1040,256]{1,0:T(8,128)(2,1)S(1)}, u32[]{:S(2)}, u32[]{:S(2)}) collective-permute-start(bf16[1040,256]{1,0:T(8,128)(2,1)S(1)} %collective-permute-done.4.rest_6_), channel_id=1, source_target_pairs={{0,32},{32,0},{1,33},{33,1},{2,34},{34,2},{3,35},{35,3},{4,36},{36... | collective-permute-start | bytes 1597448 | tf_op jit(solution)/shard_map/ppermute | solution.py:268
  54.7 13.4 %collective-permute-done.6.rest_8_ = bf16[1040,256]{1,0:T(8,128)(2,1)S(1)} collective-permute-done((bf16[1040,256]{1,0:T(8,128)(2,1)}, bf16[1040,256]{1,0:T(8,128)(2,1)S(1)}, u32[]{:S(2)}, u32[]{:S(2)}) %collective-permute-start.6) | collective-permute-done | bytes 532512 | tf_op jit(solution)/shard_map/ppermute | solution.py:268
  68.1 0.9 collective-permute-start.7
  69.2 0.7 collective-permute-start
  69.8 3.4 %collective-permute-done.rest_1_ = bf16[8,8,256]{2,1,0:T(8,128)(2,1)S(1)} collective-permute-done((bf16[8,8,256]{2,1,0:T(8,128)(2,1)S(1)}, bf16[8,8,256]{2,1,0:T(8,128)(2,1)S(1)}, u32[]{:S(2)}, u32[]{:S(2)}) %collective-permute-start) | collective-permute-done | bytes 32800 | tf_op jit(solution)/shard_map/ppermute | solution.py:268
  73.2 0.8 collective-permute-start.1
  74.0 3.5 %collective-permute-done.1.rest_2_ = bf16[8,8,256]{2,1,0:T(8,128)(2,1)S(1)} collective-permute-done((bf16[8,8,256]{2,1,0:T(8,128)(2,1)S(1)}, bf16[8,8,256]{2,1,0:T(8,128)(2,1)S(1)}, u32[]{:S(2)}, u32[]{:S(2)}) %collective-permute-start.1) | collective-permute-done | bytes 32800 | tf_op jit(solution)/shard_map/ppermute | solution.py:268
  78.0 2.2 %collective-permute-done.2.rest_3_ = bf16[8,8,256]{2,1,0:T(8,128)(2,1)S(1)} collective-permute-done((bf16[8,8,256]{2,1,0:T(8,128)(2,1)S(1)}, bf16[8,8,256]{2,1,0:T(8,128)(2,1)S(1)}, u32[]{:S(2)}, u32[]{:S(2)}) %collective-permute-start.2) | collective-permute-done | bytes 32800 | tf_op jit(solution)/shard_map/ppermute | solution.py:268
  80.3 0.7 copy-done.11
  81.3 0.8 copy-done.13
  82.1 8.4 %chain.1 = bf16[8,2,2,2,4,8,256]{6,5,4,3,2,1,0:T(8,128)(2,1)S(1)} custom-call(bf16[8,2,2,2,4,8,256]{6,5,4,3,2,1,0:T(8,128)(2,1)S(1)} %bitcast.9, bf16[256,512]{1,0:T(8,128)(2,1)S(1)} %copy-done.4, bf16[256,512]{1,0:T(8,128)(2,1)S(1)} %copy-done.3, bf16[2,256,256]{2,1,0:T(8,128)(2,1)S(1)} %copy-done.2, bf16[8,8,256]{2,1,0:T(8,128)(2,1)S(1)} %get-tuple-element.15.rest_0_, ...), custom_call_target="tpu_custom_call" | custom-call | tf_op jit(solution)/shard_map/chain/pallas_call | solution.py:322
  90.6 42.9 %all_to_all.15 = bf16[256,8,256]{2,1,0:T(8,128)(2,1)S(1)} all-to-all(bf16[256,8,256]{2,1,0:T(8,128)(2,1)S(1)} %bitcast.10), channel_id=1, replica_groups=mesh['y'=4,'core'=2,'x'=4,'z'=8] {'z','core','x','y'}, dimensions={0} | all-to-all | bytes 2097152 | tf_op jit(solution)/shard_map/all_to_all | solution.py:264
  133.5 1.5 %inverse_rows.1 = bf16[256,2048]{1,0:T(8,128)(2,1)} custom-call(bf16[256,512]{1,0:T(8,128)(2,1)S(1)} %copy-done.5, bf16[8,2,2,2,4,8,256]{6,5,4,3,2,1,0:T(8,128)(2,1)S(1)} %bitcast.13, bf16[256,2048]{1,0:T(8,128)(2,1)S(1)} %bitcast.12), custom_call_target="tpu_custom_call" | custom-call | tf_op jit(solution)/shard_map/inverse_rows/pallas_call | solution.py:335
  (34 shorter events, 1.0 us)
Async XLA Ops:
  0.0 11.0 %copy-start.1 = (bf16[1,2,128,2048]{3,2,1,0:T(8,128)(2,1)S(1)}, bf16[1,2,128,2048]{3,2,1,0:T(8,128)(2,1)}, u32[]{:S(2)}) copy-start(bf16[1,2,128,2048]{3,2,1,0:T(8,128)(2,1)} %param.11) | copy-start | bytes 3145732
  2.0 16.8 %all-to-all-start.1 = ((bf16[8,32,256]{2,1,0:T(8,128)(2,1)}), bf16[8,32,256]{2,1,0:T(8,128)(2,1)S(1)}, u32[]{:S(2)}, u32[]{:S(2)}) async-start(bf16[8,32,256]{2,1,0:T(8,128)(2,1)} %bitcast.4), calls=%async_computation.1 | async-start | bytes 262144 | tf_op jit(solution)/shard_map/all_to_all | solution.py:284
  11.0 1.0 copy-start.6
  16.2 18.9 %copy-start.7 = (bf16[1040,256]{1,0:T(8,128)(2,1)S(1)}, bf16[1040,256]{1,0:T(8,128)(2,1)}, u32[]{:S(2)}) copy-start(bf16[1040,256]{1,0:T(8,128)(2,1)} %get-tuple-element.19.rest_4_) | copy-start | bytes 1597444
  16.2 65.9 %copy-start.2 = (bf16[2,256,256]{2,1,0:T(8,128)(2,1)S(1)}, bf16[2,256,256]{2,1,0:T(8,128)(2,1)}, u32[]{:S(2)}) copy-start(bf16[2,256,256]{2,1,0:T(8,128)(2,1)} %constant.16.clone.fold_ref) | copy-start | bytes 786436
  16.2 65.9 %copy-start.3 = (bf16[256,512]{1,0:T(8,128)(2,1)S(1)}, bf16[256,512]{1,0:T(8,128)(2,1)}, u32[]{:S(2)}) copy-start(bf16[256,512]{1,0:T(8,128)(2,1)} %constant.15.clone.inv_ref) | copy-start | bytes 786436
  16.2 65.9 %copy-start.4 = (bf16[256,512]{1,0:T(8,128)(2,1)S(1)}, bf16[256,512]{1,0:T(8,128)(2,1)}, u32[]{:S(2)}) copy-start(bf16[256,512]{1,0:T(8,128)(2,1)} %constant.14.clone.col_ref) | copy-start | bytes 786436
  18.8 63.3 %all-to-all-start = ((bf16[256,8,256]{2,1,0:T(8,128)(2,1)}), bf16[256,8,256]{2,1,0:T(8,128)(2,1)S(1)}, u32[]{:S(2)}, u32[]{:S(2)}) async-start(bf16[256,8,256]{2,1,0:T(8,128)(2,1)} %bitcast.1), calls=%async_computation | async-start | bytes 2097152 | tf_op jit(solution)/shard_map/all_to_all | solution.py:264
  30.1 21.5 %collective-permute-start.4 = (bf16[1040,256]{1,0:T(8,128)(2,1)}, bf16[1040,256]{1,0:T(8,128)(2,1)S(1)}, u32[]{:S(2)}, u32[]{:S(2)}) collective-permute-start(bf16[1040,256]{1,0:T(8,128)(2,1)} %get-tuple-element.20), channel_id=1, source_target_pairs={{0,64},{64,128},{128,192},{192,0},{1,65},{65,129},{129,193},{193,1... | collective-permute-start | bytes 1597448 | tf_op jit(solution)/shard_map/ppermute | solution.py:268
  31.5 36.6 %collective-permute-start.6 = (bf16[1040,256]{1,0:T(8,128)(2,1)}, bf16[1040,256]{1,0:T(8,128)(2,1)S(1)}, u32[]{:S(2)}, u32[]{:S(2)}) collective-permute-start(bf16[1040,256]{1,0:T(8,128)(2,1)} %get-tuple-element.21), channel_id=1, source_target_pairs={{0,128},{64,192},{128,0},{192,64},{1,129},{65,193},{129,1},{193,65... | collective-permute-start | bytes 1597448 | tf_op jit(solution)/shard_map/ppermute | solution.py:268
  34.0 35.1 %collective-permute-start.8 = (bf16[1040,256]{1,0:T(8,128)(2,1)}, bf16[1040,256]{1,0:T(8,128)(2,1)S(1)}, u32[]{:S(2)}, u32[]{:S(2)}) collective-permute-start(bf16[1040,256]{1,0:T(8,128)(2,1)} %get-tuple-element.22), channel_id=1, source_target_pairs={{0,192},{64,0},{128,64},{192,128},{1,193},{65,1},{129,65},{193,129... | collective-permute-start | bytes 1597448 | tf_op jit(solution)/shard_map/ppermute | solution.py:268
  35.1 45.1 %collective-permute-start.3 = (bf16[1040,256]{1,0:T(8,128)(2,1)S(1)}, bf16[1040,256]{1,0:T(8,128)(2,1)S(1)}, u32[]{:S(2)}, u32[]{:S(2)}) collective-permute-start(bf16[1040,256]{1,0:T(8,128)(2,1)S(1)} %copy-done.7), channel_id=1, source_target_pairs={{0,32},{32,0},{1,33},{33,1},{2,34},{34,2},{3,35},{35,3},{4,36},{36... | collective-permute-start | bytes 1597448 | tf_op jit(solution)/shard_map/ppermute | solution.py:268
  51.6 30.4 %copy-start.8 = (bf16[1040,256]{1,0:T(8,128)(2,1)}, bf16[1040,256]{1,0:T(8,128)(2,1)S(1)}, u32[]{:S(2)}) copy-start(bf16[1040,256]{1,0:T(8,128)(2,1)S(1)} %collective-permute-done.4.rest_6_) | copy-start | bytes 1597444
  51.6 28.6 %collective-permute-start.5 = (bf16[1040,256]{1,0:T(8,128)(2,1)S(1)}, bf16[1040,256]{1,0:T(8,128)(2,1)S(1)}, u32[]{:S(2)}, u32[]{:S(2)}) collective-permute-start(bf16[1040,256]{1,0:T(8,128)(2,1)S(1)} %collective-permute-done.4.rest_6_), channel_id=1, source_target_pairs={{0,32},{32,0},{1,33},{33,1},{2,34},{34,2},{3,35},{35,3},{4,36},{36... | collective-permute-start | bytes 1597448 | tf_op jit(solution)/shard_map/ppermute | solution.py:268
  68.1 12.2 %copy-start.9 = (bf16[1040,256]{1,0:T(8,128)(2,1)}, bf16[1040,256]{1,0:T(8,128)(2,1)S(1)}, u32[]{:S(2)}) copy-start(bf16[1040,256]{1,0:T(8,128)(2,1)S(1)} %collective-permute-done.6.rest_8_) | copy-start | bytes 1597444
  68.1 12.2 %collective-permute-start.7 = (bf16[1040,256]{1,0:T(8,128)(2,1)S(1)}, bf16[1040,256]{1,0:T(8,128)(2,1)S(1)}, u32[]{:S(2)}, u32[]{:S(2)}) collective-permute-start(bf16[1040,256]{1,0:T(8,128)(2,1)S(1)} %collective-permute-done.6.rest_8_), channel_id=1, source_target_pairs={{0,32},{32,0},{1,33},{33,1},{2,34},{34,2},{3,35},{35,3},{4,36},{36... | collective-permute-start | bytes 1597448 | tf_op jit(solution)/shard_map/ppermute | solution.py:268
  69.0 11.3 %copy-start.10 = (bf16[1040,256]{1,0:T(8,128)(2,1)}, bf16[1040,256]{1,0:T(8,128)(2,1)S(1)}, u32[]{:S(2)}) copy-start(bf16[1040,256]{1,0:T(8,128)(2,1)S(1)} %collective-permute-done.8.rest_10_) | copy-start | bytes 1597444
  69.0 13.0 %collective-permute-start.9 = (bf16[1040,256]{1,0:T(8,128)(2,1)S(1)}, bf16[1040,256]{1,0:T(8,128)(2,1)}, u32[]{:S(2)}, u32[]{:S(2)}) collective-permute-start(bf16[1040,256]{1,0:T(8,128)(2,1)S(1)} %collective-permute-done.8.rest_10_), channel_id=1, source_target_pairs={{0,32},{32,0},{1,33},{33,1},{2,34},{34,2},{3,35},{35,3},{4,36},{36... | collective-permute-start | bytes 1597448 | tf_op jit(solution)/shard_map/ppermute | solution.py:268
  69.2 4.1 %collective-permute-start = (bf16[8,8,256]{2,1,0:T(8,128)(2,1)S(1)}, bf16[8,8,256]{2,1,0:T(8,128)(2,1)S(1)}, u32[]{:S(2)}, u32[]{:S(2)}) collective-permute-start(bf16[8,8,256]{2,1,0:T(8,128)(2,1)S(1)} %get-tuple-element.16), channel_id=1, source_target_pairs={{0,8},{8,16},{16,24},{24,0},{1,9},{9,17},{17,25},{25,1},{2,10},{10... | collective-permute-start | bytes 98312 | tf_op jit(solution)/shard_map/ppermute | solution.py:268
  73.2 4.3 %collective-permute-start.1 = (bf16[8,8,256]{2,1,0:T(8,128)(2,1)S(1)}, bf16[8,8,256]{2,1,0:T(8,128)(2,1)S(1)}, u32[]{:S(2)}, u32[]{:S(2)}) collective-permute-start(bf16[8,8,256]{2,1,0:T(8,128)(2,1)S(1)} %get-tuple-element.17), channel_id=1, source_target_pairs={{0,16},{8,24},{16,0},{24,8},{1,17},{9,25},{17,1},{25,9},{2,18},{10... | collective-permute-start | bytes 98312 | tf_op jit(solution)/shard_map/ppermute | solution.py:268
  77.5 2.8 %collective-permute-start.2 = (bf16[8,8,256]{2,1,0:T(8,128)(2,1)S(1)}, bf16[8,8,256]{2,1,0:T(8,128)(2,1)S(1)}, u32[]{:S(2)}, u32[]{:S(2)}) collective-permute-start(bf16[8,8,256]{2,1,0:T(8,128)(2,1)S(1)} %get-tuple-element.18), channel_id=1, source_target_pairs={{0,24},{8,0},{16,8},{24,16},{1,25},{9,1},{17,9},{25,17},{2,26},{10... | collective-permute-start | bytes 98312 | tf_op jit(solution)/shard_map/ppermute | solution.py:268
  80.3 1.0 copy-start.12
  90.5 42.9 %copy-start = (bf16[2,128,2048]{2,1,0:T(8,128)(2,1)S(1)}, bf16[2,128,2048]{2,1,0:T(8,128)(2,1)}, u32[]{:S(2)}) copy-start(bf16[2,128,2048]{2,1,0:T(8,128)(2,1)} %param.12) | copy-start | bytes 3145732
  90.6 42.9 %copy-start.5 = (bf16[256,512]{1,0:T(8,128)(2,1)S(1)}, bf16[256,512]{1,0:T(8,128)(2,1)}, u32[]{:S(2)}) copy-start(bf16[256,512]{1,0:T(8,128)(2,1)} %constant.17.clone.table_ref) | copy-start | bytes 786436
  (2 other events, 1.6 us)

commit v5 on v4

--- a/solution.py
+++ b/solution.py
@@ -81,38 +81,50 @@
     return dot(table_ref[:, :depth], operand) + dot(table_ref[:, depth:], operand)
 
 
-def cot_kernel(table_ref, cot_ref, out_ref, table, field, sems):
-    size = out_ref.shape[3]
+def cot_kernel(table_ref, cot_ref, *rest):
+    outs, table, field, sems = rest[:2], rest[2], rest[3], rest[4]
+    size = outs[0].shape[3]
     depth = table.shape[2] // 2
-    y, core = lax.axis_index("y"), lax.axis_index("core")
+    y, core, z = (lax.axis_index(name) for name in ("y", "core", "z"))
+    targets = [(z + y + 4 * i) & (Z - 1) for i in range(2)]
     copies = [
-        pltpu.make_async_copy(table_ref.at[:, core], table, sems.at[0]),
-        pltpu.make_async_copy(cot_ref.at[:, pl.ds(y * 2 * size, 2 * size)], field, sems.at[1]),
+        pltpu.make_async_copy(table_ref.at[targets[0], core], table.at[0], sems.at[0]),
+        pltpu.make_async_copy(table_ref.at[targets[1], core], table.at[1], sems.at[1]),
+        pltpu.make_async_copy(cot_ref, field, sems.at[2]),
     ]
     for copy in copies:
         copy.start()
-    half = Z * table.shape[1]
-    line = lax.broadcasted_iota(jnp.int32, (half, size), 0)
-    zero_mode = jnp.logical_and(jnp.logical_and(line < 8, (line & 1) == 0), core == 0)
-    factor = jnp.where(zero_mode, 1.0, 2.0).astype(F32)
+    lines = table.shape[1]
+    line = lax.broadcasted_iota(jnp.int32, (lines, size), 0)
+    first_even = jnp.logical_and(line < 8, (line & 1) == 0)
+    factors = []
+    for target in targets:
+        zero_mode = jnp.logical_and(first_even, jnp.logical_and(target == 0, core == 0))
+        factors.append(jnp.where(zero_mode, 1.0, 2.0).astype(F32))
     for copy in copies:
         copy.wait()
-    high = table[:, :, :depth].reshape(half, depth)
-    low = table[:, :, depth:].reshape(half, depth)
-    for k in range(2):
-        part = field[:, k * size : (k + 1) * size]
-        spectrum = ((dot(high, part) + dot(low, part)) * factor).astype(BF16).reshape(Z, 2, 8, size)
-        for m in range(2):
-            out_ref[:, 2 * m + k] = spectrum[:, m]
-
-
-def prologue_kernel(table_ref, act_ref, first_ref, second_ref, bias_ref, *rest):
+    rows = jnp.concatenate([table[0, :, :depth], table[1, :, :depth], table[0, :, depth:], table[1, :, depth:]], axis=0)
+    for n in range(2 * Y):
+        spectrum = dot(rows, field[:, n * size : (n + 1) * size])
+        spectrum = spectrum[: 2 * lines] + spectrum[2 * lines :]
+        for i in range(2):
+            tiles = (spectrum[i * lines : (i + 1) * lines] * factors[i]).astype(BF16)
+            for m in range(2):
+                outs[i][n // 2, 2 * m + n % 2] = tiles[m * 8 : (m + 1) * 8]
+
+
+def prologue_kernel(table_hbm, act_hbm, first_ref, second_ref, bias_ref, *rest):
     pieces = rest[:Y]
-    rows_ref, held, biases, sems, bias_sem = rest[Y:]
+    rows_ref, table_ref, act_ref, held, biases, sems, own_sems = rest[Y:]
     size = held.shape[2]
     y, odd = lax.axis_index("y"), lax.axis_index("x") & 1
-    bias_copy = pltpu.make_async_copy(bias_ref, biases, bias_sem)
-    bias_copy.start()
+    sources = (table_hbm, act_hbm, bias_ref)
+    own = [
+        pltpu.make_async_copy(source, target, own_sems.at[k])
+        for k, (source, target) in enumerate(zip(sources, (table_ref, act_ref, biases)))
+    ]
+    for copy in own:
+        copy.start()
     loads = []
     for d in range(Y):
         block = ((y + d) & (Y - 1)) * 2 + odd
@@ -130,9 +142,10 @@
         spectrum = twice(table_ref, act_ref[:, n * size : (n + 1) * size]).astype(BF16)
         rows_ref[:, :, :, n % 2, n // 2] = spectrum.reshape(Z, 2, 2, 8, size)
 
+    for copy in own:
+        copy.wait()
     for n in range(4):
         transform(n)
-    bias_copy.wait()
     for d in range(Y):
         block = ((y + d) & (Y - 1)) * 2 + odd
         bias = biases[0, :, pl.ds(block * size, size)]
@@ -154,10 +167,20 @@
         copy.wait()
 
 
-def turn_kernel(arrived_ref, *outs):
+def turn_y_kernel(*refs):
+    arrived, outs = refs[:2], refs[2:]
+    y = lax.axis_index("y")
+    for d in range(Y):
+        for i in range(2):
+            outs[d][i] = arrived[i][(y + d) & (Y - 1)]
+
+
+def turn_x_kernel(*refs):
+    arrived, outs = refs[:Y], refs[Y:]
     x = lax.axis_index("x")
     for e in range(X):
-        outs[e][...] = arrived_ref[:, (x + e) & (X - 1)]
+        for d in range(Y):
+            outs[e][d] = arrived[d][:, (x + e) & (X - 1)]
 
 
 def inverse_kernel(table_ref, spec_ref, cot_ref, out_ref, result, sems):
@@ -194,7 +217,9 @@
                 load(p, 2 * ((here // 2 - p // 2) % Y) + (p % 2 != here % 2)).start()
 
     for e in range(X):
-        found[:, (x - e) & (X - 1)] = cots[e][...]
+        for d in range(Y):
+            for i in range(2):
+                found[(z - ((y - d) & (Y - 1)) - 4 * i) & (Z - 1), (x - e) & (X - 1)] = cots[e][d, i]
     has_zero = jnp.logical_and(jnp.logical_and(core == 0, x < 2), z == 0)
     fold = jnp.where(has_zero, 1, 0)
 
@@ -271,36 +296,36 @@
     cot_rows = pl.pallas_call(
         cot_kernel,
         in_specs=[hbm] * 2,
-        out_specs=vmem,
-        out_shape=shaped(Z, X, tile, size),
+        out_specs=[vmem] * 2,
+        out_shape=[shaped(Y, X, tile, size)] * 2,
         scratch_shapes=[
-            pltpu.VMEM((Z, 2 * tile, 2 * count), BF16),
-            pltpu.VMEM((count, 2 * size), BF16),
-            pltpu.SemaphoreType.DMA((2,)),
+            pltpu.VMEM((2, 2 * tile, 2 * count), BF16),
+            pltpu.VMEM((count, channels), BF16),
+            pltpu.SemaphoreType.DMA((3,)),
         ],
         compiler_params=SMALL,
         name="cot_rows",
     )(*far(jnp.asarray(forward_rows.reshape(Z, 2, 2 * tile, -1)), flat_cot))
-    cot_blocks = lax.all_to_all(
-        cot_rows.reshape(Z, X * tile, size), "z", split_axis=0, concat_axis=0, tiled=True
-    ).reshape(cot_rows.shape)
+    arrived = []
+    for i in range(2):
+        route = [(y * Z + z, y * Z + (z + y + 4 * i) % Z) for y in range(Y) for z in range(Z)]
+        arrived.append(lax.ppermute(cot_rows[i], ("y", "z"), route))
     made = pl.pallas_call(
         prologue_kernel,
-        in_specs=[vmem] * 2 + [hbm] * 3,
+        in_specs=[hbm] * 5,
         out_specs=[hbm] * Y + [vmem],
         out_shape=[pltpu.HBM((4 * size + 16, size), BF16)] * Y + [shaped(*blocks)],
         scratch_shapes=[
+            pltpu.VMEM(forward_rows.shape, BF16),
+            pltpu.VMEM((count, channels), BF16),
             pltpu.VMEM((Y, 4 * size + 16, size), BF16),
             pltpu.VMEM(b_first.shape, F32),
             pltpu.SemaphoreType.DMA((Y, 5)),
-            pltpu.SemaphoreType.DMA(()),
+            pltpu.SemaphoreType.DMA((3,)),
         ],
         compiler_params=SMALL,
         name="prologue",
-    )(
-        *near(jnp.asarray(forward_rows), activations.reshape(count, channels)),
-        *far(w_first, w_second, b_first),
-    )
+    )(*far(jnp.asarray(forward_rows), activations.reshape(count, channels), w_first, w_second, b_first))
     pieces, act_rows = made[:Y], made[Y]
 
     weights = []
@@ -309,13 +334,22 @@
         weights += [piece, shifted(piece, "core", 1)]
     act_columns = exchange(act_rows)
     turned = pl.pallas_call(
-        turn_kernel,
-        in_specs=[vmem],
+        turn_y_kernel,
+        in_specs=[vmem] * 2,
+        out_specs=[vmem] * Y,
+        out_shape=[shaped(2, X, tile, size)] * Y,
+        compiler_params=SMALL,
+        name="turn_y",
+    )(*near(*arrived))
+    arrived = [turned[0]] + [shifted(turned[d], "y", d) for d in range(1, Y)]
+    turned = pl.pallas_call(
+        turn_x_kernel,
+        in_specs=[vmem] * Y,
         out_specs=[vmem] * X,
-        out_shape=[shaped(Z, tile, size)] * X,
-        compiler_params=SMALL,
-        name="turn",
-    )(*near(cot_blocks))
+        out_shape=[shaped(Y, 2, tile, size)] * X,
+        compiler_params=SMALL,
+        name="turn_x",
+    )(*near(*arrived))
     cots = [turned[0]] + [shifted(turned[e], "x", e) for e in range(1, X)]
 
     tables = [jnp.asarray(table) for table in (forward_columns, inverse_columns, folds)]

time: 136 us -> 158 us (1.16)
  starting transfers between devices: 32.7 us -> 41.6 us
  waiting for transfers between devices: 40.3 us -> 48 us
  blocking collectives: 42.9 us -> 48.7 us
    all_to_all x1 -> x0, starting transfers between devices: 9.01 us -> none  [body(): lax.all_to_all(cot_rows.reshape(Z, X * tile, size), 'z', split_axis=0, co...]
    ppermute x10 -> x13, waiting for transfers between devices: 37.8 us -> 46 us  [shifted(): lax.ppermute(value, axis, [(i, (i + distance) % size) for i in range(size)])]
    ppermute x10 -> x13, starting transfers between devices: 12.4 us -> 19.8 us  [shifted(): lax.ppermute(value, axis, [(i, (i + distance) % size) for i in range(size)])]
    ppermute x0 -> x2, starting transfers between devices: none -> 6.22 us  [body(): arrived.append(lax.ppermute(cot_rows[i], ('y', 'z'), route))]
    all_to_all x1, blocking collectives: 42.9 us -> 48.7 us  [exchange(): lax.all_to_all(flat, EVERYONE, split_axis=0, concat_axis=0, tiled=True)]
    all_to_all x1, starting transfers between devices: 11.3 us -> 15.7 us  [exchange(): lax.all_to_all(flat, EVERYONE, split_axis=0, concat_axis=0, tiled=True)]
    all_to_all x1 -> x0, waiting for transfers between devices: 2.56 us -> none  [body(): lax.all_to_all(cot_rows.reshape(Z, X * tile, size), 'z', split_axis=0, co...]
    ppermute x0 -> x2, waiting for transfers between devices: none -> 2 us  [body(): arrived.append(lax.ppermute(cot_rows[i], ('y', 'z'), route))]
  transfers between devices with their start and end apart: 12 -> 16, of which waited for: 6 -> 9; matrix products, arithmetic and copies ran while one was open for 0% -> 0% of each run, Pallas kernels for 3% -> 1%
where the time goes in v5:
time: 158 us; the launch traced here: 157 us
  blocking collectives  48.7 us (31%)
  waiting for transfers between devices  48 us (30%)
  starting transfers between devices  41.6 us (26%)
  Pallas kernels  16.7 us (11%)
  local copies, waits for them, and re-layouts  1.8 us (1%)
    all_to_all x1, blocking collectives, exchange(): lax.all_to_all(flat, EVERYONE, split_axis=0, concat_axis=0, tiled=True)  48.7 us
    ppermute x13, waiting for transfers between devices, shifted(): lax.ppermute(value, axis, [(i, (i + distance) % size) for i in range(size)])  46 us
    ppermute x13, starting transfers between devices, shifted(): lax.ppermute(value, axis, [(i, (i + distance) % size) for i in range(size)])  19.8 us
    all_to_all x1, starting transfers between devices, exchange(): lax.all_to_all(flat, EVERYONE, split_axis=0, concat_axis=0, tiled=True)  15.7 us
    pallas_call x1, Pallas kernels, body(): pl.pallas_call(chain_kernel, in_specs=[vmem] * (4 + X) + [hbm] * sections...  8.48 us
    ppermute x2, starting transfers between devices, body(): arrived.append(lax.ppermute(cot_rows[i], ('y', 'z'), route))  6.22 us
    pallas_call x1, Pallas kernels, body(): pl.pallas_call(prologue_kernel, in_specs=[hbm] * 5, out_specs=[hbm] * Y +...  4.98 us
  transfers between devices with their start and end apart: 16, of which 9 were waited for; matrix products, arithmetic and copies ran while one was open for 0% of the time, Pallas kernels for 1%

profile of v5, /device:TPU:1, one launch (start us, length us, event | category | flops | bytes accessed | tf_op | source)
XLA Modules:
  0.0 157.1 jit_solution(12633783064512664310)
XLA Ops:
  0.0 5.0 %prologue.1 = (bf16[1040,256]{1,0:T(8,128)(2,1)}, bf16[1040,256]{1,0:T(8,128)(2,1)}, bf16[1040,256]{1,0:T(8,128)(2,1)}, bf16[1040,256]{1,0:T(8,128)(2,1)}, bf16[8,2,2,2,4,8,256]{6,5,4,3,2,1,0:T(8,128)(2,1)}) custom-call(bf16[256,512]{1,0:T(8,128)(2,1)} %constant.13.clone.table_hbm, bf16[256,2048]{1,0:T(8,128)(2,1)} %bitcast.12, ...), custom_call_target="tpu_custom_call" | custom-call | tf_op jit(solution)/shard_map/prologue/pallas_call | solution.py:313
  5.0 15.7 %all-to-all-start = ((bf16[256,8,256]{2,1,0:T(8,128)(2,1)}), bf16[256,8,256]{2,1,0:T(8,128)(2,1)S(1)}, u32[]{:S(2)}, u32[]{:S(2)}) async-start(bf16[256,8,256]{2,1,0:T(8,128)(2,1)} %bitcast.1), calls=%async_computation | async-start | bytes 2097152 | tf_op jit(solution)/shard_map/all_to_all | solution.py:289
  20.7 1.4 collective-permute-start.9
  22.1 2.5 %collective-permute-start.11 = (bf16[1040,256]{1,0:T(8,128)(2,1)}, bf16[1040,256]{1,0:T(8,128)(2,1)S(1)}, u32[]{:S(2)}, u32[]{:S(2)}) collective-permute-start(bf16[1040,256]{1,0:T(8,128)(2,1)} %get-tuple-element.33), channel_id=1, source_target_pairs={{0,128},{64,192},{128,0},{192,64},{1,129},{65,193},{129,1},{193,65... | collective-permute-start | bytes 1597448 | tf_op jit(solution)/shard_map/ppermute | solution.py:293
  24.6 1.1 collective-permute-start.13
  25.7 1.2 collective-permute-start.8
  26.9 15.3 %collective-permute-done.9.rest_6_ = bf16[1040,256]{1,0:T(8,128)(2,1)S(1)} collective-permute-done((bf16[1040,256]{1,0:T(8,128)(2,1)}, bf16[1040,256]{1,0:T(8,128)(2,1)S(1)}, u32[]{:S(2)}, u32[]{:S(2)}) %collective-permute-start.9) | collective-permute-done | bytes 532512 | tf_op jit(solution)/shard_map/ppermute | solution.py:293
  42.2 3.1 %collective-permute-start.10 = (bf16[1040,256]{1,0:T(8,128)(2,1)S(1)}, bf16[1040,256]{1,0:T(8,128)(2,1)S(1)}, u32[]{:S(2)}, u32[]{:S(2)}) collective-permute-start(bf16[1040,256]{1,0:T(8,128)(2,1)S(1)} %collective-permute-done.9.rest_6_), channel_id=1, source_target_pairs={{0,32},{32,0},{1,33},{33,1},{2,34},{34,2},{3,35},{35,3},{4,36},{36... | collective-permute-start | bytes 1597448 | tf_op jit(solution)/shard_map/ppermute | solution.py:293
  45.3 13.4 %collective-permute-done.11.rest_8_ = bf16[1040,256]{1,0:T(8,128)(2,1)S(1)} collective-permute-done((bf16[1040,256]{1,0:T(8,128)(2,1)}, bf16[1040,256]{1,0:T(8,128)(2,1)S(1)}, u32[]{:S(2)}, u32[]{:S(2)}) %collective-permute-start.11) | collective-permute-done | bytes 532512 | tf_op jit(solution)/shard_map/ppermute | solution.py:293
  58.7 0.9 collective-permute-start.12
  59.7 1.7 %cot_rows.1 = (bf16[4,4,8,256]{3,2,1,0:T(8,128)(2,1)S(1)}, bf16[4,4,8,256]{3,2,1,0:T(8,128)(2,1)S(1)}) custom-call(bf16[8,2,16,512]{3,2,1,0:T(8,128)(2,1)} %constant.12.clone.table_ref, bf16[256,2048]{1,0:T(8,128)(2,1)} %bitcast.9), custom_call_target="tpu_custom_call" | custom-call | tf_op jit(solution)/shard_map/cot_rows/pallas_call | solution.py:296
  62.1 5.6 %collective-permute-start.1 = (bf16[4,4,8,256]{3,2,1,0:T(8,128)(2,1)S(1)}, bf16[4,4,8,256]{3,2,1,0:T(8,128)(2,1)S(1)}, u32[]{:S(2)}, u32[]{:S(2)}) collective-permute-start(bf16[4,4,8,256]{3,2,1,0:T(8,128)(2,1)S(1)} %get-tuple-element.22), channel_id=1, source_target_pairs={{0,4},{1,5},{2,6},{3,7},{4,0},{5,1},{6,2},{7,3},{64,69},{65,70},{6... | collective-permute-start | bytes 196616 | tf_op jit(solution)/shard_map/ppermute | solution.py:312
  67.7 2.0 %collective-permute-done.1.refs_1_ = bf16[4,4,8,256]{3,2,1,0:T(8,128)(2,1)S(1)} collective-permute-done((bf16[4,4,8,256]{3,2,1,0:T(8,128)(2,1)S(1)}, bf16[4,4,8,256]{3,2,1,0:T(8,128)(2,1)S(1)}, u32[]{:S(2)}, u32[]{:S(2)}) %collective-permute-start.1) | collective-permute-done | bytes 65568 | tf_op jit(solution)/shard_map/ppermute | solution.py:312
  69.7 4.7 %collective-permute-start.2 = (bf16[2,4,8,256]{3,2,1,0:T(8,128)(2,1)S(1)}, bf16[2,4,8,256]{3,2,1,0:T(8,128)(2,1)S(1)}, u32[]{:S(2)}, u32[]{:S(2)}) collective-permute-start(bf16[2,4,8,256]{3,2,1,0:T(8,128)(2,1)S(1)} %get-tuple-element.24), channel_id=1, source_target_pairs={{0,64},{64,128},{128,192},{192,0},{1,65},{65,129},{129,193},{193,1... | collective-permute-start | bytes 98312 | tf_op jit(solution)/shard_map/ppermute | solution.py:293
  74.4 3.6 %collective-permute-done.2.refs_1_ = bf16[2,4,8,256]{3,2,1,0:T(8,128)(2,1)S(1)} collective-permute-done((bf16[2,4,8,256]{3,2,1,0:T(8,128)(2,1)S(1)}, bf16[2,4,8,256]{3,2,1,0:T(8,128)(2,1)S(1)}, u32[]{:S(2)}, u32[]{:S(2)}) %collective-permute-start.2) | collective-permute-done | bytes 32800 | tf_op jit(solution)/shard_map/ppermute | solution.py:293
  78.9 3.4 %collective-permute-done.3.refs_2_ = bf16[2,4,8,256]{3,2,1,0:T(8,128)(2,1)S(1)} collective-permute-done((bf16[2,4,8,256]{3,2,1,0:T(8,128)(2,1)S(1)}, bf16[2,4,8,256]{3,2,1,0:T(8,128)(2,1)S(1)}, u32[]{:S(2)}, u32[]{:S(2)}) %collective-permute-start.3) | collective-permute-done | bytes 32800 | tf_op jit(solution)/shard_map/ppermute | solution.py:293
  82.2 1.5 collective-permute-start.4
  83.7 1.6 %collective-permute-done.4.refs_3_ = bf16[2,4,8,256]{3,2,1,0:T(8,128)(2,1)S(1)} collective-permute-done((bf16[2,4,8,256]{3,2,1,0:T(8,128)(2,1)S(1)}, bf16[2,4,8,256]{3,2,1,0:T(8,128)(2,1)S(1)}, u32[]{:S(2)}, u32[]{:S(2)}) %collective-permute-start.4) | collective-permute-done | bytes 32800 | tf_op jit(solution)/shard_map/ppermute | solution.py:293
  86.2 3.1 %collective-permute-done.5.rest_1_ = bf16[4,2,8,256]{3,2,1,0:T(8,128)(2,1)S(1)} collective-permute-done((bf16[4,2,8,256]{3,2,1,0:T(8,128)(2,1)S(1)}, bf16[4,2,8,256]{3,2,1,0:T(8,128)(2,1)S(1)}, u32[]{:S(2)}, u32[]{:S(2)}) %collective-permute-start.5) | collective-permute-done | bytes 32800 | tf_op jit(solution)/shard_map/ppermute | solution.py:293
  90.2 3.4 %collective-permute-done.6.rest_2_ = bf16[4,2,8,256]{3,2,1,0:T(8,128)(2,1)S(1)} collective-permute-done((bf16[4,2,8,256]{3,2,1,0:T(8,128)(2,1)S(1)}, bf16[4,2,8,256]{3,2,1,0:T(8,128)(2,1)S(1)}, u32[]{:S(2)}, u32[]{:S(2)}) %collective-permute-start.6) | collective-permute-done | bytes 32800 | tf_op jit(solution)/shard_map/ppermute | solution.py:293
  94.3 2.1 %collective-permute-done.7.rest_3_ = bf16[4,2,8,256]{3,2,1,0:T(8,128)(2,1)S(1)} collective-permute-done((bf16[4,2,8,256]{3,2,1,0:T(8,128)(2,1)S(1)}, bf16[4,2,8,256]{3,2,1,0:T(8,128)(2,1)S(1)}, u32[]{:S(2)}, u32[]{:S(2)}) %collective-permute-start.7) | collective-permute-done | bytes 32800 | tf_op jit(solution)/shard_map/ppermute | solution.py:293
  98.2 8.5 %chain.1 = bf16[8,2,2,2,4,8,256]{6,5,4,3,2,1,0:T(8,128)(2,1)S(1)} custom-call(bf16[8,2,2,2,4,8,256]{6,5,4,3,2,1,0:T(8,128)(2,1)S(1)} %bitcast.7, bf16[256,512]{1,0:T(8,128)(2,1)S(1)} %copy-done.3, bf16[256,512]{1,0:T(8,128)(2,1)S(1)} %copy-done.2, bf16[2,256,256]{2,1,0:T(8,128)(2,1)S(1)} %copy-done.1, bf16[4,2,8,256]{3,2,1,0:T(8,128)(2,1)S(1)} %get-tuple-element.27.rest_0_, ...), custom_call_target="tpu_custom_call" | custom-call | tf_op jit(solution)/shard_map/chain/pallas_call | solution.py:356
  106.7 48.7 %all_to_all.10 = bf16[256,8,256]{2,1,0:T(8,128)(2,1)S(1)} all-to-all(bf16[256,8,256]{2,1,0:T(8,128)(2,1)S(1)} %bitcast.8), channel_id=1, replica_groups=mesh['y'=4,'core'=2,'x'=4,'z'=8] {'z','core','x','y'}, dimensions={0} | all-to-all | bytes 2097152 | tf_op jit(solution)/shard_map/all_to_all | solution.py:289
  155.4 1.5 inverse_rows.1
  (39 shorter events, 5.9 us)
Async XLA Ops:
  5.0 93.2 %copy-start.1 = (bf16[2,256,256]{2,1,0:T(8,128)(2,1)S(1)}, bf16[2,256,256]{2,1,0:T(8,128)(2,1)}, u32[]{:S(2)}) copy-start(bf16[2,256,256]{2,1,0:T(8,128)(2,1)} %constant.16.clone.fold_ref) | copy-start | bytes 786436
  5.0 93.2 %copy-start.2 = (bf16[256,512]{1,0:T(8,128)(2,1)S(1)}, bf16[256,512]{1,0:T(8,128)(2,1)}, u32[]{:S(2)}) copy-start(bf16[256,512]{1,0:T(8,128)(2,1)} %constant.15.clone.inv_ref) | copy-start | bytes 786436
  5.0 93.2 %copy-start.3 = (bf16[256,512]{1,0:T(8,128)(2,1)S(1)}, bf16[256,512]{1,0:T(8,128)(2,1)}, u32[]{:S(2)}) copy-start(bf16[256,512]{1,0:T(8,128)(2,1)} %constant.14.clone.col_ref) | copy-start | bytes 786436
  5.0 93.2 %all-to-all-start = ((bf16[256,8,256]{2,1,0:T(8,128)(2,1)}), bf16[256,8,256]{2,1,0:T(8,128)(2,1)S(1)}, u32[]{:S(2)}, u32[]{:S(2)}) async-start(bf16[256,8,256]{2,1,0:T(8,128)(2,1)} %bitcast.1), calls=%async_computation | async-start | bytes 2097152 | tf_op jit(solution)/shard_map/all_to_all | solution.py:289
  20.7 21.5 %collective-permute-start.9 = (bf16[1040,256]{1,0:T(8,128)(2,1)}, bf16[1040,256]{1,0:T(8,128)(2,1)S(1)}, u32[]{:S(2)}, u32[]{:S(2)}) collective-permute-start(bf16[1040,256]{1,0:T(8,128)(2,1)} %get-tuple-element.32), channel_id=1, source_target_pairs={{0,64},{64,128},{128,192},{192,0},{1,65},{65,129},{129,193},{193,1... | collective-permute-start | bytes 1597448 | tf_op jit(solution)/shard_map/ppermute | solution.py:293
  22.1 36.6 %collective-permute-start.11 = (bf16[1040,256]{1,0:T(8,128)(2,1)}, bf16[1040,256]{1,0:T(8,128)(2,1)S(1)}, u32[]{:S(2)}, u32[]{:S(2)}) collective-permute-start(bf16[1040,256]{1,0:T(8,128)(2,1)} %get-tuple-element.33), channel_id=1, source_target_pairs={{0,128},{64,192},{128,0},{192,64},{1,129},{65,193},{129,1},{193,65... | collective-permute-start | bytes 1597448 | tf_op jit(solution)/shard_map/ppermute | solution.py:293
  24.6 35.1 %collective-permute-start.13 = (bf16[1040,256]{1,0:T(8,128)(2,1)}, bf16[1040,256]{1,0:T(8,128)(2,1)S(1)}, u32[]{:S(2)}, u32[]{:S(2)}) collective-permute-start(bf16[1040,256]{1,0:T(8,128)(2,1)} %get-tuple-element.34), channel_id=1, source_target_pairs={{0,192},{64,0},{128,64},{192,128},{1,193},{65,1},{129,65},{193,129... | collective-permute-start | bytes 1597448 | tf_op jit(solution)/shard_map/ppermute | solution.py:293
  25.7 70.7 %collective-permute-start.8 = (bf16[1040,256]{1,0:T(8,128)(2,1)S(1)}, bf16[1040,256]{1,0:T(8,128)(2,1)S(1)}, u32[]{:S(2)}, u32[]{:S(2)}) collective-permute-start(bf16[1040,256]{1,0:T(8,128)(2,1)S(1)} %copy-done.5), channel_id=1, source_target_pairs={{0,32},{32,0},{1,33},{33,1},{2,34},{34,2},{3,35},{35,3},{4,36},{36... | collective-permute-start | bytes 1597448 | tf_op jit(solution)/shard_map/ppermute | solution.py:293
  42.2 56.0 %copy-start.6 = (bf16[1040,256]{1,0:T(8,128)(2,1)}, bf16[1040,256]{1,0:T(8,128)(2,1)S(1)}, u32[]{:S(2)}) copy-start(bf16[1040,256]{1,0:T(8,128)(2,1)S(1)} %collective-permute-done.9.rest_6_) | copy-start | bytes 1597444
  42.2 54.2 %collective-permute-start.10 = (bf16[1040,256]{1,0:T(8,128)(2,1)S(1)}, bf16[1040,256]{1,0:T(8,128)(2,1)S(1)}, u32[]{:S(2)}, u32[]{:S(2)}) collective-permute-start(bf16[1040,256]{1,0:T(8,128)(2,1)S(1)} %collective-permute-done.9.rest_6_), channel_id=1, source_target_pairs={{0,32},{32,0},{1,33},{33,1},{2,34},{34,2},{3,35},{35,3},{4,36},{36... | collective-permute-start | bytes 1597448 | tf_op jit(solution)/shard_map/ppermute | solution.py:293
  58.7 37.7 %copy-start.7 = (bf16[1040,256]{1,0:T(8,128)(2,1)}, bf16[1040,256]{1,0:T(8,128)(2,1)S(1)}, u32[]{:S(2)}) copy-start(bf16[1040,256]{1,0:T(8,128)(2,1)S(1)} %collective-permute-done.11.rest_8_) | copy-start | bytes 1597444
  58.7 37.7 %collective-permute-start.12 = (bf16[1040,256]{1,0:T(8,128)(2,1)S(1)}, bf16[1040,256]{1,0:T(8,128)(2,1)S(1)}, u32[]{:S(2)}, u32[]{:S(2)}) collective-permute-start(bf16[1040,256]{1,0:T(8,128)(2,1)S(1)} %collective-permute-done.11.rest_8_), channel_id=1, source_target_pairs={{0,32},{32,0},{1,33},{33,1},{2,34},{34,2},{3,35},{35,3},{4,36},{36... | collective-permute-start | bytes 1597448 | tf_op jit(solution)/shard_map/ppermute | solution.py:293
  59.6 36.8 %copy-start.8 = (bf16[1040,256]{1,0:T(8,128)(2,1)}, bf16[1040,256]{1,0:T(8,128)(2,1)S(1)}, u32[]{:S(2)}) copy-start(bf16[1040,256]{1,0:T(8,128)(2,1)S(1)} %collective-permute-done.13.rest_10_) | copy-start | bytes 1597444
  59.6 38.6 %collective-permute-start.14 = (bf16[1040,256]{1,0:T(8,128)(2,1)S(1)}, bf16[1040,256]{1,0:T(8,128)(2,1)}, u32[]{:S(2)}, u32[]{:S(2)}) collective-permute-start(bf16[1040,256]{1,0:T(8,128)(2,1)S(1)} %collective-permute-done.13.rest_10_), channel_id=1, source_target_pairs={{0,32},{32,0},{1,33},{33,1},{2,34},{34,2},{3,35},{35,3},{4,36},{36... | collective-permute-start | bytes 1597448 | tf_op jit(solution)/shard_map/ppermute | solution.py:293
  61.4 0.7 collective-permute-start
  62.1 7.6 %collective-permute-start.1 = (bf16[4,4,8,256]{3,2,1,0:T(8,128)(2,1)S(1)}, bf16[4,4,8,256]{3,2,1,0:T(8,128)(2,1)S(1)}, u32[]{:S(2)}, u32[]{:S(2)}) collective-permute-start(bf16[4,4,8,256]{3,2,1,0:T(8,128)(2,1)S(1)} %get-tuple-element.22), channel_id=1, source_target_pairs={{0,4},{1,5},{2,6},{3,7},{4,0},{5,1},{6,2},{7,3},{64,69},{65,70},{6... | collective-permute-start | bytes 196616 | tf_op jit(solution)/shard_map/ppermute | solution.py:312
  69.7 8.3 %collective-permute-start.2 = (bf16[2,4,8,256]{3,2,1,0:T(8,128)(2,1)S(1)}, bf16[2,4,8,256]{3,2,1,0:T(8,128)(2,1)S(1)}, u32[]{:S(2)}, u32[]{:S(2)}) collective-permute-start(bf16[2,4,8,256]{3,2,1,0:T(8,128)(2,1)S(1)} %get-tuple-element.24), channel_id=1, source_target_pairs={{0,64},{64,128},{128,192},{192,0},{1,65},{65,129},{129,193},{193,1... | collective-permute-start | bytes 98312 | tf_op jit(solution)/shard_map/ppermute | solution.py:293
  78.0 4.3 %collective-permute-start.3 = (bf16[2,4,8,256]{3,2,1,0:T(8,128)(2,1)S(1)}, bf16[2,4,8,256]{3,2,1,0:T(8,128)(2,1)S(1)}, u32[]{:S(2)}, u32[]{:S(2)}) collective-permute-start(bf16[2,4,8,256]{3,2,1,0:T(8,128)(2,1)S(1)} %get-tuple-element.25), channel_id=1, source_target_pairs={{0,128},{64,192},{128,0},{192,64},{1,129},{65,193},{129,1},{193,65... | collective-permute-start | bytes 98312 | tf_op jit(solution)/shard_map/ppermute | solution.py:293
  82.2 3.1 %collective-permute-start.4 = (bf16[2,4,8,256]{3,2,1,0:T(8,128)(2,1)S(1)}, bf16[2,4,8,256]{3,2,1,0:T(8,128)(2,1)S(1)}, u32[]{:S(2)}, u32[]{:S(2)}) collective-permute-start(bf16[2,4,8,256]{3,2,1,0:T(8,128)(2,1)S(1)} %get-tuple-element.26), channel_id=1, source_target_pairs={{0,192},{64,0},{128,64},{192,128},{1,193},{65,1},{129,65},{193,129... | collective-permute-start | bytes 98312 | tf_op jit(solution)/shard_map/ppermute | solution.py:293
  85.3 4.1 %collective-permute-start.5 = (bf16[4,2,8,256]{3,2,1,0:T(8,128)(2,1)S(1)}, bf16[4,2,8,256]{3,2,1,0:T(8,128)(2,1)S(1)}, u32[]{:S(2)}, u32[]{:S(2)}) collective-permute-start(bf16[4,2,8,256]{3,2,1,0:T(8,128)(2,1)S(1)} %get-tuple-element.28), channel_id=1, source_target_pairs={{0,8},{8,16},{16,24},{24,0},{1,9},{9,17},{17,25},{25,1},{2,10},{10... | collective-permute-start | bytes 98312 | tf_op jit(solution)/shard_map/ppermute | solution.py:293
  89.4 4.3 %collective-permute-start.6 = (bf16[4,2,8,256]{3,2,1,0:T(8,128)(2,1)S(1)}, bf16[4,2,8,256]{3,2,1,0:T(8,128)(2,1)S(1)}, u32[]{:S(2)}, u32[]{:S(2)}) collective-permute-start(bf16[4,2,8,256]{3,2,1,0:T(8,128)(2,1)S(1)} %get-tuple-element.29), channel_id=1, source_target_pairs={{0,16},{8,24},{16,0},{24,8},{1,17},{9,25},{17,1},{25,9},{2,18},{10... | collective-permute-start | bytes 98312 | tf_op jit(solution)/shard_map/ppermute | solution.py:293
  93.6 2.8 %collective-permute-start.7 = (bf16[4,2,8,256]{3,2,1,0:T(8,128)(2,1)S(1)}, bf16[4,2,8,256]{3,2,1,0:T(8,128)(2,1)S(1)}, u32[]{:S(2)}, u32[]{:S(2)}) collective-permute-start(bf16[4,2,8,256]{3,2,1,0:T(8,128)(2,1)S(1)} %get-tuple-element.30), channel_id=1, source_target_pairs={{0,24},{8,0},{16,8},{24,16},{1,25},{9,1},{17,9},{25,17},{2,26},{10... | collective-permute-start | bytes 98312 | tf_op jit(solution)/shard_map/ppermute | solution.py:293
  106.7 48.7 %copy-start = (bf16[2,128,2048]{2,1,0:T(8,128)(2,1)S(1)}, bf16[2,128,2048]{2,1,0:T(8,128)(2,1)}, u32[]{:S(2)}) copy-start(bf16[2,128,2048]{2,1,0:T(8,128)(2,1)} %param.12) | copy-start | bytes 3145732
  106.7 48.7 %copy-start.4 = (bf16[256,512]{1,0:T(8,128)(2,1)S(1)}, bf16[256,512]{1,0:T(8,128)(2,1)}, u32[]{:S(2)}) copy-start(bf16[256,512]{1,0:T(8,128)(2,1)} %constant.17.clone.table_ref) | copy-start | bytes 786436
  (4 other events, 23.3 us)

commit v6 on v5

--- a/solution.py
+++ b/solution.py
@@ -81,29 +81,51 @@
     return dot(table_ref[:, :depth], operand) + dot(table_ref[:, depth:], operand)
 
 
-def cot_kernel(table_ref, cot_ref, *rest):
-    outs, table, field, sems = rest[:2], rest[2], rest[3], rest[4]
-    size = outs[0].shape[3]
-    depth = table.shape[2] // 2
-    y, core, z = (lax.axis_index(name) for name in ("y", "core", "z"))
+def first_kernel(table_hbm, act_hbm, cot_hbm, first_ref, second_ref, bias_hbm, *rest):
+    pieces, outs, rows_ref = rest[:Y], rest[Y : Y + 2], rest[Y + 2]
+    part, field, table_ref, act_ref, held, biases, sems, own_sems = rest[Y + 3 :]
+    size = held.shape[2]
+    y, core, z, odd = (*(lax.axis_index(name) for name in ("y", "core", "z")), lax.axis_index("x") & 1)
     targets = [(z + y + 4 * i) & (Z - 1) for i in range(2)]
-    copies = [
-        pltpu.make_async_copy(table_ref.at[targets[0], core], table.at[0], sems.at[0]),
-        pltpu.make_async_copy(table_ref.at[targets[1], core], table.at[1], sems.at[1]),
-        pltpu.make_async_copy(cot_ref, field, sems.at[2]),
+    lines = part.shape[1]
+    pairs = [
+        (table_hbm.at[pl.ds((targets[0] * 2 + core) * lines, lines)], part.at[0]),
+        (table_hbm.at[pl.ds((targets[1] * 2 + core) * lines, lines)], part.at[1]),
+        (cot_hbm, field),
+        (table_hbm, table_ref),
+        (act_hbm, act_ref),
+        (bias_hbm, biases),
     ]
-    for copy in copies:
+    own = []
+    for k, (source, target) in enumerate(pairs):
+        copy = pltpu.make_async_copy(source, target, own_sems.at[k])
         copy.start()
-    lines = table.shape[1]
+        own.append(copy)
+        if k != 2:
+            continue
+        loads = []
+        for d in range(Y):
+            block = ((y + d) & (Y - 1)) * 2 + odd
+            for i in range(2):
+                for j, ref in enumerate((first_ref, second_ref)):
+                    copy = pltpu.make_async_copy(
+                        ref.at[0, i, block],
+                        held.at[d, pl.ds((2 * j + i) * size, size)],
+                        sems.at[d, 2 * j + i],
+                    )
+                    copy.start()
+                    loads.append(copy)
+
+    depth = table_ref.shape[1] // 2
     line = lax.broadcasted_iota(jnp.int32, (lines, size), 0)
     first_even = jnp.logical_and(line < 8, (line & 1) == 0)
     factors = []
     for target in targets:
         zero_mode = jnp.logical_and(first_even, jnp.logical_and(target == 0, core == 0))
         factors.append(jnp.where(zero_mode, 1.0, 2.0).astype(F32))
-    for copy in copies:
-        copy.wait()
-    rows = jnp.concatenate([table[0, :, :depth], table[1, :, :depth], table[0, :, depth:], table[1, :, depth:]], axis=0)
+    for copy in own[:3]:
+        copy.wait()
+    rows = jnp.concatenate([part[0, :, :depth], part[1, :, :depth], part[0, :, depth:], part[1, :, depth:]], axis=0)
     for n in range(2 * Y):
         spectrum = dot(rows, field[:, n * size : (n + 1) * size])
         spectrum = spectrum[: 2 * lines] + spectrum[2 * lines :]
@@ -112,40 +134,8 @@
             for m in range(2):
                 outs[i][n // 2, 2 * m + n % 2] = tiles[m * 8 : (m + 1) * 8]
 
-
-def prologue_kernel(table_hbm, act_hbm, first_ref, second_ref, bias_ref, *rest):
-    pieces = rest[:Y]
-    rows_ref, table_ref, act_ref, held, biases, sems, own_sems = rest[Y:]
-    size = held.shape[2]
-    y, odd = lax.axis_index("y"), lax.axis_index("x") & 1
-    sources = (table_hbm, act_hbm, bias_ref)
-    own = [
-        pltpu.make_async_copy(source, target, own_sems.at[k])
-        for k, (source, target) in enumerate(zip(sources, (table_ref, act_ref, biases)))
-    ]
-    for copy in own:
-        copy.start()
-    loads = []
-    for d in range(Y):
-        block = ((y + d) & (Y - 1)) * 2 + odd
-        for i in range(2):
-            for j, ref in enumerate((first_ref, second_ref)):
-                copy = pltpu.make_async_copy(
-                    ref.at[0, i, block],
-                    held.at[d, pl.ds((2 * j + i) * size, size)],
-                    sems.at[d, 2 * j + i],
-                )
-                copy.start()
-                loads.append(copy)
-
-    def transform(n):
-        spectrum = twice(table_ref, act_ref[:, n * size : (n + 1) * size]).astype(BF16)
-        rows_ref[:, :, :, n % 2, n // 2] = spectrum.reshape(Z, 2, 2, 8, size)
-
-    for copy in own:
-        copy.wait()
-    for n in range(4):
-        transform(n)
+    for copy in own[3:]:
+        copy.wait()
     for d in range(Y):
         block = ((y + d) & (Y - 1)) * 2 + odd
         bias = biases[0, :, pl.ds(block * size, size)]
@@ -161,8 +151,9 @@
         copy = pltpu.make_async_copy(held.at[d], pieces[d], sems.at[d, 4])
         copy.start()
         stores.append(copy)
-    for n in range(4, 2 * Y):
-        transform(n)
+    for n in range(2 * Y):
+        spectrum = twice(table_ref, act_ref[:, n * size : (n + 1) * size]).astype(BF16)
+        rows_ref[:, :, :, n % 2, n // 2] = spectrum.reshape(Z, 2, 2, 8, size)
     for copy in stores:
         copy.wait()
 
@@ -293,41 +284,40 @@
         return lax.ppermute(value, axis, [(i, (i + distance) % size) for i in range(size)])
 
     flat_cot = cotangent.reshape(count, channels)
-    cot_rows = pl.pallas_call(
-        cot_kernel,
-        in_specs=[hbm] * 2,
-        out_specs=[vmem] * 2,
-        out_shape=[shaped(Y, X, tile, size)] * 2,
+    made = pl.pallas_call(
+        first_kernel,
+        in_specs=[hbm] * 6,
+        out_specs=[hbm] * Y + [vmem] * 3,
+        out_shape=[pltpu.HBM((4 * size + 16, size), BF16)] * Y
+        + [shaped(Y, X, tile, size)] * 2
+        + [shaped(*blocks)],
         scratch_shapes=[
             pltpu.VMEM((2, 2 * tile, 2 * count), BF16),
             pltpu.VMEM((count, channels), BF16),
-            pltpu.SemaphoreType.DMA((3,)),
-        ],
-        compiler_params=SMALL,
-        name="cot_rows",
-    )(*far(jnp.asarray(forward_rows.reshape(Z, 2, 2 * tile, -1)), flat_cot))
-    arrived = []
-    for i in range(2):
-        route = [(y * Z + z, y * Z + (z + y + 4 * i) % Z) for y in range(Y) for z in range(Z)]
-        arrived.append(lax.ppermute(cot_rows[i], ("y", "z"), route))
-    made = pl.pallas_call(
-        prologue_kernel,
-        in_specs=[hbm] * 5,
-        out_specs=[hbm] * Y + [vmem],
-        out_shape=[pltpu.HBM((4 * size + 16, size), BF16)] * Y + [shaped(*blocks)],
-        scratch_shapes=[
             pltpu.VMEM(forward_rows.shape, BF16),
             pltpu.VMEM((count, channels), BF16),
             pltpu.VMEM((Y, 4 * size + 16, size), BF16),
             pltpu.VMEM(b_first.shape, F32),
             pltpu.SemaphoreType.DMA((Y, 5)),
-            pltpu.SemaphoreType.DMA((3,)),
+            pltpu.SemaphoreType.DMA((6,)),
         ],
         compiler_params=SMALL,
-        name="prologue",
-    )(*far(jnp.asarray(forward_rows), activations.reshape(count, channels), w_first, w_second, b_first))
-    pieces, act_rows = made[:Y], made[Y]
-
+        name="first",
+    )(
+        *far(
+            jnp.asarray(forward_rows),
+            activations.reshape(count, channels),
+            flat_cot,
+            w_first,
+            w_second,
+            b_first,
+        )
+    )
+    pieces, cot_rows, act_rows = made[:Y], made[Y : Y + 2], made[Y + 2]
+    arrived = []
+    for i in range(2):
+        route = [(y * Z + z, y * Z + (z + y + 4 * i) % Z) for y in range(Y) for z in range(Z)]
+        arrived.append(lax.ppermute(cot_rows[i], ("y", "z"), route))
     weights = []
     for d in range(Y):
         piece = shifted(pieces[d], "y", d) if d else pieces[0]

time: 158 us -> 156 us (0.987)
  Pallas kernels: 16.7 us -> 15 us
    pallas_call x2 -> x1, Pallas kernels: 6.67 us -> 4.95 us  [body(): pl.pallas_call(first_kernel, in_specs=[hbm] * 6, out_specs=[hbm] * Y + [v...]
  transfers between devices with their start and end apart: 16 -> 16, of which waited for: 9 -> 9; matrix products, arithmetic and copies ran while one was open for 0% -> 0% of each run, Pallas kernels for 1% -> 0%
where the time goes in v6:
time: 156 us; the launch traced here: 155 us
  blocking collectives  48.7 us (31%)
  waiting for transfers between devices  47.5 us (30%)
  starting transfers between devices  42.2 us (27%)
  Pallas kernels  15 us (10%)
  local copies, waits for them, and re-layouts  1.79 us (1%)
    all_to_all x1, blocking collectives, exchange(): lax.all_to_all(flat, EVERYONE, split_axis=0, concat_axis=0, tiled=True)  48.7 us
    ppermute x13, waiting for transfers between devices, shifted(): lax.ppermute(value, axis, [(i, (i + distance) % size) for i in range(size)])  45.8 us
    ppermute x13, starting transfers between devices, shifted(): lax.ppermute(value, axis, [(i, (i + distance) % size) for i in range(size)])  20.3 us
    all_to_all x1, starting transfers between devices, exchange(): lax.all_to_all(flat, EVERYONE, split_axis=0, concat_axis=0, tiled=True)  15.7 us
    pallas_call x1, Pallas kernels, body(): pl.pallas_call(chain_kernel, in_specs=[vmem] * (4 + X) + [hbm] * sections...  8.47 us
    ppermute x2, starting transfers between devices, body(): arrived.append(lax.ppermute(cot_rows[i], ('y', 'z'), route))  6.21 us
    pallas_call x1, Pallas kernels, body(): pl.pallas_call(first_kernel, in_specs=[hbm] * 6, out_specs=[hbm] * Y + [v...  4.95 us
  transfers between devices with their start and end apart: 16, of which 9 were waited for; matrix products, arithmetic and copies ran while one was open for 0% of the time, Pallas kernels for 0%

profile of v6, /device:TPU:1, one launch (start us, length us, event | category | flops | bytes accessed | tf_op | source)
XLA Modules:
  0.0 155.5 jit_solution(10916457362062338150)
XLA Ops:
  0.0 5.0 %first.1 = (bf16[1040,256]{1,0:T(8,128)(2,1)}, bf16[1040,256]{1,0:T(8,128)(2,1)}, bf16[1040,256]{1,0:T(8,128)(2,1)}, bf16[1040,256]{1,0:T(8,128)(2,1)}, bf16[4,4...) custom-call(bf16[256,512]{1,0:T(8,128)(2,1)} %constant.10.clone.table_hbm,, ...), custom_call_target="tpu_custom_call" | custom-call | tf_op jit(solution)/shard_map/first/pallas_call | solution.py:287
  5.0 15.7 %all-to-all-start = ((bf16[256,8,256]{2,1,0:T(8,128)(2,1)}), bf16[256,8,256]{2,1,0:T(8,128)(2,1)S(1)}, u32[]{:S(2)}, u32[]{:S(2)}) async-start(bf16[256,8,256]{2,1,0:T(8,128)(2,1)} %bitcast.2), calls=%async_computation | async-start | bytes 2097152 | tf_op jit(solution)/shard_map/all_to_all | solution.py:280
  20.7 1.4 collective-permute-start.9
  22.1 2.5 %collective-permute-start.11 = (bf16[1040,256]{1,0:T(8,128)(2,1)}, bf16[1040,256]{1,0:T(8,128)(2,1)S(1)}, u32[]{:S(2)}, u32[]{:S(2)}) collective-permute-start(bf16[1040,256]{1,0:T(8,128)(2,1)} %get-tuple-element.33), channel_id=1, source_target_pairs={{0,128},{64,192},{128,0},{192,64},{1,129},{65,193},{129,1},{193,65... | collective-permute-start | bytes 1597448 | tf_op jit(solution)/shard_map/ppermute | solution.py:284
  24.6 1.1 collective-permute-start.13
  25.7 1.2 collective-permute-start.8
  26.9 15.3 %collective-permute-done.9.rest_6_ = bf16[1040,256]{1,0:T(8,128)(2,1)S(1)} collective-permute-done((bf16[1040,256]{1,0:T(8,128)(2,1)}, bf16[1040,256]{1,0:T(8,128)(2,1)S(1)}, u32[]{:S(2)}, u32[]{:S(2)}) %collective-permute-start.9) | collective-permute-done | bytes 532512 | tf_op jit(solution)/shard_map/ppermute | solution.py:284
  42.2 3.1 %collective-permute-start.10 = (bf16[1040,256]{1,0:T(8,128)(2,1)S(1)}, bf16[1040,256]{1,0:T(8,128)(2,1)S(1)}, u32[]{:S(2)}, u32[]{:S(2)}) collective-permute-start(bf16[1040,256]{1,0:T(8,128)(2,1)S(1)} %collective-permute-done.9.rest_6_), channel_id=1, source_target_pairs={{0,32},{32,0},{1,33},{33,1},{2,34},{34,2},{3,35},{35,3},{4,36},{36... | collective-permute-start | bytes 1597448 | tf_op jit(solution)/shard_map/ppermute | solution.py:284
  45.3 13.4 %collective-permute-done.11.rest_8_ = bf16[1040,256]{1,0:T(8,128)(2,1)S(1)} collective-permute-done((bf16[1040,256]{1,0:T(8,128)(2,1)}, bf16[1040,256]{1,0:T(8,128)(2,1)S(1)}, u32[]{:S(2)}, u32[]{:S(2)}) %collective-permute-start.11) | collective-permute-done | bytes 532512 | tf_op jit(solution)/shard_map/ppermute | solution.py:284
  58.7 0.9 collective-permute-start.12
  60.4 5.6 %collective-permute-start.1 = (bf16[4,4,8,256]{3,2,1,0:T(8,128)(2,1)S(1)}, bf16[4,4,8,256]{3,2,1,0:T(8,128)(2,1)S(1)}, u32[]{:S(2)}, u32[]{:S(2)}) collective-permute-start(bf16[4,4,8,256]{3,2,1,0:T(8,128)(2,1)S(1)} %get-tuple-element.22), channel_id=1, source_target_pairs={{0,4},{1,5},{2,6},{3,7},{4,0},{5,1},{6,2},{7,3},{64,69},{65,70},{6... | collective-permute-start | bytes 196616 | tf_op jit(solution)/shard_map/ppermute | solution.py:320
  65.9 1.7 %collective-permute-done.1.refs_1_ = bf16[4,4,8,256]{3,2,1,0:T(8,128)(2,1)S(1)} collective-permute-done((bf16[4,4,8,256]{3,2,1,0:T(8,128)(2,1)S(1)}, bf16[4,4,8,256]{3,2,1,0:T(8,128)(2,1)S(1)}, u32[]{:S(2)}, u32[]{:S(2)}) %collective-permute-start.1) | collective-permute-done | bytes 65568 | tf_op jit(solution)/shard_map/ppermute | solution.py:320
  67.7 5.3 %collective-permute-start.2 = (bf16[2,4,8,256]{3,2,1,0:T(8,128)(2,1)S(1)}, bf16[2,4,8,256]{3,2,1,0:T(8,128)(2,1)S(1)}, u32[]{:S(2)}, u32[]{:S(2)}) collective-permute-start(bf16[2,4,8,256]{3,2,1,0:T(8,128)(2,1)S(1)} %get-tuple-element.24), channel_id=1, source_target_pairs={{0,64},{64,128},{128,192},{192,0},{1,65},{65,129},{129,193},{193,1... | collective-permute-start | bytes 98312 | tf_op jit(solution)/shard_map/ppermute | solution.py:284
  72.9 3.4 %collective-permute-done.2.refs_1_ = bf16[2,4,8,256]{3,2,1,0:T(8,128)(2,1)S(1)} collective-permute-done((bf16[2,4,8,256]{3,2,1,0:T(8,128)(2,1)S(1)}, bf16[2,4,8,256]{3,2,1,0:T(8,128)(2,1)S(1)}, u32[]{:S(2)}, u32[]{:S(2)}) %collective-permute-start.2) | collective-permute-done | bytes 32800 | tf_op jit(solution)/shard_map/ppermute | solution.py:284
  77.2 3.4 %collective-permute-done.3.refs_2_ = bf16[2,4,8,256]{3,2,1,0:T(8,128)(2,1)S(1)} collective-permute-done((bf16[2,4,8,256]{3,2,1,0:T(8,128)(2,1)S(1)}, bf16[2,4,8,256]{3,2,1,0:T(8,128)(2,1)S(1)}, u32[]{:S(2)}, u32[]{:S(2)}) %collective-permute-start.3) | collective-permute-done | bytes 32800 | tf_op jit(solution)/shard_map/ppermute | solution.py:284
  80.6 1.5 collective-permute-start.4
  82.0 1.6 %collective-permute-done.4.refs_3_ = bf16[2,4,8,256]{3,2,1,0:T(8,128)(2,1)S(1)} collective-permute-done((bf16[2,4,8,256]{3,2,1,0:T(8,128)(2,1)S(1)}, bf16[2,4,8,256]{3,2,1,0:T(8,128)(2,1)S(1)}, u32[]{:S(2)}, u32[]{:S(2)}) %collective-permute-start.4) | collective-permute-done | bytes 32800 | tf_op jit(solution)/shard_map/ppermute | solution.py:284
  83.7 0.9 collective-permute-start.5
  84.6 3.1 %collective-permute-done.5.rest_1_ = bf16[4,2,8,256]{3,2,1,0:T(8,128)(2,1)S(1)} collective-permute-done((bf16[4,2,8,256]{3,2,1,0:T(8,128)(2,1)S(1)}, bf16[4,2,8,256]{3,2,1,0:T(8,128)(2,1)S(1)}, u32[]{:S(2)}, u32[]{:S(2)}) %collective-permute-start.5) | collective-permute-done | bytes 32800 | tf_op jit(solution)/shard_map/ppermute | solution.py:284
  88.5 3.4 %collective-permute-done.6.rest_2_ = bf16[4,2,8,256]{3,2,1,0:T(8,128)(2,1)S(1)} collective-permute-done((bf16[4,2,8,256]{3,2,1,0:T(8,128)(2,1)S(1)}, bf16[4,2,8,256]{3,2,1,0:T(8,128)(2,1)S(1)}, u32[]{:S(2)}, u32[]{:S(2)}) %collective-permute-start.6) | collective-permute-done | bytes 32800 | tf_op jit(solution)/shard_map/ppermute | solution.py:284
  92.6 2.1 %collective-permute-done.7.rest_3_ = bf16[4,2,8,256]{3,2,1,0:T(8,128)(2,1)S(1)} collective-permute-done((bf16[4,2,8,256]{3,2,1,0:T(8,128)(2,1)S(1)}, bf16[4,2,8,256]{3,2,1,0:T(8,128)(2,1)S(1)}, u32[]{:S(2)}, u32[]{:S(2)}) %collective-permute-start.7) | collective-permute-done | bytes 32800 | tf_op jit(solution)/shard_map/ppermute | solution.py:284
  96.6 8.5 %chain.1 = bf16[8,2,2,2,4,8,256]{6,5,4,3,2,1,0:T(8,128)(2,1)S(1)} custom-call(bf16[8,2,2,2,4,8,256]{6,5,4,3,2,1,0:T(8,128)(2,1)S(1)} %bitcast.9, bf16[256,512]{1,0:T(8,128)(2,1)S(1)} %copy-done.3, bf16[256,512]{1,0:T(8,128)(2,1)S(1)} %copy-done.2, bf16[2,256,256]{2,1,0:T(8,128)(2,1)S(1)} %copy-done.1, bf16[4,2,8,256]{3,2,1,0:T(8,128)(2,1)S(1)} %get-tuple-element.27.rest_0_, ...), custom_call_target="tpu_custom_call" | custom-call | tf_op jit(solution)/shard_map/chain/pallas_call | solution.py:346
  105.1 48.7 %all_to_all.10 = bf16[256,8,256]{2,1,0:T(8,128)(2,1)S(1)} all-to-all(bf16[256,8,256]{2,1,0:T(8,128)(2,1)S(1)} %bitcast.10), channel_id=1, replica_groups=mesh['y'=4,'core'=2,'x'=4,'z'=8] {'z','core','x','y'}, dimensions={0} | all-to-all | bytes 2097152 | tf_op jit(solution)/shard_map/all_to_all | solution.py:280
  153.8 1.5 inverse_rows.1
  (38 shorter events, 4.9 us)
Async XLA Ops:
  5.0 91.6 %copy-start.1 = (bf16[2,256,256]{2,1,0:T(8,128)(2,1)S(1)}, bf16[2,256,256]{2,1,0:T(8,128)(2,1)}, u32[]{:S(2)}) copy-start(bf16[2,256,256]{2,1,0:T(8,128)(2,1)} %constant.13.clone.fold_ref) | copy-start | bytes 786436
  5.0 91.6 %copy-start.2 = (bf16[256,512]{1,0:T(8,128)(2,1)S(1)}, bf16[256,512]{1,0:T(8,128)(2,1)}, u32[]{:S(2)}) copy-start(bf16[256,512]{1,0:T(8,128)(2,1)} %constant.12.clone.inv_ref) | copy-start | bytes 786436
  5.0 91.6 %copy-start.3 = (bf16[256,512]{1,0:T(8,128)(2,1)S(1)}, bf16[256,512]{1,0:T(8,128)(2,1)}, u32[]{:S(2)}) copy-start(bf16[256,512]{1,0:T(8,128)(2,1)} %constant.11.clone.col_ref) | copy-start | bytes 786436
  5.0 91.5 %all-to-all-start = ((bf16[256,8,256]{2,1,0:T(8,128)(2,1)}), bf16[256,8,256]{2,1,0:T(8,128)(2,1)S(1)}, u32[]{:S(2)}, u32[]{:S(2)}) async-start(bf16[256,8,256]{2,1,0:T(8,128)(2,1)} %bitcast.2), calls=%async_computation | async-start | bytes 2097152 | tf_op jit(solution)/shard_map/all_to_all | solution.py:280
  20.7 21.5 %collective-permute-start.9 = (bf16[1040,256]{1,0:T(8,128)(2,1)}, bf16[1040,256]{1,0:T(8,128)(2,1)S(1)}, u32[]{:S(2)}, u32[]{:S(2)}) collective-permute-start(bf16[1040,256]{1,0:T(8,128)(2,1)} %get-tuple-element.32), channel_id=1, source_target_pairs={{0,64},{64,128},{128,192},{192,0},{1,65},{65,129},{129,193},{193,1... | collective-permute-start | bytes 1597448 | tf_op jit(solution)/shard_map/ppermute | solution.py:284
  22.1 36.6 %collective-permute-start.11 = (bf16[1040,256]{1,0:T(8,128)(2,1)}, bf16[1040,256]{1,0:T(8,128)(2,1)S(1)}, u32[]{:S(2)}, u32[]{:S(2)}) collective-permute-start(bf16[1040,256]{1,0:T(8,128)(2,1)} %get-tuple-element.33), channel_id=1, source_target_pairs={{0,128},{64,192},{128,0},{192,64},{1,129},{65,193},{129,1},{193,65... | collective-permute-start | bytes 1597448 | tf_op jit(solution)/shard_map/ppermute | solution.py:284
  24.6 35.1 %collective-permute-start.13 = (bf16[1040,256]{1,0:T(8,128)(2,1)}, bf16[1040,256]{1,0:T(8,128)(2,1)S(1)}, u32[]{:S(2)}, u32[]{:S(2)}) collective-permute-start(bf16[1040,256]{1,0:T(8,128)(2,1)} %get-tuple-element.34), channel_id=1, source_target_pairs={{0,192},{64,0},{128,64},{192,128},{1,193},{65,1},{129,65},{193,129... | collective-permute-start | bytes 1597448 | tf_op jit(solution)/shard_map/ppermute | solution.py:284
  25.7 69.1 %collective-permute-start.8 = (bf16[1040,256]{1,0:T(8,128)(2,1)S(1)}, bf16[1040,256]{1,0:T(8,128)(2,1)S(1)}, u32[]{:S(2)}, u32[]{:S(2)}) collective-permute-start(bf16[1040,256]{1,0:T(8,128)(2,1)S(1)} %copy-done.5), channel_id=1, source_target_pairs={{0,32},{32,0},{1,33},{33,1},{2,34},{34,2},{3,35},{35,3},{4,36},{36... | collective-permute-start | bytes 1597448 | tf_op jit(solution)/shard_map/ppermute | solution.py:284
  42.2 54.3 %copy-start.6 = (bf16[1040,256]{1,0:T(8,128)(2,1)}, bf16[1040,256]{1,0:T(8,128)(2,1)S(1)}, u32[]{:S(2)}) copy-start(bf16[1040,256]{1,0:T(8,128)(2,1)S(1)} %collective-permute-done.9.rest_6_) | copy-start | bytes 1597444
  42.2 52.5 %collective-permute-start.10 = (bf16[1040,256]{1,0:T(8,128)(2,1)S(1)}, bf16[1040,256]{1,0:T(8,128)(2,1)S(1)}, u32[]{:S(2)}, u32[]{:S(2)}) collective-permute-start(bf16[1040,256]{1,0:T(8,128)(2,1)S(1)} %collective-permute-done.9.rest_6_), channel_id=1, source_target_pairs={{0,32},{32,0},{1,33},{33,1},{2,34},{34,2},{3,35},{35,3},{4,36},{36... | collective-permute-start | bytes 1597448 | tf_op jit(solution)/shard_map/ppermute | solution.py:284
  58.7 36.1 %copy-start.7 = (bf16[1040,256]{1,0:T(8,128)(2,1)}, bf16[1040,256]{1,0:T(8,128)(2,1)S(1)}, u32[]{:S(2)}) copy-start(bf16[1040,256]{1,0:T(8,128)(2,1)S(1)} %collective-permute-done.11.rest_8_) | copy-start | bytes 1597444
  58.7 36.1 %collective-permute-start.12 = (bf16[1040,256]{1,0:T(8,128)(2,1)S(1)}, bf16[1040,256]{1,0:T(8,128)(2,1)S(1)}, u32[]{:S(2)}, u32[]{:S(2)}) collective-permute-start(bf16[1040,256]{1,0:T(8,128)(2,1)S(1)} %collective-permute-done.11.rest_8_), channel_id=1, source_target_pairs={{0,32},{32,0},{1,33},{33,1},{2,34},{34,2},{3,35},{35,3},{4,36},{36... | collective-permute-start | bytes 1597448 | tf_op jit(solution)/shard_map/ppermute | solution.py:284
  59.6 35.2 %copy-start.8 = (bf16[1040,256]{1,0:T(8,128)(2,1)}, bf16[1040,256]{1,0:T(8,128)(2,1)S(1)}, u32[]{:S(2)}) copy-start(bf16[1040,256]{1,0:T(8,128)(2,1)S(1)} %collective-permute-done.13.rest_10_) | copy-start | bytes 1597444
  59.6 36.9 %collective-permute-start.14 = (bf16[1040,256]{1,0:T(8,128)(2,1)S(1)}, bf16[1040,256]{1,0:T(8,128)(2,1)}, u32[]{:S(2)}, u32[]{:S(2)}) collective-permute-start(bf16[1040,256]{1,0:T(8,128)(2,1)S(1)} %collective-permute-done.13.rest_10_), channel_id=1, source_target_pairs={{0,32},{32,0},{1,33},{33,1},{2,34},{34,2},{3,35},{35,3},{4,36},{36... | collective-permute-start | bytes 1597448 | tf_op jit(solution)/shard_map/ppermute | solution.py:284
  59.7 0.7 collective-permute-start
  60.4 7.3 %collective-permute-start.1 = (bf16[4,4,8,256]{3,2,1,0:T(8,128)(2,1)S(1)}, bf16[4,4,8,256]{3,2,1,0:T(8,128)(2,1)S(1)}, u32[]{:S(2)}, u32[]{:S(2)}) collective-permute-start(bf16[4,4,8,256]{3,2,1,0:T(8,128)(2,1)S(1)} %get-tuple-element.22), channel_id=1, source_target_pairs={{0,4},{1,5},{2,6},{3,7},{4,0},{5,1},{6,2},{7,3},{64,69},{65,70},{6... | collective-permute-start | bytes 196616 | tf_op jit(solution)/shard_map/ppermute | solution.py:320
  67.7 8.6 %collective-permute-start.2 = (bf16[2,4,8,256]{3,2,1,0:T(8,128)(2,1)S(1)}, bf16[2,4,8,256]{3,2,1,0:T(8,128)(2,1)S(1)}, u32[]{:S(2)}, u32[]{:S(2)}) collective-permute-start(bf16[2,4,8,256]{3,2,1,0:T(8,128)(2,1)S(1)} %get-tuple-element.24), channel_id=1, source_target_pairs={{0,64},{64,128},{128,192},{192,0},{1,65},{65,129},{129,193},{193,1... | collective-permute-start | bytes 98312 | tf_op jit(solution)/shard_map/ppermute | solution.py:284
  76.3 4.3 %collective-permute-start.3 = (bf16[2,4,8,256]{3,2,1,0:T(8,128)(2,1)S(1)}, bf16[2,4,8,256]{3,2,1,0:T(8,128)(2,1)S(1)}, u32[]{:S(2)}, u32[]{:S(2)}) collective-permute-start(bf16[2,4,8,256]{3,2,1,0:T(8,128)(2,1)S(1)} %get-tuple-element.25), channel_id=1, source_target_pairs={{0,128},{64,192},{128,0},{192,64},{1,129},{65,193},{129,1},{193,65... | collective-permute-start | bytes 98312 | tf_op jit(solution)/shard_map/ppermute | solution.py:284
  80.6 3.1 %collective-permute-start.4 = (bf16[2,4,8,256]{3,2,1,0:T(8,128)(2,1)S(1)}, bf16[2,4,8,256]{3,2,1,0:T(8,128)(2,1)S(1)}, u32[]{:S(2)}, u32[]{:S(2)}) collective-permute-start(bf16[2,4,8,256]{3,2,1,0:T(8,128)(2,1)S(1)} %get-tuple-element.26), channel_id=1, source_target_pairs={{0,192},{64,0},{128,64},{192,128},{1,193},{65,1},{129,65},{193,129... | collective-permute-start | bytes 98312 | tf_op jit(solution)/shard_map/ppermute | solution.py:284
  83.7 4.1 %collective-permute-start.5 = (bf16[4,2,8,256]{3,2,1,0:T(8,128)(2,1)S(1)}, bf16[4,2,8,256]{3,2,1,0:T(8,128)(2,1)S(1)}, u32[]{:S(2)}, u32[]{:S(2)}) collective-permute-start(bf16[4,2,8,256]{3,2,1,0:T(8,128)(2,1)S(1)} %get-tuple-element.28), channel_id=1, source_target_pairs={{0,8},{8,16},{16,24},{24,0},{1,9},{9,17},{17,25},{25,1},{2,10},{10... | collective-permute-start | bytes 98312 | tf_op jit(solution)/shard_map/ppermute | solution.py:284
  87.7 4.3 %collective-permute-start.6 = (bf16[4,2,8,256]{3,2,1,0:T(8,128)(2,1)S(1)}, bf16[4,2,8,256]{3,2,1,0:T(8,128)(2,1)S(1)}, u32[]{:S(2)}, u32[]{:S(2)}) collective-permute-start(bf16[4,2,8,256]{3,2,1,0:T(8,128)(2,1)S(1)} %get-tuple-element.29), channel_id=1, source_target_pairs={{0,16},{8,24},{16,0},{24,8},{1,17},{9,25},{17,1},{25,9},{2,18},{10... | collective-permute-start | bytes 98312 | tf_op jit(solution)/shard_map/ppermute | solution.py:284
  92.0 2.8 %collective-permute-start.7 = (bf16[4,2,8,256]{3,2,1,0:T(8,128)(2,1)S(1)}, bf16[4,2,8,256]{3,2,1,0:T(8,128)(2,1)S(1)}, u32[]{:S(2)}, u32[]{:S(2)}) collective-permute-start(bf16[4,2,8,256]{3,2,1,0:T(8,128)(2,1)S(1)} %get-tuple-element.30), channel_id=1, source_target_pairs={{0,24},{8,0},{16,8},{24,16},{1,25},{9,1},{17,9},{25,17},{2,26},{10... | collective-permute-start | bytes 98312 | tf_op jit(solution)/shard_map/ppermute | solution.py:284
  105.1 48.7 %copy-start = (bf16[2,128,2048]{2,1,0:T(8,128)(2,1)S(1)}, bf16[2,128,2048]{2,1,0:T(8,128)(2,1)}, u32[]{:S(2)}) copy-start(bf16[2,128,2048]{2,1,0:T(8,128)(2,1)} %param.11) | copy-start | bytes 3145732
  105.1 48.7 %copy-start.4 = (bf16[256,512]{1,0:T(8,128)(2,1)S(1)}, bf16[256,512]{1,0:T(8,128)(2,1)}, u32[]{:S(2)}) copy-start(bf16[256,512]{1,0:T(8,128)(2,1)} %constant.14.clone.table_ref) | copy-start | bytes 786436
  (4 other events, 23.3 us)

commit v7 on v6

--- a/solution.py
+++ b/solution.py
@@ -82,26 +82,25 @@
 
 
 def first_kernel(table_hbm, act_hbm, cot_hbm, first_ref, second_ref, bias_hbm, *rest):
-    pieces, outs, rows_ref = rest[:Y], rest[Y : Y + 2], rest[Y + 2]
-    part, field, table_ref, act_ref, held, biases, sems, own_sems = rest[Y + 3 :]
+    pieces, cot_rows_ref, rows_ref = rest[:Y], rest[Y], rest[Y + 1]
+    part, field, table_ref, act_ref, held, biases, sems, own_sems = rest[Y + 2 :]
     size = held.shape[2]
     y, core, z, odd = (*(lax.axis_index(name) for name in ("y", "core", "z")), lax.axis_index("x") & 1)
-    targets = [(z + y + 4 * i) & (Z - 1) for i in range(2)]
-    lines = part.shape[1]
+    target = (z + y + 4 * core) & (Z - 1)
+    lines = part.shape[0]
     pairs = [
-        (table_hbm.at[pl.ds((targets[0] * 2 + core) * lines, lines)], part.at[0]),
-        (table_hbm.at[pl.ds((targets[1] * 2 + core) * lines, lines)], part.at[1]),
+        (table_hbm.at[pl.ds(target * lines, lines)], part),
         (cot_hbm, field),
         (table_hbm, table_ref),
         (act_hbm, act_ref),
         (bias_hbm, biases),
     ]
     own = []
-    for k, (source, target) in enumerate(pairs):
-        copy = pltpu.make_async_copy(source, target, own_sems.at[k])
+    for k, (source, place) in enumerate(pairs):
+        copy = pltpu.make_async_copy(source, place, own_sems.at[k])
         copy.start()
         own.append(copy)
-        if k != 2:
+        if k != 1:
             continue
         loads = []
         for d in range(Y):
@@ -118,23 +117,19 @@
 
     depth = table_ref.shape[1] // 2
     line = lax.broadcasted_iota(jnp.int32, (lines, size), 0)
-    first_even = jnp.logical_and(line < 8, (line & 1) == 0)
-    factors = []
-    for target in targets:
-        zero_mode = jnp.logical_and(first_even, jnp.logical_and(target == 0, core == 0))
-        factors.append(jnp.where(zero_mode, 1.0, 2.0).astype(F32))
-    for copy in own[:3]:
-        copy.wait()
-    rows = jnp.concatenate([part[0, :, :depth], part[1, :, :depth], part[0, :, depth:], part[1, :, depth:]], axis=0)
+    zero_mode = jnp.logical_and(jnp.logical_and(line < 8, (line & 1) == 0), target == 0)
+    factor = jnp.where(zero_mode, 1.0, 2.0).astype(F32)
+    for copy in own[:2]:
+        copy.wait()
+    rows = jnp.concatenate([part[:, :depth], part[:, depth:]], axis=0)
     for n in range(2 * Y):
         spectrum = dot(rows, field[:, n * size : (n + 1) * size])
-        spectrum = spectrum[: 2 * lines] + spectrum[2 * lines :]
+        tiles = ((spectrum[:lines] + spectrum[lines:]) * factor).astype(BF16)
         for i in range(2):
-            tiles = (spectrum[i * lines : (i + 1) * lines] * factors[i]).astype(BF16)
             for m in range(2):
-                outs[i][n // 2, 2 * m + n % 2] = tiles[m * 8 : (m + 1) * 8]
-
-    for copy in own[3:]:
+                cot_rows_ref[i, n // 2, 2 * m + n % 2] = tiles[(2 * i + m) * 8 : (2 * i + m + 1) * 8]
+
+    for copy in own[2:]:
         copy.wait()
     for d in range(Y):
         block = ((y + d) & (Y - 1)) * 2 + odd
@@ -158,12 +153,18 @@
         copy.wait()
 
 
-def turn_y_kernel(*refs):
-    arrived, outs = refs[:2], refs[2:]
-    y = lax.axis_index("y")
+def turn_core_kernel(arrived_ref, kept_ref, sent_ref):
+    core = lax.axis_index("core")
+    kept_ref[...] = arrived_ref[core]
+    sent_ref[...] = arrived_ref[1 - core]
+
+
+def turn_y_kernel(kept_ref, arrived_ref, *outs):
+    y, core = lax.axis_index("y"), lax.axis_index("core")
     for d in range(Y):
-        for i in range(2):
-            outs[d][i] = arrived[i][(y + d) & (Y - 1)]
+        to = (y + d) & (Y - 1)
+        outs[d][core] = kept_ref[to]
+        outs[d][1 - core] = arrived_ref[to]
 
 
 def turn_x_kernel(*refs):
@@ -287,19 +288,17 @@
     made = pl.pallas_call(
         first_kernel,
         in_specs=[hbm] * 6,
-        out_specs=[hbm] * Y + [vmem] * 3,
-        out_shape=[pltpu.HBM((4 * size + 16, size), BF16)] * Y
-        + [shaped(Y, X, tile, size)] * 2
-        + [shaped(*blocks)],
+        out_specs=[hbm] * Y + [vmem] * 2,
+        out_shape=[pltpu.HBM((4 * size + 16, size), BF16)] * Y + [shaped(2, Y, X, tile, size), shaped(*blocks)],
         scratch_shapes=[
-            pltpu.VMEM((2, 2 * tile, 2 * count), BF16),
+            pltpu.VMEM((4 * tile, 2 * count), BF16),
             pltpu.VMEM((count, channels), BF16),
             pltpu.VMEM(forward_rows.shape, BF16),
             pltpu.VMEM((count, channels), BF16),
             pltpu.VMEM((Y, 4 * size + 16, size), BF16),
             pltpu.VMEM(b_first.shape, F32),
             pltpu.SemaphoreType.DMA((Y, 5)),
-            pltpu.SemaphoreType.DMA((6,)),
+            pltpu.SemaphoreType.DMA((5,)),
         ],
         compiler_params=SMALL,
         name="first",
@@ -313,16 +312,26 @@
             b_first,
         )
     )
-    pieces, cot_rows, act_rows = made[:Y], made[Y : Y + 2], made[Y + 2]
-    arrived = []
-    for i in range(2):
-        route = [(y * Z + z, y * Z + (z + y + 4 * i) % Z) for y in range(Y) for z in range(Z)]
-        arrived.append(lax.ppermute(cot_rows[i], ("y", "z"), route))
+    pieces, cot_rows, act_rows = made[:Y], made[Y], made[Y + 1]
+    route = []
+    for line in range(2 * Y):
+        shift = line // 2 + 4 * (line % 2)
+        route += [(line * Z + z, line * Z + (z + shift) % Z) for z in range(Z)]
+    arrived = lax.ppermute(cot_rows, ("y", "core", "z"), route)
     weights = []
     for d in range(Y):
         piece = shifted(pieces[d], "y", d) if d else pieces[0]
         weights += [piece, shifted(piece, "core", 1)]
     act_columns = exchange(act_rows)
+    kept, sent = pl.pallas_call(
+        turn_core_kernel,
+        in_specs=[vmem],
+        out_specs=[vmem] * 2,
+        out_shape=[shaped(Y, X, tile, size)] * 2,
+        compiler_params=SMALL,
+        name="turn_core",
+    )(*near(arrived))
+    arrived = shifted(sent, "core", 1)
     turned = pl.pallas_call(
         turn_y_kernel,
         in_specs=[vmem] * 2,
@@ -330,7 +339,7 @@
         out_shape=[shaped(2, X, tile, size)] * Y,
         compiler_params=SMALL,
         name="turn_y",
-    )(*near(*arrived))
+    )(*near(kept, arrived))
     arrived = [turned[0]] + [shifted(turned[d], "y", d) for d in range(1, Y)]
     turned = pl.pallas_call(
         turn_x_kernel,

time: 156 us -> 154 us (0.987)
  starting transfers between devices: 42.2 us -> 38.5 us
  waiting for transfers between devices: 47.5 us -> 49.8 us
    ppermute x13 -> x14, starting transfers between devices: 20.3 us -> 15.5 us  [shifted(): lax.ppermute(value, axis, [(i, (i + distance) % size) for i in range(size)])]
    ppermute x13 -> x14, waiting for transfers between devices: 45.8 us -> 47.3 us  [shifted(): lax.ppermute(value, axis, [(i, (i + distance) % size) for i in range(size)])]
    ppermute x2 -> x1, starting transfers between devices: 6.21 us -> 7.38 us  [body(): arrived = lax.ppermute(cot_rows, ('y', 'core', 'z'), route)]
  transfers between devices with their start and end apart: 16 -> 16, of which waited for: 9 -> 10; matrix products, arithmetic and copies ran while one was open for 0% -> 0% of each run, Pallas kernels for 0% -> 0%
where the time goes in v7:
time: 154 us; the launch traced here: 153 us
  waiting for transfers between devices  49.8 us (32%)
  blocking collectives  47.7 us (31%)
  starting transfers between devices  38.5 us (25%)
  Pallas kernels  15 us (10%)
  local copies, waits for them, and re-layouts  1.8 us (1%)
    all_to_all x1, blocking collectives, exchange(): lax.all_to_all(flat, EVERYONE, split_axis=0, concat_axis=0, tiled=True)  47.7 us
    ppermute x14, waiting for transfers between devices, shifted(): lax.ppermute(value, axis, [(i, (i + distance) % size) for i in range(size)])  47.3 us
    all_to_all x1, starting transfers between devices, exchange(): lax.all_to_all(flat, EVERYONE, split_axis=0, concat_axis=0, tiled=True)  15.7 us
    ppermute x14, starting transfers between devices, shifted(): lax.ppermute(value, axis, [(i, (i + distance) % size) for i in range(size)])  15.5 us
    pallas_call x1, Pallas kernels, body(): pl.pallas_call(chain_kernel, in_specs=[vmem] * (4 + X) + [hbm] * sections...  8.47 us
    ppermute x1, starting transfers between devices, body(): arrived = lax.ppermute(cot_rows, ('y', 'core', 'z'), route)  7.38 us
    pallas_call x1, Pallas kernels, body(): pl.pallas_call(first_kernel, in_specs=[hbm] * 6, out_specs=[hbm] * Y + [v...  4.94 us
  transfers between devices with their start and end apart: 16, of which 10 were waited for; matrix products, arithmetic and copies ran while one was open for 0% of the time, Pallas kernels for 0%

profile of v7, /device:TPU:1, one launch (start us, length us, event | category | flops | bytes accessed | tf_op | source)
XLA Modules:
  0.0 153.2 jit_solution(1126676133614967797)
XLA Ops:
  0.0 4.9 %first.1 = (bf16[1040,256]{1,0:T(8,128)(2,1)}, bf16[1040,256]{1,0:T(8,128)(2,1)}, bf16[1040,256]{1,0:T(8,128)(2,1)}, bf16[1040,256]{1,0:T(8,128)(2,1)}, bf16[2,4...) custom-call(bf16[256,512]{1,0:T(8,128)(2,1)} %constant.10.clone.table_hbm, ...), custom_call_target="tpu_custom_call" | custom-call | tf_op jit(solution)/shard_map/first/pallas_call | solution.py:288
  5.0 15.7 %all-to-all-start = ((bf16[256,8,256]{2,1,0:T(8,128)(2,1)}), bf16[256,8,256]{2,1,0:T(8,128)(2,1)S(1)}, u32[]{:S(2)}, u32[]{:S(2)}) async-start(bf16[256,8,256]{2,1,0:T(8,128)(2,1)} %bitcast.2), calls=%async_computation | async-start | bytes 2097152 | tf_op jit(solution)/shard_map/all_to_all | solution.py:281
  20.7 1.4 collective-permute-start.9
  22.1 2.5 %collective-permute-start.11 = (bf16[1040,256]{1,0:T(8,128)(2,1)}, bf16[1040,256]{1,0:T(8,128)(2,1)S(1)}, u32[]{:S(2)}, u32[]{:S(2)}) collective-permute-start(bf16[1040,256]{1,0:T(8,128)(2,1)} %get-tuple-element.35), channel_id=1, source_target_pairs={{0,128},{64,192},{128,0},{192,64},{1,129},{65,193},{129,1},{193,65... | collective-permute-start | bytes 1597448 | tf_op jit(solution)/shard_map/ppermute | solution.py:285
  24.5 1.1 collective-permute-start.13
  25.7 1.2 collective-permute-start.8
  26.9 15.3 %collective-permute-done.9.rest_6_ = bf16[1040,256]{1,0:T(8,128)(2,1)S(1)} collective-permute-done((bf16[1040,256]{1,0:T(8,128)(2,1)}, bf16[1040,256]{1,0:T(8,128)(2,1)S(1)}, u32[]{:S(2)}, u32[]{:S(2)}) %collective-permute-start.9) | collective-permute-done | bytes 532512 | tf_op jit(solution)/shard_map/ppermute | solution.py:285
  42.2 3.1 %collective-permute-start.10 = (bf16[1040,256]{1,0:T(8,128)(2,1)S(1)}, bf16[1040,256]{1,0:T(8,128)(2,1)S(1)}, u32[]{:S(2)}, u32[]{:S(2)}) collective-permute-start(bf16[1040,256]{1,0:T(8,128)(2,1)S(1)} %collective-permute-done.9.rest_6_), channel_id=1, source_target_pairs={{0,32},{32,0},{1,33},{33,1},{2,34},{34,2},{3,35},{35,3},{4,36},{36... | collective-permute-start | bytes 1597448 | tf_op jit(solution)/shard_map/ppermute | solution.py:285
  45.3 13.4 %collective-permute-done.11.rest_8_ = bf16[1040,256]{1,0:T(8,128)(2,1)S(1)} collective-permute-done((bf16[1040,256]{1,0:T(8,128)(2,1)}, bf16[1040,256]{1,0:T(8,128)(2,1)S(1)}, u32[]{:S(2)}, u32[]{:S(2)}) %collective-permute-start.11) | collective-permute-done | bytes 532512 | tf_op jit(solution)/shard_map/ppermute | solution.py:285
  59.7 7.4 %collective-permute-start = (bf16[2,4,4,8,256]{4,3,2,1,0:T(8,128)(2,1)S(1)}, bf16[2,4,4,8,256]{4,3,2,1,0:T(8,128)(2,1)S(1)}, u32[]{:S(2)}, u32[]{:S(2)}) collective-permute-start(bf16[2,4,4,8,256]{4,3,2,1,0:T(8,128)(2,1)S(1)} %get-tuple-element.22), channel_id=1, source_target_pairs={{0,0},{1,1},{2,2},{3,3},{4,4},{5,5},{6,6},{7,7},{32,36},{33,37},{3... | collective-permute-start | bytes 393224 | tf_op jit(solution)/shard_map/ppermute | solution.py:320
  67.1 2.4 %collective-permute-done.arrived_ref = bf16[2,4,4,8,256]{4,3,2,1,0:T(8,128)(2,1)S(1)} collective-permute-done((bf16[2,4,4,8,256]{4,3,2,1,0:T(8,128)(2,1)S(1)}, bf16[2,4,4,8,256]{4,3,2,1,0:T(8,128)(2,1)S(1)}, u32[]{:S(2)}, u32[]{:S(2)}) %collective-permute-start) | collective-permute-done | bytes 131104 | tf_op jit(solution)/shard_map/ppermute | solution.py:320
  69.6 1.2 collective-permute-done.1.arrived_ref
  70.9 1.8 %collective-permute-start.2 = (bf16[2,4,8,256]{3,2,1,0:T(8,128)(2,1)S(1)}, bf16[2,4,8,256]{3,2,1,0:T(8,128)(2,1)S(1)}, u32[]{:S(2)}, u32[]{:S(2)}) collective-permute-start(bf16[2,4,8,256]{3,2,1,0:T(8,128)(2,1)S(1)} %get-tuple-element.26), channel_id=1, source_target_pairs={{0,64},{64,128},{128,192},{192,0},{1,65},{65,129},{129,193},{193,1... | collective-permute-start | bytes 98312 | tf_op jit(solution)/shard_map/ppermute | solution.py:285
  72.7 2.3 %collective-permute-done.2.refs_1_ = bf16[2,4,8,256]{3,2,1,0:T(8,128)(2,1)S(1)} collective-permute-done((bf16[2,4,8,256]{3,2,1,0:T(8,128)(2,1)S(1)}, bf16[2,4,8,256]{3,2,1,0:T(8,128)(2,1)S(1)}, u32[]{:S(2)}, u32[]{:S(2)}) %collective-permute-start.2) | collective-permute-done | bytes 32800 | tf_op jit(solution)/shard_map/ppermute | solution.py:285
  75.0 1.1 collective-permute-start.3
  76.1 3.1 %collective-permute-done.3.refs_2_ = bf16[2,4,8,256]{3,2,1,0:T(8,128)(2,1)S(1)} collective-permute-done((bf16[2,4,8,256]{3,2,1,0:T(8,128)(2,1)S(1)}, bf16[2,4,8,256]{3,2,1,0:T(8,128)(2,1)S(1)}, u32[]{:S(2)}, u32[]{:S(2)}) %collective-permute-start.3) | collective-permute-done | bytes 32800 | tf_op jit(solution)/shard_map/ppermute | solution.py:285
  79.2 2.8 %collective-permute-done.4.refs_3_ = bf16[2,4,8,256]{3,2,1,0:T(8,128)(2,1)S(1)} collective-permute-done((bf16[2,4,8,256]{3,2,1,0:T(8,128)(2,1)S(1)}, bf16[2,4,8,256]{3,2,1,0:T(8,128)(2,1)S(1)}, u32[]{:S(2)}, u32[]{:S(2)}) %collective-permute-start.4) | collective-permute-done | bytes 32800 | tf_op jit(solution)/shard_map/ppermute | solution.py:285
  82.8 3.3 %collective-permute-done.5.rest_1_ = bf16[4,2,8,256]{3,2,1,0:T(8,128)(2,1)S(1)} collective-permute-done((bf16[4,2,8,256]{3,2,1,0:T(8,128)(2,1)S(1)}, bf16[4,2,8,256]{3,2,1,0:T(8,128)(2,1)S(1)}, u32[]{:S(2)}, u32[]{:S(2)}) %collective-permute-start.5) | collective-permute-done | bytes 32800 | tf_op jit(solution)/shard_map/ppermute | solution.py:285
  86.1 1.0 collective-permute-start.6
  87.0 3.6 %collective-permute-done.6.rest_2_ = bf16[4,2,8,256]{3,2,1,0:T(8,128)(2,1)S(1)} collective-permute-done((bf16[4,2,8,256]{3,2,1,0:T(8,128)(2,1)S(1)}, bf16[4,2,8,256]{3,2,1,0:T(8,128)(2,1)S(1)}, u32[]{:S(2)}, u32[]{:S(2)}) %collective-permute-start.6) | collective-permute-done | bytes 32800 | tf_op jit(solution)/shard_map/ppermute | solution.py:285
  91.1 2.3 %collective-permute-done.7.rest_3_ = bf16[4,2,8,256]{3,2,1,0:T(8,128)(2,1)S(1)} collective-permute-done((bf16[4,2,8,256]{3,2,1,0:T(8,128)(2,1)S(1)}, bf16[4,2,8,256]{3,2,1,0:T(8,128)(2,1)S(1)}, u32[]{:S(2)}, u32[]{:S(2)}) %collective-permute-start.7) | collective-permute-done | bytes 32800 | tf_op jit(solution)/shard_map/ppermute | solution.py:285
  95.2 8.5 %chain.1 = bf16[8,2,2,2,4,8,256]{6,5,4,3,2,1,0:T(8,128)(2,1)S(1)} custom-call(bf16[8,2,2,2,4,8,256]{6,5,4,3,2,1,0:T(8,128)(2,1)S(1)} %bitcast.9, bf16[256,512]{1,0:T(8,128)(2,1)S(1)} %copy-done.3, bf16[256,512]{1,0:T(8,128)(2,1)S(1)} %copy-done.2, bf16[2,256,256]{2,1,0:T(8,128)(2,1)S(1)} %copy-done.1, bf16[4,2,8,256]{3,2,1,0:T(8,128)(2,1)S(1)} %get-tuple-element.29.rest_0_, ...), custom_call_target="tpu_custom_call" | custom-call | tf_op jit(solution)/shard_map/chain/pallas_call | solution.py:355
  103.7 47.7 %all_to_all.10 = bf16[256,8,256]{2,1,0:T(8,128)(2,1)S(1)} all-to-all(bf16[256,8,256]{2,1,0:T(8,128)(2,1)S(1)} %bitcast.10), channel_id=1, replica_groups=mesh['y'=4,'core'=2,'x'=4,'z'=8] {'z','core','x','y'}, dimensions={0} | all-to-all | bytes 2097152 | tf_op jit(solution)/shard_map/all_to_all | solution.py:281
  151.5 1.5 %inverse_rows.1 = bf16[256,2048]{1,0:T(8,128)(2,1)} custom-call(bf16[256,512]{1,0:T(8,128)(2,1)S(1)} %copy-done.4, bf16[8,2,2,2,4,8,256]{6,5,4,3,2,1,0:T(8,128)(2,1)S(1)} %bitcast.11, bf16[256,2048]{1,0:T(8,128)(2,1)S(1)} %bitcast.8), custom_call_target="tpu_custom_call" | custom-call | tf_op jit(solution)/shard_map/inverse_rows/pallas_call | solution.py:368
  (39 shorter events, 4.2 us)
Async XLA Ops:
  5.0 90.2 %copy-start.1 = (bf16[2,256,256]{2,1,0:T(8,128)(2,1)S(1)}, bf16[2,256,256]{2,1,0:T(8,128)(2,1)}, u32[]{:S(2)}) copy-start(bf16[2,256,256]{2,1,0:T(8,128)(2,1)} %constant.13.clone.fold_ref) | copy-start | bytes 786436
  5.0 90.2 %copy-start.2 = (bf16[256,512]{1,0:T(8,128)(2,1)S(1)}, bf16[256,512]{1,0:T(8,128)(2,1)}, u32[]{:S(2)}) copy-start(bf16[256,512]{1,0:T(8,128)(2,1)} %constant.12.clone.inv_ref) | copy-start | bytes 786436
  5.0 90.2 %copy-start.3 = (bf16[256,512]{1,0:T(8,128)(2,1)S(1)}, bf16[256,512]{1,0:T(8,128)(2,1)}, u32[]{:S(2)}) copy-start(bf16[256,512]{1,0:T(8,128)(2,1)} %constant.11.clone.col_ref) | copy-start | bytes 786436
  5.0 90.2 %all-to-all-start = ((bf16[256,8,256]{2,1,0:T(8,128)(2,1)}), bf16[256,8,256]{2,1,0:T(8,128)(2,1)S(1)}, u32[]{:S(2)}, u32[]{:S(2)}) async-start(bf16[256,8,256]{2,1,0:T(8,128)(2,1)} %bitcast.2), calls=%async_computation | async-start | bytes 2097152 | tf_op jit(solution)/shard_map/all_to_all | solution.py:281
  20.7 21.5 %collective-permute-start.9 = (bf16[1040,256]{1,0:T(8,128)(2,1)}, bf16[1040,256]{1,0:T(8,128)(2,1)S(1)}, u32[]{:S(2)}, u32[]{:S(2)}) collective-permute-start(bf16[1040,256]{1,0:T(8,128)(2,1)} %get-tuple-element.34), channel_id=1, source_target_pairs={{0,64},{64,128},{128,192},{192,0},{1,65},{65,129},{129,193},{193,1... | collective-permute-start | bytes 1597448 | tf_op jit(solution)/shard_map/ppermute | solution.py:285
  22.1 36.6 %collective-permute-start.11 = (bf16[1040,256]{1,0:T(8,128)(2,1)}, bf16[1040,256]{1,0:T(8,128)(2,1)S(1)}, u32[]{:S(2)}, u32[]{:S(2)}) collective-permute-start(bf16[1040,256]{1,0:T(8,128)(2,1)} %get-tuple-element.35), channel_id=1, source_target_pairs={{0,128},{64,192},{128,0},{192,64},{1,129},{65,193},{129,1},{193,65... | collective-permute-start | bytes 1597448 | tf_op jit(solution)/shard_map/ppermute | solution.py:285
  24.5 35.1 %collective-permute-start.13 = (bf16[1040,256]{1,0:T(8,128)(2,1)}, bf16[1040,256]{1,0:T(8,128)(2,1)S(1)}, u32[]{:S(2)}, u32[]{:S(2)}) collective-permute-start(bf16[1040,256]{1,0:T(8,128)(2,1)} %get-tuple-element.36), channel_id=1, source_target_pairs={{0,192},{64,0},{128,64},{192,128},{1,193},{65,1},{129,65},{193,129... | collective-permute-start | bytes 1597448 | tf_op jit(solution)/shard_map/ppermute | solution.py:285
  25.7 67.7 %collective-permute-start.8 = (bf16[1040,256]{1,0:T(8,128)(2,1)S(1)}, bf16[1040,256]{1,0:T(8,128)(2,1)S(1)}, u32[]{:S(2)}, u32[]{:S(2)}) collective-permute-start(bf16[1040,256]{1,0:T(8,128)(2,1)S(1)} %copy-done.5), channel_id=1, source_target_pairs={{0,32},{32,0},{1,33},{33,1},{2,34},{34,2},{3,35},{35,3},{4,36},{36... | collective-permute-start | bytes 1597448 | tf_op jit(solution)/shard_map/ppermute | solution.py:285
  42.2 53.0 %copy-start.6 = (bf16[1040,256]{1,0:T(8,128)(2,1)}, bf16[1040,256]{1,0:T(8,128)(2,1)S(1)}, u32[]{:S(2)}) copy-start(bf16[1040,256]{1,0:T(8,128)(2,1)S(1)} %collective-permute-done.9.rest_6_) | copy-start | bytes 1597444
  42.2 51.2 %collective-permute-start.10 = (bf16[1040,256]{1,0:T(8,128)(2,1)S(1)}, bf16[1040,256]{1,0:T(8,128)(2,1)S(1)}, u32[]{:S(2)}, u32[]{:S(2)}) collective-permute-start(bf16[1040,256]{1,0:T(8,128)(2,1)S(1)} %collective-permute-done.9.rest_6_), channel_id=1, source_target_pairs={{0,32},{32,0},{1,33},{33,1},{2,34},{34,2},{3,35},{35,3},{4,36},{36... | collective-permute-start | bytes 1597448 | tf_op jit(solution)/shard_map/ppermute | solution.py:285
  58.7 34.7 %copy-start.7 = (bf16[1040,256]{1,0:T(8,128)(2,1)}, bf16[1040,256]{1,0:T(8,128)(2,1)S(1)}, u32[]{:S(2)}) copy-start(bf16[1040,256]{1,0:T(8,128)(2,1)S(1)} %collective-permute-done.11.rest_8_) | copy-start | bytes 1597444
  58.7 34.7 %collective-permute-start.12 = (bf16[1040,256]{1,0:T(8,128)(2,1)S(1)}, bf16[1040,256]{1,0:T(8,128)(2,1)S(1)}, u32[]{:S(2)}, u32[]{:S(2)}) collective-permute-start(bf16[1040,256]{1,0:T(8,128)(2,1)S(1)} %collective-permute-done.11.rest_8_), channel_id=1, source_target_pairs={{0,32},{32,0},{1,33},{33,1},{2,34},{34,2},{3,35},{35,3},{4,36},{36... | collective-permute-start | bytes 1597448 | tf_op jit(solution)/shard_map/ppermute | solution.py:285
  59.6 33.8 %copy-start.8 = (bf16[1040,256]{1,0:T(8,128)(2,1)}, bf16[1040,256]{1,0:T(8,128)(2,1)S(1)}, u32[]{:S(2)}) copy-start(bf16[1040,256]{1,0:T(8,128)(2,1)S(1)} %collective-permute-done.13.rest_10_) | copy-start | bytes 1597444
  59.6 35.6 %collective-permute-start.14 = (bf16[1040,256]{1,0:T(8,128)(2,1)S(1)}, bf16[1040,256]{1,0:T(8,128)(2,1)}, u32[]{:S(2)}, u32[]{:S(2)}) collective-permute-start(bf16[1040,256]{1,0:T(8,128)(2,1)S(1)} %collective-permute-done.13.rest_10_), channel_id=1, source_target_pairs={{0,32},{32,0},{1,33},{33,1},{2,34},{34,2},{3,35},{35,3},{4,36},{36... | collective-permute-start | bytes 1597448 | tf_op jit(solution)/shard_map/ppermute | solution.py:285
  59.7 9.8 %collective-permute-start = (bf16[2,4,4,8,256]{4,3,2,1,0:T(8,128)(2,1)S(1)}, bf16[2,4,4,8,256]{4,3,2,1,0:T(8,128)(2,1)S(1)}, u32[]{:S(2)}, u32[]{:S(2)}) collective-permute-start(bf16[2,4,4,8,256]{4,3,2,1,0:T(8,128)(2,1)S(1)} %get-tuple-element.22), channel_id=1, source_target_pairs={{0,0},{1,1},{2,2},{3,3},{4,4},{5,5},{6,6},{7,7},{32,36},{33,37},{3... | collective-permute-start | bytes 393224 | tf_op jit(solution)/shard_map/ppermute | solution.py:320
  69.5 1.3 collective-permute-start.1
  70.9 4.1 %collective-permute-start.2 = (bf16[2,4,8,256]{3,2,1,0:T(8,128)(2,1)S(1)}, bf16[2,4,8,256]{3,2,1,0:T(8,128)(2,1)S(1)}, u32[]{:S(2)}, u32[]{:S(2)}) collective-permute-start(bf16[2,4,8,256]{3,2,1,0:T(8,128)(2,1)S(1)} %get-tuple-element.26), channel_id=1, source_target_pairs={{0,64},{64,128},{128,192},{192,0},{1,65},{65,129},{129,193},{193,1... | collective-permute-start | bytes 98312 | tf_op jit(solution)/shard_map/ppermute | solution.py:285
  75.0 4.3 %collective-permute-start.3 = (bf16[2,4,8,256]{3,2,1,0:T(8,128)(2,1)S(1)}, bf16[2,4,8,256]{3,2,1,0:T(8,128)(2,1)S(1)}, u32[]{:S(2)}, u32[]{:S(2)}) collective-permute-start(bf16[2,4,8,256]{3,2,1,0:T(8,128)(2,1)S(1)} %get-tuple-element.27), channel_id=1, source_target_pairs={{0,128},{64,192},{128,0},{192,64},{1,129},{65,193},{129,1},{193,65... | collective-permute-start | bytes 98312 | tf_op jit(solution)/shard_map/ppermute | solution.py:285
  79.2 2.8 %collective-permute-start.4 = (bf16[2,4,8,256]{3,2,1,0:T(8,128)(2,1)S(1)}, bf16[2,4,8,256]{3,2,1,0:T(8,128)(2,1)S(1)}, u32[]{:S(2)}, u32[]{:S(2)}) collective-permute-start(bf16[2,4,8,256]{3,2,1,0:T(8,128)(2,1)S(1)} %get-tuple-element.28), channel_id=1, source_target_pairs={{0,192},{64,0},{128,64},{192,128},{1,193},{65,1},{129,65},{193,129... | collective-permute-start | bytes 98312 | tf_op jit(solution)/shard_map/ppermute | solution.py:285
  82.0 4.1 %collective-permute-start.5 = (bf16[4,2,8,256]{3,2,1,0:T(8,128)(2,1)S(1)}, bf16[4,2,8,256]{3,2,1,0:T(8,128)(2,1)S(1)}, u32[]{:S(2)}, u32[]{:S(2)}) collective-permute-start(bf16[4,2,8,256]{3,2,1,0:T(8,128)(2,1)S(1)} %get-tuple-element.30), channel_id=1, source_target_pairs={{0,8},{8,16},{16,24},{24,0},{1,9},{9,17},{17,25},{25,1},{2,10},{10... | collective-permute-start | bytes 98312 | tf_op jit(solution)/shard_map/ppermute | solution.py:285
  86.1 4.6 %collective-permute-start.6 = (bf16[4,2,8,256]{3,2,1,0:T(8,128)(2,1)S(1)}, bf16[4,2,8,256]{3,2,1,0:T(8,128)(2,1)S(1)}, u32[]{:S(2)}, u32[]{:S(2)}) collective-permute-start(bf16[4,2,8,256]{3,2,1,0:T(8,128)(2,1)S(1)} %get-tuple-element.31), channel_id=1, source_target_pairs={{0,16},{8,24},{16,0},{24,8},{1,17},{9,25},{17,1},{25,9},{2,18},{10... | collective-permute-start | bytes 98312 | tf_op jit(solution)/shard_map/ppermute | solution.py:285
  90.6 2.8 %collective-permute-start.7 = (bf16[4,2,8,256]{3,2,1,0:T(8,128)(2,1)S(1)}, bf16[4,2,8,256]{3,2,1,0:T(8,128)(2,1)S(1)}, u32[]{:S(2)}, u32[]{:S(2)}) collective-permute-start(bf16[4,2,8,256]{3,2,1,0:T(8,128)(2,1)S(1)} %get-tuple-element.32), channel_id=1, source_target_pairs={{0,24},{8,0},{16,8},{24,16},{1,25},{9,1},{17,9},{25,17},{2,26},{10... | collective-permute-start | bytes 98312 | tf_op jit(solution)/shard_map/ppermute | solution.py:285
  103.7 47.7 %copy-start = (bf16[2,128,2048]{2,1,0:T(8,128)(2,1)S(1)}, bf16[2,128,2048]{2,1,0:T(8,128)(2,1)}, u32[]{:S(2)}) copy-start(bf16[2,128,2048]{2,1,0:T(8,128)(2,1)} %param.11) | copy-start | bytes 3145732
  103.7 47.7 %copy-start.4 = (bf16[256,512]{1,0:T(8,128)(2,1)S(1)}, bf16[256,512]{1,0:T(8,128)(2,1)}, u32[]{:S(2)}) copy-start(bf16[256,512]{1,0:T(8,128)(2,1)} %constant.14.clone.table_ref) | copy-start | bytes 786436
  (4 other events, 23.3 us)
